TPU v7x, 32 devices: a whole 2x2x4 slice. The times are simulated.
32 devices in a mesh: region: 2 (over y), tx: 4 (over z), ty: 2 (over x), band: 2 (over core).
Axes of the slice: x: 2, y: 2, z: 4, core: 2. Of those that a mesh axis runs over, the one named last changes fastest.
Arguments:
- scenes: bfloat16 [4, 256, 12, 256], P(('region', 'ty'), 'tx', 'band'), parts along dimension 0, may hold values from -6 to 6
- cloud: bfloat16 [4, 256, 256], P(('region', 'ty'), 'tx'), parts along dimension 0, may hold values from 0.049804688 to 1
- destination: int32 [4, 256], P(('region', 'ty'), 'tx'), parts along dimension 0, may hold values from 0 to 3, as said below
- offset: int32 [4, 256], P(('region', 'ty'), 'tx'), parts along dimension 0, may hold values from 0 to 63
- counts: int32 [4, 4], P(('region', 'ty'), 'tx'), parts along dimension 0, may hold values from 32 to 64
Outputs:
- composite: bfloat16 [12, 4, 128, 512], P('band', ('region', 'ty'), 'tx'), parts along dimension 1
There are 2 independent parts, one for each index of `region`. A program takes and returns all parts, laid end to end along the dimension named above; each array names one. Nothing has to cross between parts.
Inputs may be any that keep to these rules, and one draw needn't show every extreme that they name: `destination`: among the 64 blocks of one device no tile row is named more than 32 times, and the first 32 blocks of every device in one column of tiles name one common tile row. `offset`: slots are numbered row by row, 8 slots to a row. A device's first counts blocks are live; its other blocks add nothing.
All inputs are finite; a program needn't handle non-finite values.
Results may differ from a plain program's by a relative error of at most 0.0025.
Values may be sent and summed in bfloat16 or wider, within the bound.
No kernel may reach another device: no remote copies, remote signals or barrier semaphores. Data moves between devices by JAX's collectives and lax.ppermute only.
A program may use at most 64 MiB of HBM per device.

v0:
```python
import jax
import jax.numpy as jnp
from jax import lax
from jax.sharding import PartitionSpec as P

TS = 128
BS = 16
S_DEV = 64
MARGIN = 32
LEVELS = 4
SLOTS = 64


BINOMIAL = (0.0625, 0.25, 0.375, 0.25, 0.0625)
BACKGROUND = 0.25


def with_halo(shard, sides, width):
    for axis, dim in sides:
        devices, length = (lax.axis_size(axis), shard.shape[dim])
        up = [(i, (i + 1) % devices) for i in range(devices - 1)]
        down = [(j, i) for i, j in up]
        last = lax.slice_in_dim(shard, length - width, length, axis=dim)
        leading = lax.slice_in_dim(shard, 0, width, axis=dim)
        before = lax.ppermute(last, axis, up)
        after = lax.ppermute(leading, axis, down)
        shard = jnp.concatenate([before, shard, after], axis=dim)
    return shard


def shrink_table(length, rim_in, rim_out):
    extent = length - 2 * rim_in
    outputs = extent // 2 + 2 * rim_out
    first_index = rim_in - 2 - 2 * rim_out
    out_pos = jnp.arange(outputs, dtype=jnp.int32)[:, None]
    in_pos = jnp.arange(length, dtype=jnp.int32)[None, :]
    spacing = in_pos - first_index - 2 * out_pos
    table = jnp.zeros((outputs, length), jnp.float32)
    for tap_index, tap_weight in enumerate(BINOMIAL):
        table = table + tap_weight * (spacing == tap_index).astype(jnp.float32)
    return table


def grow_table(length, rim_in, rim_out):
    excess = 2 * rim_in - 2 - rim_out
    outputs = 2 * (length - 2) - 2 * excess
    paired = jnp.arange(outputs, dtype=jnp.int32)[:, None] + excess
    source = paired // 2
    parity = paired % 2
    spacing = jnp.arange(length, dtype=jnp.int32)[None, :] - source
    even_part = (
        0.125 * (spacing == 0).astype(jnp.float32)
        + 0.75 * (spacing == 1).astype(jnp.float32)
        + 0.125 * (spacing == 2).astype(jnp.float32)
    )
    odd_part = 0.5 * (spacing == 1).astype(jnp.float32) + 0.5 * (spacing == 2).astype(jnp.float32)
    return jnp.where(parity == 0, even_part, odd_part)


def apply_both(field, row_table, col_table):
    rows_done = jnp.einsum("ki,bic->bkc", row_table, field, precision=lax.Precision.HIGHEST)
    return jnp.einsum("bkc,mc->bkm", rows_done, col_table, precision=lax.Precision.HIGHEST)


def shrink(field, rim_in, rim_out):
    row_table = shrink_table(field.shape[-2], rim_in, rim_out)
    col_table = shrink_table(field.shape[-1], rim_in, rim_out)
    return apply_both(field, row_table, col_table)


def grow(field, rim_in, rim_out):
    row_table = grow_table(field.shape[-2], rim_in, rim_out)
    col_table = grow_table(field.shape[-1], rim_in, rim_out)
    return apply_both(field, row_table, col_table)


def trim(field, rim_have, rim_want):
    excess = rim_have - rim_want
    return field[..., excess : field.shape[-2] - excess, excess : field.shape[-1] - excess]


def border(extent, rim, begin, whole):
    position = begin - rim + jnp.arange(extent + 2 * rim, dtype=jnp.int32)
    return ((position >= 0) & (position < whole)).astype(jnp.float32)


def local(scenes, cloud, destination, offset, counts):
    row_tiles = lax.axis_size("tx")
    col_tiles = lax.axis_size("ty")
    row_tile = lax.axis_index("tx")
    col_tile = lax.axis_index("ty")
    spread = max(2, 2 * S_DEV // row_tiles)
    blocks = scenes[0]
    weights = cloud[0]
    target_row = destination[0]
    placed = offset[0]
    live_count = counts[0, 0]
    own_bands = blocks.shape[1]
    living = jnp.arange(S_DEV, dtype=jnp.int32) < live_count
    matches = (target_row[:, None] == jnp.arange(row_tiles, dtype=jnp.int32)[None, :]) & living[
        :, None
    ]
    ordinal = jnp.cumsum(matches.astype(jnp.int32), axis=0) - 1
    ranking = jnp.sum(jnp.where(matches, ordinal, 0), axis=1)
    target = target_row * spread + ranking
    chooser = (
        (jnp.arange(row_tiles * spread, dtype=jnp.int32)[:, None] == target[None, :])
        & living[None, :]
    ).astype(jnp.bfloat16)
    merged = jnp.concatenate([blocks, weights[:, None, :]], axis=1).reshape(
        S_DEV, (own_bands + 1) * BS * BS
    )
    packed = jnp.dot(chooser, merged, preferred_element_type=jnp.float32).astype(jnp.bfloat16)
    packed = packed.reshape(row_tiles, spread, own_bands + 1, BS * BS)
    slot_ids = jnp.arange(SLOTS, dtype=jnp.int32)
    tag_send = jnp.dot(
        chooser, (placed + 1).astype(jnp.bfloat16)[:, None], preferred_element_type=jnp.float32
    )
    tag_send = tag_send.astype(jnp.bfloat16).reshape(row_tiles, spread)
    arrived, tag_back = (
        lax.all_to_all(packed, "tx", split_axis=0, concat_axis=0, tiled=True),
        lax.all_to_all(tag_send, "tx", split_axis=0, concat_axis=0, tiled=True),
    )
    landing = (slot_ids + 1).astype(jnp.float32)[:, None] == tag_back.reshape(-1).astype(
        jnp.float32
    )[None, :]
    arrived = arrived.reshape(row_tiles * spread, own_bands + 1, BS * BS)
    coverage = arrived[:, own_bands:].astype(jnp.float32)
    payload = jnp.concatenate(
        [arrived[:, :own_bands].astype(jnp.float32) * coverage, coverage], axis=1
    )
    payload = payload.reshape(row_tiles * spread, (own_bands + 1) * BS * BS)
    slot_sums = jnp.dot(landing.astype(jnp.float32), payload, precision=lax.Precision.HIGHEST)
    per_row = TS // BS
    tile_field = slot_sums.reshape(per_row, per_row, own_bands + 1, BS, BS).transpose(2, 0, 3, 1, 4)
    tile_field = tile_field.reshape(own_bands + 1, TS, TS)

    def masked(field, extent, rim):
        row_mask = border(extent, rim, row_tile * extent, extent * row_tiles)
        col_mask = border(extent, rim, col_tile * extent, extent * col_tiles)
        return field * row_mask[:, None] * col_mask[None, :]

    def enlarge(field, rim_in, rim_out):
        return grow(field, rim_in, rim_out)

    ground = with_halo(tile_field, (("tx", 1), ("ty", 2)), MARGIN)
    margin = MARGIN
    needed = [0]
    for tier_index in range(1, LEVELS):
        needed.append((needed[-1] + 3) // 2)
    pyramid = [(ground, margin)]
    extent = TS
    for tier_index in range(1, LEVELS):
        source, rim_in = pyramid[-1]
        rim_out = (rim_in - 2) // 2
        extent = extent // 2
        reduced = masked(shrink(source, rim_in, rim_out), extent, rim_out)
        pyramid.append((reduced, rim_out))
    deepest = LEVELS - 1
    summit, rim_top = pyramid[-1]
    summit = trim(summit, rim_top, needed[deepest])
    collapsed = summit[:own_bands] / (BACKGROUND + summit[own_bands])
    for tier_index in range(LEVELS - 2, -1, -1):
        current, rim_here = pyramid[tier_index]
        coarser, rim_below = pyramid[tier_index + 1]
        current = trim(current, rim_here, needed[tier_index])
        detail = current[:own_bands] - enlarge(coarser[:own_bands], rim_below, needed[tier_index])
        band_part = detail / (BACKGROUND + current[own_bands])
        collapsed = band_part + enlarge(collapsed, needed[tier_index + 1], needed[tier_index])
        collapsed = masked(collapsed, TS >> tier_index, needed[tier_index])
    blended = collapsed.astype(jnp.bfloat16)
    flipped = jnp.swapaxes(blended, 1, 2)
    strips = lax.all_to_all(flipped, "tx", split_axis=1, concat_axis=2, tiled=True)
    return strips[:, None]


def solution(mesh):
    placed = (
        P(("region", "ty"), "tx", "band", None),
        P(("region", "ty"), "tx", None),
        P(("region", "ty"), "tx"),
        P(("region", "ty"), "tx"),
        P(("region", "ty"), "tx"),
    )
    return jax.shard_map(
        local,
        mesh=mesh,
        in_specs=placed,
        out_specs=P("band", ("region", "ty"), "tx", None),
        check_vma=False,
    )
```

profile of v0, /device:TPU:0, one launch (start us, length us, event | category | flops | bytes accessed | tf_op | source)
XLA Modules:
  0.0 95.1 jit_solution(7972287795352572783)
XLA Ops:
  0.7 0.7 fusion.53
  1.4 0.1 reduce_window_sum.11
  1.5 0.8 select_reduce_fusion
  2.3 0.7 fusion.167
  3.0 0.8 fusion.27
  3.8 0.7 all_to_all.26
  4.5 6.3 %all-to-all-start = ((bf16[4,1,32]{2,1,0:T(2,128)(2,1)}), bf16[4,1,32]{2,1,0:T(2,128)(2,1)S(1)}, u32[]{:S(2)}, u32[]{:S(2)}) async-start(bf16[4,1,32]{2,1,0:T(2,128)(2,1)} %all_to_all.26), calls=%async_computation | async-start | bytes 4096 | tf_op jit(solution)/shard_map/all_to_all | solution.py:122
  10.9 1.0 %maximum_bitcast_fusion = bf16[7,8,8,256]{3,2,1,0:T(8,128)(2,1)S(1)} fusion(bf16[64,1,256]{2,0,1:T(8,128)(2,1)} %bitcast.147, bf16[64,6,256]{2,0,1:T(8,128)(2,1)} %bitcast.146), kind=kLoop, calls=%fused_computation.52 | loop fusion | flops 114688 | bytes 458752
  11.9 0.3 convolution_convert_fusion
  12.3 0.5 reshape.478
  12.8 0.9 copy.71
  13.7 2.7 %all-to-all-done = bf16[4,1,32]{2,1,0:T(2,128)(2,1)S(1)} async-done(((bf16[4,1,32]{2,1,0:T(2,128)(2,1)}), bf16[4,1,32]{2,1,0:T(2,128)(2,1)S(1)}, u32[]{:S(2)}, u32[]{:S(2)}) %all-to-all-start) | async-done | bytes 288 | tf_op jit(solution)/shard_map/all_to_all | solution.py:122
  16.3 3.5 %all-to-all-start.1 = ((bf16[4,32,7,256]{3,1,2,0:T(8,128)(2,1)}), bf16[4,32,7,256]{3,1,2,0:T(8,128)(2,1)S(1)}, u32[]{:S(2)}, u32[]{:S(2)}) async-start(bf16[4,32,7,256]{3,1,2,0:T(8,128)(2,1)} %copy.71), calls=%async_computation.1 | async-start | bytes 917504 | tf_op jit(solution)/shard_map/all_to_all | solution.py:121
  19.9 0.1 reshape.482
  20.0 11.7 %all-to-all-done.1 = bf16[4,32,7,256]{3,1,2,0:T(8,128)(2,1)S(1)} async-done(((bf16[4,32,7,256]{3,1,2,0:T(8,128)(2,1)}), bf16[4,32,7,256]{3,1,2,0:T(8,128)(2,1)S(1)}, u32[]{:S(2)}, u32[]{:S(2)}) %all-to-all-start.1) | async-done | bytes 458784 | tf_op jit(solution)/shard_map/all_to_all | solution.py:121
  31.8 0.1 convert_multiply_fusion
  31.9 0.1 pad_maximum_fusion
  31.9 0.3 copy.73
  32.2 5.9 %convolution_bitcast_fusion = f32[7,8,16,8,16]{4,3,2,0,1:T(8,128)} fusion(f32[7,16,16,128,1]{3,2,1,0,4:T(8,128)S(1)} %bitcast.141, f32[128]{0:T(128)S(1)} %reshape.482, f32[8,8]{1,0:T(8,128)S(1)} %add_convert_fusion), kind=kOutput, calls=%fused_computation.1 | convolution fusion | flops 176168960 | bytes 1377024 | tf_op jit(solution)/shard_map/dot_general | solution.py:133
  38.1 4.7 %copy.99 = f32[7,8,16,8,16]{2,1,4,3,0:T(8,128)} copy(f32[7,8,16,8,16]{4,3,2,0,1:T(8,128)} %convolution_bitcast_fusion) | data formatting | bytes 917504 | tf_op jit(solution)/shard_map/reshape | solution.py:136
  42.8 2.5 %reshape.495 = f32[7,128,128]{1,2,0:T(8,128)S(1)} reshape(f32[7,8,16,8,16]{2,1,4,3,0:T(8,128)} %copy.99) | data formatting | bytes 917504 | tf_op jit(solution)/shard_map/reshape | solution.py:136
  45.4 0.0 copy-start
  45.4 1.2 %fusion.311 = (f32[7,32,128]{1,2,0:T(8,128)}, f32[7,32,128]{1,2,0:T(8,128)}) fusion(f32[7,128,128]{1,2,0:T(8,128)S(1)} %reshape.495), kind=kLoop, calls=%fused_computation.410 | loop fusion | bytes 458752 | tf_op jit(solution)/shard_map/slice | solution.py:23
  46.6 1.3 %collective-permute-start.1 = (f32[7,32,128]{1,2,0:T(8,128)}, f32[7,32,128]{1,2,0:T(8,128)}, u32[]{:S(2)}, u32[]{:S(2)}) collective-permute-start(f32[7,32,128]{1,2,0:T(8,128)} %get-tuple-element.8), channel_id=1, source_target_pairs={{4,0},{8,4},{12,8},{5,1},{9,5},{13,9},{6,2},{10,6},{14,10},{7,3},{... | collective-permute-start | bytes 344072 | tf_op jit(solution)/shard_map/ppermute | solution.py:26
  47.8 5.4 %collective-permute-start = (f32[7,32,128]{1,2,0:T(8,128)}, f32[7,32,128]{1,2,0:T(8,128)}, u32[]{:S(2)}, u32[]{:S(2)}) collective-permute-start(f32[7,32,128]{1,2,0:T(8,128)} %get-tuple-element.7), channel_id=1, source_target_pairs={{0,4},{4,8},{8,12},{1,5},{5,9},{9,13},{2,6},{6,10},{10,14},{3,7},{... | collective-permute-start | bytes 344072 | tf_op jit(solution)/shard_map/ppermute | solution.py:25
  53.2 0.0 copy-done
  53.2 0.0 slice-start
  53.2 1.9 %slice-done = f32[6,8,16,8,16]{4,3,2,0,1:T(8,128)S(1)} async-done(((f32[7,8,16,8,16]{4,3,2,0,1:T(8,128)}), f32[6,8,16,8,16]{4,3,2,0,1:T(8,128)S(1)}, s32[]{:S(2)}) %slice-start) | async-done | bytes 393240 | tf_op jit(solution)/shard_map/slice | solution.py:167
  55.1 1.9 %copy.74 = f32[6,8,16,8,16]{4,3,2,1,0:T(8,128)} copy(f32[6,8,16,8,16]{4,3,2,0,1:T(8,128)S(1)} %slice-done) | data formatting | bytes 786432 | tf_op jit(solution)/shard_map/slice | solution.py:167
  57.0 2.5 %slice.62 = f32[6,128,128]{2,1,0:T(8,128)S(1)} reshape(f32[6,8,16,8,16]{4,3,2,1,0:T(8,128)} %copy.74) | data formatting | bytes 786432 | tf_op jit(solution)/shard_map/slice | solution.py:167
  59.5 0.2 collective-permute-done.1
  59.7 1.2 %collective-permute-done = f32[7,32,128]{1,2,0:T(8,128)} collective-permute-done((f32[7,32,128]{1,2,0:T(8,128)}, f32[7,32,128]{1,2,0:T(8,128)}, u32[]{:S(2)}, u32[]{:S(2)}) %collective-permute-start) | collective-permute-done | bytes 114720 | tf_op jit(solution)/shard_map/ppermute | solution.py:25
  60.9 0.0 copy-done.1
  60.9 1.3 %pad_maximum_fusion.3 = (f32[7,192,32]{1,2,0:T(8,128)S(1)}, f32[7,192,32]{1,2,0:T(8,128)S(1)}) fusion(f32[7,32,128]{1,2,0:T(8,128)} %collective-permute-done.1, f32[7,128,128]{1,2,0:T(8,128)S(1)} %copy-done.1, f32[7,32,128]{1,2,0:T(8,128)} %collective-permute-done), kind=kLoop, calls=%fused_computation.51 | loop fusion | flops 172032 | bytes 1032192 | tf_op jit(solution)/shard_map/slice | solution.py:23
  62.2 1.3 %collective-permute-start.3 = (f32[7,192,32]{1,2,0:T(8,128)S(1)}, f32[7,192,32]{1,2,0:T(8,128)S(1)}, u32[]{:S(2)}, u32[]{:S(2)}) collective-permute-start(f32[7,192,32]{1,2,0:T(8,128)S(1)} %get-tuple-element.6), channel_id=1, source_target_pairs={{2,0},{3,1},{6,4},{7,5},{10,8},{11,9},{14,12},{15,13},{18,16},{19,... | collective-permute-start | bytes 516104 | tf_op jit(solution)/shard_map/ppermute | solution.py:26
  63.5 4.8 %collective-permute-start.2 = (f32[7,192,32]{1,2,0:T(8,128)S(1)}, f32[7,192,32]{1,2,0:T(8,128)S(1)}, u32[]{:S(2)}, u32[]{:S(2)}) collective-permute-start(f32[7,192,32]{1,2,0:T(8,128)S(1)} %get-tuple-element.5), channel_id=1, source_target_pairs={{0,2},{1,3},{4,6},{5,7},{8,10},{9,11},{12,14},{13,15},{16,18},{17,... | collective-permute-start | bytes 516104 | tf_op jit(solution)/shard_map/ppermute | solution.py:25
  68.2 1.1 %slice_add_fusion = f32[1,8,16,8,16]{4,3,2,0,1:T(8,128)S(1)} fusion(f32[7,8,16,8,16]{4,3,2,0,1:T(8,128)} %convolution_bitcast_fusion), kind=kLoop, calls=%fused_computation.48 | loop fusion | flops 16384 | bytes 131072 | tf_op jit(solution)/shard_map/add | solution.py:168
  69.3 0.2 add.547
  69.5 0.6 collective-permute-done.3
  70.1 1.5 %collective-permute-done.2 = f32[7,192,32]{1,2,0:T(8,128)S(1)} collective-permute-done((f32[7,192,32]{1,2,0:T(8,128)S(1)}, f32[7,192,32]{1,2,0:T(8,128)S(1)}, u32[]{:S(2)}, u32[]{:S(2)}) %collective-permute-start.2) | collective-permute-done | bytes 172064 | tf_op jit(solution)/shard_map/ppermute | solution.py:25
  71.6 2.5 %fusion.10 = f32[7,94,192]{1,2,0:T(8,128)S(1)} fusion(f32[7,192,32]{1,2,0:T(8,128)S(1)} %collective-permute-done.3, f32[7,32,128]{1,2,0:T(8,128)} %collective-permute-done.1, f32[7,128,128]{1,2,0:T(8,128)S(1)} %copy-done.1, f32[7,32,128]{1,2,0:T(8,128)} %collective-permute-done, f32[7,192,32]{1,2,0:T(8,128)S(1)} %collective-permute-done.2, ...), kind=kOutput, calls=%fused_computation.12 | convolution fusion | flops 292381056 | bytes 1537912 | tf_op jit(solution)/shard_map/ki,bic->bkc/dot_general | solution.py:61
  74.1 1.5 %fusion.16 = f32[7,94,94]{2,1,0:T(8,128)S(1)} fusion(f32[7,94,192]{1,2,0:T(8,128)S(1)} %fusion.10, f32[94]{0:T(128)S(1)} %get-tuple-element.11, f32[94]{0:T(128)S(1)} %get-tuple-element.12, s32[94]{0:T(128)S(1)} %iota_multiply_fusion.2), kind=kOutput, calls=%fused_computation.19 | convolution fusion | flops 142901440 | bytes 753880 | tf_op jit(solution)/shard_map/bkc,mc->bkm/dot_general | solution.py:62
  75.6 0.1 fusion.43
  75.6 0.4 convolution_bitcast_fusion.3
  76.0 0.4 fusion.22
  76.4 0.1 fusion.84
  76.5 0.3 convolution_bitcast_fusion.6
  76.8 0.4 fusion.26
  77.1 0.3 convolution_bitcast_fusion.7
  77.4 0.3 convolution_bitcast_fusion.8
  77.8 0.6 convolution_bitcast_fusion.1
  78.4 0.4 convolution_bitcast_fusion.4
  78.8 0.5 fusion.20
  79.4 0.4 fusion.24
  79.8 0.8 fusion.13
  80.6 0.4 fusion.25
  81.0 0.4 convolution_bitcast_fusion.5
  81.4 0.6 fusion.19
  82.0 0.5 convolution_bitcast_fusion.2
  82.5 0.8 fusion.21
  83.3 0.2 copy.86
  83.5 10.7 %all_to_all.30 = bf16[6,128,128]{2,0,1:T(8,128)(2,1)S(1)} all-to-all(bf16[6,128,128]{2,0,1:T(8,128)(2,1)S(1)} %copy.86), channel_id=1, replica_groups=mesh['region'=2,'tx'=4,'ty'=2,'band'=2] {'tx'}, dimensions={1} | all-to-all | bytes 393216 | tf_op jit(solution)/shard_map/all_to_all | solution.py:173
  94.2 0.2 copy.88
  94.4 0.8 broadcast_in_dim.136
  (28 shorter events, 0.2 us)
Async XLA Ops:
  4.5 11.8 %all-to-all-start = ((bf16[4,1,32]{2,1,0:T(2,128)(2,1)}), bf16[4,1,32]{2,1,0:T(2,128)(2,1)S(1)}, u32[]{:S(2)}, u32[]{:S(2)}) async-start(bf16[4,1,32]{2,1,0:T(2,128)(2,1)} %all_to_all.26), calls=%async_computation | async-start | bytes 4096 | tf_op jit(solution)/shard_map/all_to_all | solution.py:122
  16.3 15.4 %all-to-all-start.1 = ((bf16[4,32,7,256]{3,1,2,0:T(8,128)(2,1)}), bf16[4,32,7,256]{3,1,2,0:T(8,128)(2,1)S(1)}, u32[]{:S(2)}, u32[]{:S(2)}) async-start(bf16[4,32,7,256]{3,1,2,0:T(8,128)(2,1)} %copy.71), calls=%async_computation.1 | async-start | bytes 917504 | tf_op jit(solution)/shard_map/all_to_all | solution.py:121
  45.4 7.8 %copy-start = (f32[7,128,128]{1,2,0:T(8,128)}, f32[7,128,128]{1,2,0:T(8,128)S(1)}, u32[]{:S(2)}) copy-start(f32[7,128,128]{1,2,0:T(8,128)S(1)} %reshape.495) | copy-start | bytes 1376260
  46.6 13.1 %collective-permute-start.1 = (f32[7,32,128]{1,2,0:T(8,128)}, f32[7,32,128]{1,2,0:T(8,128)}, u32[]{:S(2)}, u32[]{:S(2)}) collective-permute-start(f32[7,32,128]{1,2,0:T(8,128)} %get-tuple-element.8), channel_id=1, source_target_pairs={{4,0},{8,4},{12,8},{5,1},{9,5},{13,9},{6,2},{10,6},{14,10},{7,3},{... | collective-permute-start | bytes 344072 | tf_op jit(solution)/shard_map/ppermute | solution.py:26
  47.8 13.0 %collective-permute-start = (f32[7,32,128]{1,2,0:T(8,128)}, f32[7,32,128]{1,2,0:T(8,128)}, u32[]{:S(2)}, u32[]{:S(2)}) collective-permute-start(f32[7,32,128]{1,2,0:T(8,128)} %get-tuple-element.7), channel_id=1, source_target_pairs={{0,4},{4,8},{8,12},{1,5},{5,9},{9,13},{2,6},{6,10},{10,14},{3,7},{... | collective-permute-start | bytes 344072 | tf_op jit(solution)/shard_map/ppermute | solution.py:25
  53.2 1.9 %slice-start = ((f32[7,8,16,8,16]{4,3,2,0,1:T(8,128)}), f32[6,8,16,8,16]{4,3,2,0,1:T(8,128)S(1)}, s32[]{:S(2)}) async-start(f32[7,8,16,8,16]{4,3,2,0,1:T(8,128)} %convolution_bitcast_fusion), calls=%async_computation.3 | async-start | bytes 6291456 | tf_op jit(solution)/shard_map/slice | solution.py:167
  57.0 3.8 %copy-start.1 = (f32[7,128,128]{1,2,0:T(8,128)S(1)}, f32[7,128,128]{1,2,0:T(8,128)}, u32[]{:S(2)}) copy-start(f32[7,128,128]{1,2,0:T(8,128)} %copy-done) | copy-start | bytes 1376260
  62.2 7.9 %collective-permute-start.3 = (f32[7,192,32]{1,2,0:T(8,128)S(1)}, f32[7,192,32]{1,2,0:T(8,128)S(1)}, u32[]{:S(2)}, u32[]{:S(2)}) collective-permute-start(f32[7,192,32]{1,2,0:T(8,128)S(1)} %get-tuple-element.6), channel_id=1, source_target_pairs={{2,0},{3,1},{6,4},{7,5},{10,8},{11,9},{14,12},{15,13},{18,16},{19,... | collective-permute-start | bytes 516104 | tf_op jit(solution)/shard_map/ppermute | solution.py:26
  63.5 8.1 %collective-permute-start.2 = (f32[7,192,32]{1,2,0:T(8,128)S(1)}, f32[7,192,32]{1,2,0:T(8,128)S(1)}, u32[]{:S(2)}, u32[]{:S(2)}) collective-permute-start(f32[7,192,32]{1,2,0:T(8,128)S(1)} %get-tuple-element.5), channel_id=1, source_target_pairs={{0,2},{1,3},{4,6},{5,7},{8,10},{9,11},{12,14},{13,15},{16,18},{17,... | collective-permute-start | bytes 516104 | tf_op jit(solution)/shard_map/ppermute | solution.py:25
where the time goes:
time: 95.7 us; the launch traced here: 95.1 us
  starting transfers between devices  22.5 us (24%)
  local copies, waits for them, and re-layouts  18.5 us (19%)
  matrix products  18.4 us (19%)
  waiting for transfers between devices  17.8 us (19%)
  blocking collectives  10.7 us (11%)
  other arithmetic  6.16 us (6%)
  between operations  1.13 us (1%)
    all_to_all x1, waiting for transfers between devices, local(): lax.all_to_all(packed, 'tx', split_axis=0, concat_axis=0, tiled=True)  11.7 us
    all_to_all x1, blocking collectives, local(): lax.all_to_all(flipped, 'tx', split_axis=1, concat_axis=2, tiled=True)  10.7 us
    ppermute x2, starting transfers between devices, with_halo(): before = lax.ppermute(last, axis, up)  10.1 us
    reshape x2, local copies, waits for them, and re-layouts, local(): tile_field = tile_field.reshape(own_bands + 1, TS, TS)  7.26 us
    all_to_all x1, starting transfers between devices, local(): lax.all_to_all(tag_send, 'tx', split_axis=0, concat_axis=0, tiled=True)  6.35 us
    slice x4, local copies, waits for them, and re-layouts, local(): current[:own_bands]  6.24 us
    dot_general x1, matrix products, local(): jnp.dot(landing.astype(jnp.float32), payload, precision=lax.Precision.HIG...  5.9 us
    dot_general x9, matrix products, apply_both(): jnp.einsum('ki,bic->bkc', row_table, field, precision=lax.Precision.HIGHEST)  5.73 us
  transfers between devices with their start and end apart: 6, of which 6 were waited for; matrix products, arithmetic and copies ran while one was open for 9% of the time, Pallas kernels for 0%

commit v1 on v0

--- a/solution.py
+++ b/solution.py
@@ -1,6 +1,11 @@
+import functools
+
 import jax
 import jax.numpy as jnp
+import numpy as np
 from jax import lax
+from jax.experimental import pallas as pl
+from jax.experimental.pallas import tpu as pltpu
 from jax.sharding import PartitionSpec as P
 
 TS = 128
@@ -174,6 +179,397 @@
     return strips[:, None]
 
 
+BF = jnp.bfloat16
+F32 = jnp.float32
+EDGE = 3
+
+
+def up8(v):
+    return -(-v // 8) * 8
+
+
+def shrink_grid(length):
+    table = np.zeros((length // 2, length))
+    for i in range(length // 2):
+        for tap, weight in enumerate(BINOMIAL):
+            k = 2 * i + tap - 2
+            if 0 <= k < length:
+                table[i, k] += weight
+    return table
+
+
+def grow_grid(length):
+    table = np.zeros((2 * length, length))
+    for i in range(length):
+        for k, weight in ((i - 1, 0.125), (i, 0.75), (i + 1, 0.125)):
+            if 0 <= k < length:
+                table[2 * i, k] += weight
+        for k in (i, i + 1):
+            if k < length:
+                table[2 * i + 1, k] += 0.5
+    return table
+
+
+def split_table(table):
+    high = table.astype(BF)
+    return high, (table - high.astype(np.float64)).astype(BF)
+
+
+def row_shrinks(rows):
+    tables, current = [], np.eye(rows)
+    for level in range(1, LEVELS):
+        current = shrink_grid(rows >> (level - 1)) @ current
+        tables.append(current)
+    return tables
+
+
+class Plan:
+    def __init__(self, n, m, bands):
+        self.n, self.m, self.bands = n, m, bands
+        self.rows = n * TS
+        self.strip = TS // n
+        self.slots = n * SLOTS
+        self.slot_rows = n * (TS // BS)
+        w = self.strip
+        self.held = [w, w // 2 + 2, w // 4 + 3, w // 8 + 3]
+        self.size = [w] + [up8(h) for h in self.held[1:]]
+        self.first = [0, -1, -1, -1]
+        self.at = [0]
+        for size in self.size:
+            self.at.append(self.at[-1] + size)
+        self.edge_at = [None] + [self.at[LEVELS] + 8 * k for k in range(LEVELS - 1)]
+        self.main = self.at[LEVELS] + 8 * (LEVELS - 1)
+        self.low_at = self.main
+        self.low_edge_at = self.main + self.size[3]
+        self.total = self.main + self.size[3] + 8
+
+    def column_tables(self):
+        n, m, w = self.n, self.m, self.strip
+        width = m * TS
+        grids = [np.eye(width)] + row_shrinks(width)
+        tables = np.zeros((n, m, self.total, TS))
+        for t in range(n):
+            for j in range(m):
+                for level in range(LEVELS):
+                    base = ((j * TS + t * w) >> level) + self.first[level]
+                    for k in range(self.held[level]):
+                        o = base + k
+                        if 0 <= o < width >> level:
+                            tables[t, j, self.at[level] + k] = grids[level][o, j * TS : (j + 1) * TS]
+                    if level == 0:
+                        continue
+                    if 2 * t < n:
+                        base = ((j + 1) * TS >> level) - 1
+                    else:
+                        base = (j * TS >> level) - 1
+                    for k in range(EDGE):
+                        o = base + k
+                        if 0 <= o < width >> level:
+                            tables[t, j, self.edge_at[level] + k] = grids[level][o, j * TS : (j + 1) * TS]
+        high, low = split_table(tables)
+        high[:, :, self.low_at : self.low_at + self.size[3]] = low[:, :, self.at[3] : self.at[4]]
+        edge = self.edge_at[3]
+        high[:, :, self.low_edge_at : self.low_edge_at + 8] = low[:, :, edge : edge + 8]
+        return np.concatenate([high, high], axis=-1).reshape(n * m, self.total, 2 * TS)
+
+
+def halves(value):
+    high = value.astype(BF)
+    return high, (value - high.astype(F32)).astype(BF)
+
+
+def dot2(value, table):
+    high, low = halves(value)
+    return jnp.dot(high, table, preferred_element_type=F32) + jnp.dot(
+        low, table, preferred_element_type=F32
+    )
+
+
+def note_kernel(plan, count_ref, cloud_ref, dest_ref, offset_ref, out_ref):
+    out_ref[:S_DEV, :] = cloud_ref[...]
+    per_row = TS // BS
+    offset = offset_ref[...]
+    code = (offset % per_row) * plan.slot_rows + dest_ref[...] * per_row + offset // per_row
+    live = lax.broadcasted_iota(jnp.int32, (1, S_DEV), 1) < count_ref[0, 0]
+    code = jnp.where(live, code, -1).astype(F32)
+    tail = out_ref.shape[0] - S_DEV
+    out_ref[S_DEV:, :] = jnp.full((tail, BS * BS), -1.0, BF)
+    out_ref[S_DEV:, :S_DEV] = jnp.broadcast_to(code, (tail, S_DEV)).astype(BF)
+
+
+def place_kernel(plan, *refs):
+    n, bands = plan.n, plan.bands
+    scenes, notes = refs[:n], refs[n : 2 * n]
+    column_ref, row1_ref, row2_ref, row3_ref, a0_ref, a1_ref, a2_ref, a3_ref, edge_ref = refs[
+        2 * n : 2 * n + 9
+    ]
+    prod_ref, tile_ref, z1_ref, z2_ref, z3_ref = refs[2 * n + 9 :]
+    blocks = n * S_DEV
+    area = BS * BS
+    codes = notes[0][S_DEV : S_DEV + 16, :].astype(F32)
+    for p in range(1, n):
+        codes = jnp.maximum(
+            codes, pltpu.roll(notes[p][S_DEV : S_DEV + 16, :].astype(F32), S_DEV * p, 1)
+        )
+    codes = codes[:1, :blocks]
+    slot = lax.broadcasted_iota(jnp.int32, (plan.slots, blocks), 0).astype(F32)
+    landing = jnp.where(slot == codes, 1.0, 0.0).astype(BF)
+    landing2 = jnp.concatenate([landing, landing], axis=1)
+    group = lax.broadcasted_iota(jnp.int32, (plan.slot_rows, TS), 1) // BS
+    per_row = TS // BS
+    column = column_ref[...]
+    e1 = plan.size[1]
+    for f in range(bands + 1):
+        for p in range(n):
+            weight = notes[p][:S_DEV, :]
+            at = pl.ds(p * S_DEV, S_DEV)
+            if f == bands:
+                prod_ref[at, :] = weight
+            else:
+                value = scenes[p][f].astype(F32) * weight.astype(F32)
+                high, low = halves(value)
+                prod_ref[at, :] = high
+                prod_ref[pl.ds(blocks + p * S_DEV, S_DEV), :] = low
+        if f == bands:
+            sums = jnp.dot(landing, prod_ref[:blocks, :], preferred_element_type=F32)
+        else:
+            sums = jnp.dot(landing2, prod_ref[...], preferred_element_type=F32)
+        for half in range(area // TS):
+            part = [
+                sums[b * plan.slot_rows : (b + 1) * plan.slot_rows, half * TS : (half + 1) * TS]
+                for b in range(per_row)
+            ]
+            step = per_row // 2
+            while step:
+                odd = (group & step) != 0
+                for i in range(per_row):
+                    if i & step:
+                        continue
+                    a, b = part[i], part[i + step]
+                    part[i] = jnp.where(odd, pltpu.roll(b, step * BS, 1), a)
+                    part[i + step] = jnp.where(odd, b, pltpu.roll(a, TS - step * BS, 1))
+                step //= 2
+            for r in range(per_row):
+                tile_ref[pl.ds(half * per_row + r, plan.slot_rows, stride=BS), :] = part[r]
+        high, low = halves(tile_ref[...])
+        tile = jnp.concatenate([high, low], axis=1)
+        cols = lax.dot_general(
+            column, tile, (((1,), (1,)), ((), ())), preferred_element_type=F32
+        )
+        at, size, edge = plan.at, plan.size, plan.edge_at
+        a0_ref[f] = cols[at[0] : at[1]]
+        z1_ref[f, : size[1]] = cols[at[1] : at[2]]
+        z1_ref[f, size[1] :] = cols[edge[1] : edge[1] + 8]
+        z2_ref[f, : size[2]] = cols[at[2] : at[3]]
+        z2_ref[f, size[2] :] = cols[edge[2] : edge[2] + 8]
+        z3_ref[f, : size[3]] = (
+            cols[at[3] : at[4]] + cols[plan.low_at : plan.low_at + size[3]]
+        )
+        z3_ref[f, size[3] :] = (
+            cols[edge[3] : edge[3] + 8] + cols[plan.low_edge_at : plan.low_edge_at + 8]
+        )
+    planes = bands + 1
+    rows = plan.rows
+    z1 = dot2(z1_ref[...].reshape(planes * (size[1] + 8), rows), row1_ref[...])
+    z2 = dot2(z2_ref[...].reshape(planes * (size[2] + 8), rows), row2_ref[...])
+    z3 = z3_ref[...].reshape(planes * (size[3] + 8), rows)
+    z3 = dot2(z3, row3_ref[0]) + jnp.dot(
+        z3.astype(BF), row3_ref[1], preferred_element_type=F32
+    )
+    start = 0
+    edge_ref[...] = jnp.zeros(edge_ref.shape, F32)
+    for z, out_ref, level in ((z1, a1_ref, 1), (z2, a2_ref, 2), (z3, a3_ref, 3)):
+        lanes = z.shape[-1]
+        z = z.reshape(planes, size[level] + 8, lanes)
+        out_ref[...] = z[:, : size[level]]
+        for f in range(planes):
+            edge_ref[pl.ds(EDGE * f, EDGE), start : start + lanes] = z[
+                f, size[level] : size[level] + EDGE
+            ]
+        start += lanes
+
+
+def grow_columns(value, outputs):
+    half = outputs // 2
+    a, b, c = value[:, :half], value[:, 1 : half + 1], value[:, 2 : half + 2]
+    return (a + b) * 0.5, (a + 6.0 * b + c) * 0.125
+
+
+def weave(even, odd, ref, size):
+    k, half, lanes = even.shape
+    if 2 * half < size:
+        ref[...] = jnp.zeros(ref.shape, F32)
+    for q in range(k):
+        for chunk in range(lanes // TS):
+            part = slice(chunk * TS, (chunk + 1) * TS)
+            ref[q, chunk, pl.ds(0, half, stride=2), :] = even[q][:, part]
+            ref[q, chunk, pl.ds(1, half, stride=2), :] = odd[q][:, part]
+    return jnp.concatenate([ref[:, chunk] for chunk in range(lanes // TS)], axis=-1)
+
+
+def blend_kernel(plan, flag_ref, a0_ref, a1_ref, a2_ref, a3_ref, edge_ref, grow1_ref, grow2_ref, grow3_ref,
+                 out_ref, g1_ref, g2_ref, g3_ref, e2_ref, e1_ref, e0_ref):
+    bands = plan.bands
+    planes = bands + 1
+    w = plan.strip
+    left, right = flag_ref[0], flag_ref[1]
+    start = 0
+    for level, (src, dst) in enumerate(((a1_ref, g1_ref), (a2_ref, g2_ref), (a3_ref, g3_ref)), 1):
+        lanes = src.shape[-1]
+        dst[...] = src[...]
+        for f in range(planes):
+            edge = edge_ref[pl.ds(EDGE * f, EDGE), start : start + lanes]
+            far = w >> level
+            dst[f, :EDGE] += jnp.where(left > 0, edge, 0.0)
+            dst[f, far : far + EDGE] += jnp.where(right > 0, edge, 0.0)
+        start += lanes
+    first = flag_ref[2]
+    last = flag_ref[3]
+
+    def inside(level, columns):
+        column = lax.broadcasted_iota(jnp.int32, (columns, 1), 0) - 1
+        keep = ((column >= 0) | (first == 0)) & ((column < (w >> level)) | (last == 0))
+        return keep.astype(F32)
+
+    top = g3_ref[...]
+    blend = top[:bands] / (BACKGROUND + top[bands:])
+    for level, cur_ref, below_ref, grow_ref, up_ref in (
+        (2, g2_ref, g3_ref, grow3_ref, e2_ref),
+        (1, g1_ref, g2_ref, grow2_ref, e1_ref),
+    ):
+        stacked = jnp.concatenate([below_ref[:bands], blend], axis=0)
+        k, c, r = stacked.shape
+        wide = dot2(stacked.reshape(k * c, r), grow_ref[...])
+        wide = wide.reshape(k, c, wide.shape[-1])
+        pairs = up8(plan.held[level]) // 2
+        pairs = min(pairs, c - 2)
+        even, odd = grow_columns(wide, 2 * pairs)
+        size = cur_ref.shape[1]
+        up = weave(even, odd, up_ref, size)
+        current = cur_ref[...]
+        inverse = 1.0 / (BACKGROUND + current[bands])
+        blend = (current[:bands] - up[:bands]) * inverse + up[bands:]
+        blend = blend * inside(level, blend.shape[1])
+    stacked = jnp.concatenate([g1_ref[:bands], blend], axis=0)
+    k, c, r = stacked.shape
+    wide = dot2(stacked.reshape(k * c, r), grow1_ref[...]).reshape(k, c, plan.rows)
+    half = w // 2
+    a, b, c = wide[:, :half], wide[:, 1 : half + 1], wide[:, 2 : half + 2]
+    even, odd = (a + 6.0 * b + c) * 0.125, (b + c) * 0.5
+    up = weave(even, odd, e0_ref, w)
+    inverse = 1.0 / (BACKGROUND + a0_ref[bands])
+    for f in range(bands):
+        value = (a0_ref[f] - up[f]) * inverse + up[bands + f]
+        out_ref[f] = value.astype(BF)
+
+
+def strip_local(scenes, cloud, destination, offset, counts):
+    n, m = lax.axis_size("tx"), lax.axis_size("ty")
+    row_tile, col_tile = lax.axis_index("tx"), lax.axis_index("ty")
+    bands = scenes.shape[2]
+    plan = Plan(n, m, bands)
+    planes = bands + 1
+    area = BS * BS
+    vmem = pl.BlockSpec(memory_space=pltpu.VMEM)
+    smem = pl.BlockSpec(memory_space=pltpu.SMEM)
+    blocks = jnp.swapaxes(scenes[0], 0, 1)
+    note = pl.pallas_call(
+        functools.partial(note_kernel, plan),
+        out_shape=jax.ShapeDtypeStruct((S_DEV + 16, area), BF),
+        in_specs=[smem, vmem, vmem, vmem],
+        out_specs=vmem,
+        name="note",
+    )(counts, cloud[0], destination, offset)
+
+    def swap(value, mask):
+        return lax.ppermute(value, "tx", [(i, i ^ mask) for i in range(n)])
+
+    gathered = [(blocks, note)]
+    mask = 1
+    masks = []
+    while mask < n:
+        masks.append(2 * mask - 1)
+        mask *= 2
+    for mask in masks:
+        gathered = gathered + [(swap(b, mask), swap(s, mask)) for b, s in gathered]
+
+    column = lax.dynamic_index_in_dim(
+        jnp.asarray(plan.column_tables()), row_tile * m + col_tile, keepdims=False
+    )
+    shrinks = row_shrinks(plan.rows)
+    row1 = jnp.asarray(shrinks[0].T.astype(BF))
+    row2 = jnp.asarray(shrinks[1].T.astype(BF))
+    top = plan.rows >> 3
+    wide_top = max(top, 128)
+    padded = np.zeros((plan.rows, wide_top))
+    padded[:, :top] = shrinks[2].T
+    row3 = jnp.asarray(np.stack(split_table(padded)))
+    size = plan.size
+    shapes = [
+        (planes, size[0], plan.rows),
+        (planes, size[1], plan.rows >> 1),
+        (planes, size[2], plan.rows >> 2),
+        (planes, size[3], wide_top),
+    ]
+    edge_lanes = sum(s[-1] for s in shapes[1:])
+    edge_shape = (up8(EDGE * planes), edge_lanes)
+    a0, a1, a2, a3, edge = pl.pallas_call(
+        functools.partial(place_kernel, plan),
+        out_shape=[jax.ShapeDtypeStruct(s, F32) for s in shapes + [edge_shape]],
+        in_specs=[vmem] * (2 * n + 4),
+        out_specs=[vmem] * 5,
+        scratch_shapes=[
+            pltpu.VMEM((2 * n * S_DEV, area), BF),
+            pltpu.VMEM((plan.rows, TS), F32),
+            pltpu.VMEM((planes, size[1] + 8, plan.rows), F32),
+            pltpu.VMEM((planes, size[2] + 8, plan.rows), F32),
+            pltpu.VMEM((planes, size[3] + 8, plan.rows), F32),
+        ],
+        name="place",
+    )(*[b for b, _ in gathered], *[s for _, s in gathered], column, row1, row2, row3)
+
+    pairs = []
+    for t in range(n):
+        for j in range(m):
+            other = (j + 1) % m if 2 * t < n else (j - 1) % m
+            pairs.append((t * m + j, t * m + other))
+    edge = lax.ppermute(edge, ("tx", "ty"), pairs)
+
+    first, last = row_tile == 0, row_tile == n - 1
+    flags = jnp.stack(
+        [first & (col_tile > 0), last & (col_tile < m - 1), first & (col_tile == 0), last & (col_tile == m - 1)]
+    ).astype(jnp.int32)
+    grow3 = np.zeros((wide_top, plan.rows >> 2))
+    grow3[:top] = grow_grid(top).T
+    grow2 = grow_grid(plan.rows >> 2).T
+    grow1 = grow_grid(plan.rows >> 1).T
+    out = pl.pallas_call(
+        functools.partial(blend_kernel, plan),
+        out_shape=jax.ShapeDtypeStruct((bands, size[0], plan.rows), BF),
+        in_specs=[smem] + [vmem] * 8,
+        out_specs=vmem,
+        scratch_shapes=[
+            pltpu.VMEM(shapes[1], F32),
+            pltpu.VMEM(shapes[2], F32),
+            pltpu.VMEM(shapes[3], F32),
+            pltpu.VMEM((2 * bands, (plan.rows >> 2) // TS, size[2], TS), F32),
+            pltpu.VMEM((2 * bands, (plan.rows >> 1) // TS, size[1], TS), F32),
+            pltpu.VMEM((2 * bands, plan.rows // TS, size[0], TS), F32),
+        ],
+        name="blend",
+    )(
+        flags, a0, a1, a2, a3, edge,
+        jnp.asarray(grow1.astype(BF)), jnp.asarray(grow2.astype(BF)), jnp.asarray(grow3.astype(BF)),
+    )
+    return out[:, None]
+
+
+def use_strips(n, m):
+    power = n & (n - 1) == 0
+    spread = max(2, 2 * S_DEV // n)
+    return power and 2 <= n and TS // n >= 32 and m >= 2 and S_DEV <= 2 * spread
+
+
 def solution(mesh):
     placed = (
         P(("region", "ty"), "tx", "band", None),
@@ -182,8 +578,9 @@
         P(("region", "ty"), "tx"),
         P(("region", "ty"), "tx"),
     )
+    body = strip_local if use_strips(mesh.shape["tx"], mesh.shape["ty"]) else local
     return jax.shard_map(
-        local,
+        body,
         mesh=mesh,
         in_specs=placed,
         out_specs=P("band", ("region", "ty"), "tx", None),

time: 95.7 us -> 44.6 us (0.47)
  matrix products: 18.4 us -> 0 us
  local copies, waits for them, and re-layouts: 18.5 us -> 3.43 us
  blocking collectives: 10.7 us -> 0 us
  Pallas kernels: 0 us -> 8.92 us
  waiting for transfers between devices: 17.8 us -> 12.1 us
  other arithmetic: 6.16 us -> 0.6 us
  starting transfers between devices: 22.5 us -> 18.5 us
    dot_general x21 -> x0, matrix products: 18.4 us -> none  [the longest x1 5.9 us: local(): jnp.dot(landing.astype(jnp.float32), payload, precision=lax.Precision.HIG...]
    all_to_all x2 -> x0, waiting for transfers between devices: 14.4 us -> none  [the longest x1 11.7 us: local(): lax.all_to_all(packed, 'tx', split_axis=0, concat_axis=0, tiled=True)]
    all_to_all x1 -> x0, blocking collectives: 10.7 us -> none  [local(): lax.all_to_all(flipped, 'tx', split_axis=1, concat_axis=2, tiled=True)]
    all_to_all x2 -> x0, starting transfers between devices: 9.81 us -> none  [the longest x1 6.35 us: local(): lax.all_to_all(tag_send, 'tx', split_axis=0, concat_axis=0, tiled=True)]
    pallas_call x0 -> x3, Pallas kernels: none -> 8.92 us  [the longest x1 4.69 us: strip_local(): pl.pallas_call(functools.partial(place_kernel, plan), out_shape=[jax.Shap...]
    ppermute x4 -> x7, waiting for transfers between devices: 3.41 us -> 12.1 us  [the longest x6 9.9 us: swap(): return lax.ppermute(value, 'tx', [(i, i ^ mask) for i in range(n)])]
    reshape x5 -> x0, local copies, waits for them, and re-layouts: 8.68 us -> none  [the longest x2 7.26 us: local(): tile_field = tile_field.reshape(own_bands + 1, TS, TS)]
    slice x5 -> x0, local copies, waits for them, and re-layouts: 7.4 us -> none  [the longest x4 6.24 us: local(): current[:own_bands]]
  transfers between devices with their start and end apart: 6 -> 7, of which waited for: 6 -> 4; matrix products, arithmetic and copies ran while one was open for 9% -> 5% of each run, Pallas kernels for 0% -> 3%
where the time goes in v1:
time: 44.6 us; the launch traced here: 44.3 us
  starting transfers between devices  18.5 us (41%)
  waiting for transfers between devices  12.1 us (27%)
  Pallas kernels  8.92 us (20%)
  local copies, waits for them, and re-layouts  3.43 us (8%)
  between operations  0.69 us (2%)
  other arithmetic  0.6 us (1%)
    ppermute x6, starting transfers between devices, swap(): return lax.ppermute(value, 'tx', [(i, i ^ mask) for i in range(n)])  17 us
    ppermute x6, waiting for transfers between devices, swap(): return lax.ppermute(value, 'tx', [(i, i ^ mask) for i in range(n)])  9.9 us
    pallas_call x1, Pallas kernels, strip_local(): pl.pallas_call(functools.partial(place_kernel, plan), out_shape=[jax.Shap...  4.69 us
    pallas_call x1, Pallas kernels, strip_local(): pl.pallas_call(functools.partial(blend_kernel, plan), out_shape=jax.Shape...  2.82 us
    ppermute x1, waiting for transfers between devices, strip_local(): edge = lax.ppermute(edge, ('tx', 'ty'), pairs)  2.21 us
    unnamed x14, local copies, waits for them, and re-layouts  1.97 us
    ppermute x1, starting transfers between devices, strip_local(): edge = lax.ppermute(edge, ('tx', 'ty'), pairs)  1.49 us
    squeeze x1, local copies, waits for them, and re-layouts, strip_local(): lax.dynamic_index_in_dim(jnp.asarray(plan.column_tables()), row_tile * m...  1.46 us
  transfers between devices with their start and end apart: 7, of which 4 were waited for; matrix products, arithmetic and copies ran while one was open for 5% of the time, Pallas kernels for 3%

profile of v1, /device:TPU:0, one launch (start us, length us, event | category | flops | bytes accessed | tf_op | source)
XLA Modules:
  0.0 44.3 jit_solution(15213454061948161937)
XLA Ops:
  0.0 3.1 %collective-permute-start = (bf16[6,64,256]{2,1,0:T(8,128)(2,1)}, bf16[6,64,256]{2,1,0:T(8,128)(2,1)S(1)}, u32[]{:S(2)}, u32[]{:S(2)}) collective-permute-start(bf16[6,64,256]{2,1,0:T(8,128)(2,1)} %bitcast.13), channel_id=1, source_target_pairs={{0,4},{4,0},{8,12},{12,8},{1,5},{5,1},{9,13},{13,9},{2,6},{6,2},{1... | collective-permute-start | bytes 589832 | tf_op jit(solution)/shard_map/ppermute | solution.py:485
  3.1 2.5 %collective-permute-start.1 = (bf16[6,64,256]{2,1,0:T(8,128)(2,1)}, bf16[6,64,256]{2,1,0:T(8,128)(2,1)S(1)}, u32[]{:S(2)}, u32[]{:S(2)}) collective-permute-start(bf16[6,64,256]{2,1,0:T(8,128)(2,1)} %bitcast.14), channel_id=1, source_target_pairs={{0,12},{4,8},{8,4},{12,0},{1,13},{5,9},{9,5},{13,1},{2,14},{6,10},... | collective-permute-start | bytes 589832 | tf_op jit(solution)/shard_map/ppermute | solution.py:485
  5.5 3.1 %collective-permute-done.refs_1_ = bf16[6,64,256]{2,1,0:T(8,128)(2,1)S(1)} collective-permute-done((bf16[6,64,256]{2,1,0:T(8,128)(2,1)}, bf16[6,64,256]{2,1,0:T(8,128)(2,1)S(1)}, u32[]{:S(2)}, u32[]{:S(2)}) %collective-permute-start) | collective-permute-done | bytes 196640 | tf_op jit(solution)/shard_map/ppermute | solution.py:485
  8.7 0.0 copy-start
  8.7 9.7 %collective-permute-start.2 = (bf16[6,64,256]{2,1,0:T(8,128)(2,1)S(1)}, bf16[6,64,256]{2,1,0:T(8,128)(2,1)S(1)}, u32[]{:S(2)}, u32[]{:S(2)}) collective-permute-start(bf16[6,64,256]{2,1,0:T(8,128)(2,1)S(1)} %collective-permute-done.refs_1_), channel_id=1, source_target_pairs={{0,12},{4,8},{8,4},{12,0},{1,13},{5,9},{9,5},{13,1},{2,14},{6,10},... | collective-permute-start | bytes 589832 | tf_op jit(solution)/shard_map/ppermute | solution.py:485
  19.0 1.4 %note.1.refs_4_ = bf16[80,256]{1,0:T(8,128)(2,1)} custom-call(s32[1,1]{1,0:T(1,128)S(6)} %copy.14.count_ref, bf16[64,256]{1,0:T(8,128)(2,1)} %bitcast.16, s32[1,64]{1,0:T(1,128)} %dest_ref.1, s32[1,64]{1,0:T(1,128)} %offset_ref.1), custom_call_target="tpu_custom_call" | custom-call | tf_op jit(solution)/shard_map/note/pallas_call | solution.py:476
  20.4 0.0 collective-permute-start.3
  20.4 0.0 collective-permute-start.4
  20.4 4.2 %collective-permute-done.3.refs_5_ = bf16[80,256]{1,0:T(8,128)(2,1)S(1)} collective-permute-done((bf16[80,256]{1,0:T(8,128)(2,1)}, bf16[80,256]{1,0:T(8,128)(2,1)S(1)}, u32[]{:S(2)}, u32[]{:S(2)}) %collective-permute-start.3) | collective-permute-done | bytes 40992 | tf_op jit(solution)/shard_map/ppermute | solution.py:485
  24.6 0.0 copy-start.4
  24.7 1.8 %collective-permute-start.5 = (bf16[80,256]{1,0:T(8,128)(2,1)S(1)}, bf16[80,256]{1,0:T(8,128)(2,1)S(1)}, u32[]{:S(2)}, u32[]{:S(2)}) collective-permute-start(bf16[80,256]{1,0:T(8,128)(2,1)S(1)} %collective-permute-done.3.refs_5_), channel_id=1, source_target_pairs={{0,12},{4,8},{8,4},{12,0},{1,13},{5,9},{9,5},{13,1},{2,14},{6,10},... | collective-permute-start | bytes 122888 | tf_op jit(solution)/shard_map/ppermute | solution.py:485
  26.4 1.5 %dynamic-slice_bitcast_fusion.refs_8_ = bf16[120,256]{1,0:T(8,128)(2,1)} fusion(bf16[8,120,256]{2,1,0:T(8,128)(2,1)} %constant.36.clone, s32[]{:T(128)S(6)} %select_n.4), kind=kLoop, calls=%fused_computation | loop fusion | bytes 122884 | tf_op jit(solution)/shard_map/jit(dynamic_index_in_dim)/squeeze | solution.py:496
  27.9 0.0 collective-permute-done.4.refs_6_
  27.9 0.0 copy-start.5
  27.9 2.6 %collective-permute-done.5.refs_7_ = bf16[80,256]{1,0:T(8,128)(2,1)S(1)} collective-permute-done((bf16[80,256]{1,0:T(8,128)(2,1)S(1)}, bf16[80,256]{1,0:T(8,128)(2,1)S(1)}, u32[]{:S(2)}, u32[]{:S(2)}) %collective-permute-start.5) | collective-permute-done | bytes 40992 | tf_op jit(solution)/shard_map/ppermute | solution.py:485
  30.5 0.0 copy-start.6
  30.5 0.0 collective-permute-done.1.refs_2_
  30.5 0.0 copy-start.1
  30.5 0.0 collective-permute-done.2.refs_3_
  30.5 0.0 copy-done
  30.5 0.0 copy-done.4
  30.5 0.0 copy-done.5
  30.5 0.6 %copy-done.6 = bf16[80,256]{1,0:T(8,128)(2,1)} copy-done((bf16[80,256]{1,0:T(8,128)(2,1)}, bf16[80,256]{1,0:T(8,128)(2,1)S(1)}, u32[]{:S(2)}) %copy-start.6) | copy-done | bytes 40984
  31.1 0.1 copy-done.1
  31.1 0.0 copy-start.2
  31.1 0.7 %copy-done.2 = bf16[6,64,256]{2,1,0:T(8,128)(2,1)} copy-done((bf16[6,64,256]{2,1,0:T(8,128)(2,1)}, bf16[6,64,256]{2,1,0:T(8,128)(2,1)S(1)}, u32[]{:S(2)}) %copy-start.2) | copy-done | bytes 196632
  31.8 4.7 %place.1 = (f32[7,32,512]{2,1,0:T(8,128)}, f32[7,24,256]{2,1,0:T(8,128)}, f32[7,16,128]{2,1,0:T(8,128)}, f32[7,8,128]{2,1,0:T(8,128)}, f32[24,512]{1,0:T(8,128)}) custom-call(bf16[6,64,256]{2,1,0:T(8,128)(2,1)} %bitcast.15, bf16[6,64,256]{2,1,0:T(8,128)(2,1)} %copy-done, bf16[6,64,256]{2,1,0:T(8,128)(2,1)} %copy-done.1, bf16[6,64,256]{2,1,0:T(8,128)(2,1)} %copy-done.2, ...), custom_call_target="tpu_custom_call" | custom-call | tf_op jit(solution)/shard_map/place/pallas_call | solution.py:516
  36.5 1.5 %collective-permute-start.6 = (f32[24,512]{1,0:T(8,128)}, f32[24,512]{1,0:T(8,128)S(1)}, u32[]{:S(2)}, u32[]{:S(2)}) collective-permute-start(f32[24,512]{1,0:T(8,128)} %get-tuple-element.14), channel_id=1, source_target_pairs={{0,2},{2,0},{4,6},{6,4},{8,10},{10,8},{12,14},{14,12},{1,3},{3,1},... | collective-permute-start | bytes 147464 | tf_op jit(solution)/shard_map/ppermute | solution.py:536
  38.0 0.6 %add_convert_fusion.flag_ref = s32[4]{0:T(128)} fusion(pred[1]{0:T(512)(128)(4,1)} %bitcast.3, pred[1]{0:T(512)(128)(4,1)} %bitcast.2, pred[1]{0:T(512)(128)(4,1)} %bitcast.1, pred[1]{0:T(512)(128)(4,1)} %bitcast), kind=kLoop, calls=%fused_computation.1 | loop fusion | flops 16 | bytes 20 | tf_op jit(solution)/shard_map/convert_element_type | solution.py:541
  38.6 2.2 %collective-permute-done.6.edge_ref = f32[24,512]{1,0:T(8,128)S(1)} collective-permute-done((f32[24,512]{1,0:T(8,128)}, f32[24,512]{1,0:T(8,128)S(1)}, u32[]{:S(2)}, u32[]{:S(2)}) %collective-permute-start.6) | collective-permute-done | bytes 49184 | tf_op jit(solution)/shard_map/ppermute | solution.py:536
  40.8 0.0 copy-start.3
  40.8 0.6 %copy-done.3 = f32[24,512]{1,0:T(8,128)} copy-done((f32[24,512]{1,0:T(8,128)}, f32[24,512]{1,0:T(8,128)S(1)}, u32[]{:S(2)}) %copy-start.3) | copy-done | bytes 49176
  41.4 2.8 %blend.1 = bf16[6,32,512]{2,1,0:T(8,128)(2,1)} custom-call(s32[4]{0:T(128)} %add_convert_fusion.flag_ref, f32[7,32,512]{2,1,0:T(8,128)} %get-tuple-element.10.a0_ref, f32[7,24,256]{2,1,0:T(8,128)} %get-tuple-element.11.a1_ref, f32[7,16,128]{2,1,0:T(8,128)} %get-tuple-element.12.a2_ref, f32[7,8,128]{2,1,0:T(8,128)} %get-tuple-element.13.a3_ref, ...), custom_call_target="tpu_custom_call" | custom-call | tf_op jit(solution)/shard_map/blend/pallas_call | solution.py:546
Async XLA Ops:
  0.0 8.7 %collective-permute-start = (bf16[6,64,256]{2,1,0:T(8,128)(2,1)}, bf16[6,64,256]{2,1,0:T(8,128)(2,1)S(1)}, u32[]{:S(2)}, u32[]{:S(2)}) collective-permute-start(bf16[6,64,256]{2,1,0:T(8,128)(2,1)} %bitcast.13), channel_id=1, source_target_pairs={{0,4},{4,0},{8,12},{12,8},{1,5},{5,1},{9,13},{13,9},{2,6},{6,2},{1... | collective-permute-start | bytes 589832 | tf_op jit(solution)/shard_map/ppermute | solution.py:485
  3.1 27.4 %collective-permute-start.1 = (bf16[6,64,256]{2,1,0:T(8,128)(2,1)}, bf16[6,64,256]{2,1,0:T(8,128)(2,1)S(1)}, u32[]{:S(2)}, u32[]{:S(2)}) collective-permute-start(bf16[6,64,256]{2,1,0:T(8,128)(2,1)} %bitcast.14), channel_id=1, source_target_pairs={{0,12},{4,8},{8,4},{12,0},{1,13},{5,9},{9,5},{13,1},{2,14},{6,10},... | collective-permute-start | bytes 589832 | tf_op jit(solution)/shard_map/ppermute | solution.py:485
  8.7 21.8 %copy-start = (bf16[6,64,256]{2,1,0:T(8,128)(2,1)}, bf16[6,64,256]{2,1,0:T(8,128)(2,1)S(1)}, u32[]{:S(2)}) copy-start(bf16[6,64,256]{2,1,0:T(8,128)(2,1)S(1)} %collective-permute-done.refs_1_) | copy-start | bytes 589828
  8.7 21.8 %collective-permute-start.2 = (bf16[6,64,256]{2,1,0:T(8,128)(2,1)S(1)}, bf16[6,64,256]{2,1,0:T(8,128)(2,1)S(1)}, u32[]{:S(2)}, u32[]{:S(2)}) collective-permute-start(bf16[6,64,256]{2,1,0:T(8,128)(2,1)S(1)} %collective-permute-done.refs_1_), channel_id=1, source_target_pairs={{0,12},{4,8},{8,4},{12,0},{1,13},{5,9},{9,5},{13,1},{2,14},{6,10},... | collective-permute-start | bytes 589832 | tf_op jit(solution)/shard_map/ppermute | solution.py:485
  20.4 4.2 %collective-permute-start.3 = (bf16[80,256]{1,0:T(8,128)(2,1)}, bf16[80,256]{1,0:T(8,128)(2,1)S(1)}, u32[]{:S(2)}, u32[]{:S(2)}) collective-permute-start(bf16[80,256]{1,0:T(8,128)(2,1)} %note.1.refs_4_), channel_id=1, source_target_pairs={{0,4},{4,0},{8,12},{12,8},{1,5},{5,1},{9,13},{13,9},{2,6},{6,2},{1... | collective-permute-start | bytes 122888 | tf_op jit(solution)/shard_map/ppermute | solution.py:485
  20.4 7.5 %collective-permute-start.4 = (bf16[80,256]{1,0:T(8,128)(2,1)}, bf16[80,256]{1,0:T(8,128)(2,1)S(1)}, u32[]{:S(2)}, u32[]{:S(2)}) collective-permute-start(bf16[80,256]{1,0:T(8,128)(2,1)} %note.1.refs_4_), channel_id=1, source_target_pairs={{0,12},{4,8},{8,4},{12,0},{1,13},{5,9},{9,5},{13,1},{2,14},{6,10},... | collective-permute-start | bytes 122888 | tf_op jit(solution)/shard_map/ppermute | solution.py:485
  24.6 5.8 %copy-start.4 = (bf16[80,256]{1,0:T(8,128)(2,1)}, bf16[80,256]{1,0:T(8,128)(2,1)S(1)}, u32[]{:S(2)}) copy-start(bf16[80,256]{1,0:T(8,128)(2,1)S(1)} %collective-permute-done.3.refs_5_) | copy-start | bytes 122884
  24.7 5.8 %collective-permute-start.5 = (bf16[80,256]{1,0:T(8,128)(2,1)S(1)}, bf16[80,256]{1,0:T(8,128)(2,1)S(1)}, u32[]{:S(2)}, u32[]{:S(2)}) collective-permute-start(bf16[80,256]{1,0:T(8,128)(2,1)S(1)} %collective-permute-done.3.refs_5_), channel_id=1, source_target_pairs={{0,12},{4,8},{8,4},{12,0},{1,13},{5,9},{9,5},{13,1},{2,14},{6,10},... | collective-permute-start | bytes 122888 | tf_op jit(solution)/shard_map/ppermute | solution.py:485
  27.9 2.6 %copy-start.5 = (bf16[80,256]{1,0:T(8,128)(2,1)}, bf16[80,256]{1,0:T(8,128)(2,1)S(1)}, u32[]{:S(2)}) copy-start(bf16[80,256]{1,0:T(8,128)(2,1)S(1)} %collective-permute-done.4.refs_6_) | copy-start | bytes 122884
  30.5 0.6 %copy-start.6 = (bf16[80,256]{1,0:T(8,128)(2,1)}, bf16[80,256]{1,0:T(8,128)(2,1)S(1)}, u32[]{:S(2)}) copy-start(bf16[80,256]{1,0:T(8,128)(2,1)S(1)} %collective-permute-done.5.refs_7_) | copy-start | bytes 122884
  30.5 0.7 %copy-start.1 = (bf16[6,64,256]{2,1,0:T(8,128)(2,1)}, bf16[6,64,256]{2,1,0:T(8,128)(2,1)S(1)}, u32[]{:S(2)}) copy-start(bf16[6,64,256]{2,1,0:T(8,128)(2,1)S(1)} %collective-permute-done.1.refs_2_) | copy-start | bytes 589828
  31.1 0.7 %copy-start.2 = (bf16[6,64,256]{2,1,0:T(8,128)(2,1)}, bf16[6,64,256]{2,1,0:T(8,128)(2,1)S(1)}, u32[]{:S(2)}) copy-start(bf16[6,64,256]{2,1,0:T(8,128)(2,1)S(1)} %collective-permute-done.2.refs_3_) | copy-start | bytes 589828
  36.5 4.3 %collective-permute-start.6 = (f32[24,512]{1,0:T(8,128)}, f32[24,512]{1,0:T(8,128)S(1)}, u32[]{:S(2)}, u32[]{:S(2)}) collective-permute-start(f32[24,512]{1,0:T(8,128)} %get-tuple-element.14), channel_id=1, source_target_pairs={{0,2},{2,0},{4,6},{6,4},{8,10},{10,8},{12,14},{14,12},{1,3},{3,1},... | collective-permute-start | bytes 147464 | tf_op jit(solution)/shard_map/ppermute | solution.py:536
  40.8 0.6 %copy-start.3 = (f32[24,512]{1,0:T(8,128)}, f32[24,512]{1,0:T(8,128)S(1)}, u32[]{:S(2)}) copy-start(f32[24,512]{1,0:T(8,128)S(1)} %collective-permute-done.6.edge_ref) | copy-start | bytes 147460

commit v2 on v1

--- a/solution.py
+++ b/solution.py
@@ -7,6 +7,7 @@
 from jax.experimental import pallas as pl
 from jax.experimental.pallas import tpu as pltpu
 from jax.sharding import PartitionSpec as P
+
 
 TS = 128
 BS = 16
@@ -151,11 +152,11 @@
     ground = with_halo(tile_field, (("tx", 1), ("ty", 2)), MARGIN)
     margin = MARGIN
     needed = [0]
-    for tier_index in range(1, LEVELS):
+    for _ in range(1, LEVELS):
         needed.append((needed[-1] + 3) // 2)
     pyramid = [(ground, margin)]
     extent = TS
-    for tier_index in range(1, LEVELS):
+    for _ in range(1, LEVELS):
         source, rim_in = pyramid[-1]
         rim_out = (rim_in - 2) // 2
         extent = extent // 2
@@ -182,6 +183,7 @@
 BF = jnp.bfloat16
 F32 = jnp.float32
 EDGE = 3
+CODE_ROWS = 8
 
 
 def up8(v):
@@ -285,55 +287,88 @@
     )
 
 
-def note_kernel(plan, count_ref, cloud_ref, dest_ref, offset_ref, out_ref):
-    out_ref[:S_DEV, :] = cloud_ref[...]
+def pack_kernel(plan, count_ref, scenes_ref, cloud_ref, dest_ref, offset_ref, out_ref, dest, offset, sems):
+    rows = plan.bands * S_DEV
+    copies = [
+        pltpu.make_async_copy(source, target, sems.at[k])
+        for k, (source, target) in enumerate(
+            (
+                (dest_ref, dest),
+                (offset_ref, offset),
+                (cloud_ref, out_ref.at[pl.ds(rows, S_DEV)]),
+                (scenes_ref, out_ref.at[pl.ds(0, rows)]),
+            )
+        )
+    ]
+    for copy in copies:
+        copy.start()
+    for copy in copies[:2]:
+        copy.wait()
     per_row = TS // BS
-    offset = offset_ref[...]
-    code = (offset % per_row) * plan.slot_rows + dest_ref[...] * per_row + offset // per_row
+    slot = offset[...]
+    code = (slot % per_row) * plan.slot_rows + dest[...] * per_row + slot // per_row
     live = lax.broadcasted_iota(jnp.int32, (1, S_DEV), 1) < count_ref[0, 0]
     code = jnp.where(live, code, -1).astype(F32)
-    tail = out_ref.shape[0] - S_DEV
-    out_ref[S_DEV:, :] = jnp.full((tail, BS * BS), -1.0, BF)
-    out_ref[S_DEV:, :S_DEV] = jnp.broadcast_to(code, (tail, S_DEV)).astype(BF)
-
-
-def place_kernel(plan, *refs):
-    n, bands = plan.n, plan.bands
-    scenes, notes = refs[:n], refs[n : 2 * n]
-    column_ref, row1_ref, row2_ref, row3_ref, a0_ref, a1_ref, a2_ref, a3_ref, edge_ref = refs[
-        2 * n : 2 * n + 9
-    ]
-    prod_ref, tile_ref, z1_ref, z2_ref, z3_ref = refs[2 * n + 9 :]
-    blocks = n * S_DEV
+    rows += S_DEV
+    tail = out_ref.shape[0] - rows
+    out_ref[rows:, :] = jnp.full((tail, BS * BS), -1.0, BF)
+    out_ref[rows:, :S_DEV] = jnp.broadcast_to(code, (tail, S_DEV)).astype(BF)
+    for copy in copies[2:]:
+        copy.wait()
+
+
+def landing_of(plan, packs):
+    tail = slice((plan.bands + 1) * S_DEV, (plan.bands + 1) * S_DEV + CODE_ROWS)
+    codes = packs[0][tail, :].astype(F32)
+    for p in range(1, len(packs)):
+        codes = jnp.maximum(codes, pltpu.roll(packs[p][tail, :].astype(F32), S_DEV * p, 1))
+    blocks = len(packs) * S_DEV
+    slot = lax.broadcasted_iota(jnp.int32, (plan.slots, blocks), 0).astype(F32)
+    landing = jnp.where(slot == codes[:1, :blocks], 1.0, 0.0).astype(BF)
+    return jnp.concatenate([landing, landing], axis=1)
+
+
+def slot_sums(plan, packs, landing2, prod_ref, f):
+    blocks = len(packs) * S_DEV
+    weights = pl.ds(plan.bands * S_DEV, S_DEV)
+    for p, pack in enumerate(packs):
+        weight = pack[weights, :]
+        if f == plan.bands:
+            prod_ref[pl.ds(p * S_DEV, S_DEV), :] = weight
+            continue
+        value = pack[f * S_DEV : (f + 1) * S_DEV, :].astype(F32) * weight.astype(F32)
+        high, low = halves(value)
+        prod_ref[pl.ds(p * S_DEV, S_DEV), :] = high
+        prod_ref[pl.ds(blocks + p * S_DEV, S_DEV), :] = low
+    used = blocks if f == plan.bands else 2 * blocks
+    return jnp.dot(landing2[:, :used], prod_ref[:used, :], preferred_element_type=F32)
+
+
+def sum_kernel(plan, count, *refs):
+    packs, rest = refs[:count], refs[count:]
+    before_ref = rest[0] if len(rest) == 3 else None
+    out_ref, prod_ref = rest[-2:]
+    landing2 = landing_of(plan, packs)
+    for f in range(plan.bands + 1):
+        sums = slot_sums(plan, packs, landing2, prod_ref, f)
+        out_ref[f] = sums if before_ref is None else before_ref[f] + sums
+
+
+def place_kernel(plan, count, *refs):
+    bands = plan.bands
+    packs = refs[:count]
+    before_ref, column_ref, row1_ref, row2_ref, row3_ref = refs[count : count + 5]
+    a0_ref, a1_ref, a2_ref, a3_ref, edge_ref = refs[count + 5 : count + 10]
+    prod_ref, sums_ref, tile_ref, z1_ref, z2_ref, z3_ref = refs[count + 10 :]
     area = BS * BS
-    codes = notes[0][S_DEV : S_DEV + 16, :].astype(F32)
-    for p in range(1, n):
-        codes = jnp.maximum(
-            codes, pltpu.roll(notes[p][S_DEV : S_DEV + 16, :].astype(F32), S_DEV * p, 1)
-        )
-    codes = codes[:1, :blocks]
-    slot = lax.broadcasted_iota(jnp.int32, (plan.slots, blocks), 0).astype(F32)
-    landing = jnp.where(slot == codes, 1.0, 0.0).astype(BF)
-    landing2 = jnp.concatenate([landing, landing], axis=1)
+    landing2 = landing_of(plan, packs)
     group = lax.broadcasted_iota(jnp.int32, (plan.slot_rows, TS), 1) // BS
     per_row = TS // BS
     column = column_ref[...]
-    e1 = plan.size[1]
     for f in range(bands + 1):
-        for p in range(n):
-            weight = notes[p][:S_DEV, :]
-            at = pl.ds(p * S_DEV, S_DEV)
-            if f == bands:
-                prod_ref[at, :] = weight
-            else:
-                value = scenes[p][f].astype(F32) * weight.astype(F32)
-                high, low = halves(value)
-                prod_ref[at, :] = high
-                prod_ref[pl.ds(blocks + p * S_DEV, S_DEV), :] = low
-        if f == bands:
-            sums = jnp.dot(landing, prod_ref[:blocks, :], preferred_element_type=F32)
-        else:
-            sums = jnp.dot(landing2, prod_ref[...], preferred_element_type=F32)
+        sums_ref[f] = before_ref[f] + slot_sums(plan, packs, landing2, prod_ref, f)
+    for f in range(bands + 1):
+        sums = sums_ref[f]
         for half in range(area // TS):
             part = [
                 sums[b * plan.slot_rows : (b + 1) * plan.slot_rows, half * TS : (half + 1) * TS]
@@ -463,6 +498,14 @@
         out_ref[f] = value.astype(BF)
 
 
+def on_chip(value):
+    return pltpu.with_memory_space_constraint(value, pltpu.VMEM)
+
+
+def off_chip(value):
+    return pltpu.with_memory_space_constraint(value, pltpu.HBM)
+
+
 def strip_local(scenes, cloud, destination, offset, counts):
     n, m = lax.axis_size("tx"), lax.axis_size("ty")
     row_tile, col_tile = lax.axis_index("tx"), lax.axis_index("ty")
@@ -472,26 +515,54 @@
     area = BS * BS
     vmem = pl.BlockSpec(memory_space=pltpu.VMEM)
     smem = pl.BlockSpec(memory_space=pltpu.SMEM)
-    blocks = jnp.swapaxes(scenes[0], 0, 1)
-    note = pl.pallas_call(
-        functools.partial(note_kernel, plan),
-        out_shape=jax.ShapeDtypeStruct((S_DEV + 16, area), BF),
-        in_specs=[smem, vmem, vmem, vmem],
+    hbm = pl.BlockSpec(memory_space=pl.ANY)
+    blocks = jnp.swapaxes(scenes[0], 0, 1).reshape(bands * S_DEV, area)
+    pack = pl.pallas_call(
+        functools.partial(pack_kernel, plan),
+        out_shape=pltpu.VMEM((planes * S_DEV + CODE_ROWS, area), BF),
+        in_specs=[smem] + [hbm] * 4,
         out_specs=vmem,
-        name="note",
-    )(counts, cloud[0], destination, offset)
+        scratch_shapes=[
+            pltpu.VMEM(destination.shape, jnp.int32),
+            pltpu.VMEM(offset.shape, jnp.int32),
+            pltpu.SemaphoreType.DMA((4,)),
+        ],
+        compiler_params=pltpu.CompilerParams(vmem_limit_bytes=4 << 20),
+        name="pack",
+    )(counts, *[off_chip(v) for v in (blocks, cloud[0], destination, offset)])
 
     def swap(value, mask):
         return lax.ppermute(value, "tx", [(i, i ^ mask) for i in range(n)])
 
-    gathered = [(blocks, note)]
-    mask = 1
-    masks = []
-    while mask < n:
-        masks.append(2 * mask - 1)
-        mask *= 2
-    for mask in masks:
-        gathered = gathered + [(swap(b, mask), swap(s, mask)) for b, s in gathered]
+    def sum_blocks(packs, before):
+        count = len(packs)
+        operands = [on_chip(v) for v in packs + before]
+        return pl.pallas_call(
+            functools.partial(sum_kernel, plan, count),
+            out_shape=pltpu.VMEM((planes, plan.slots, area), F32),
+            in_specs=[vmem] * len(operands),
+            out_specs=vmem,
+            scratch_shapes=[pltpu.VMEM((2 * count * S_DEV, area), BF)],
+            input_output_aliases={count: 0} if before else {},
+            compiler_params=pltpu.CompilerParams(vmem_limit_bytes=4 << 20),
+            cost_estimate=pl.CostEstimate(
+                flops=4 * planes * plan.slots * area * count * S_DEV,
+                bytes_accessed=planes * plan.slots * area * 4,
+                transcendentals=0,
+            ),
+        )(*operands)
+
+    gathered = [pack]
+    sums = [sum_blocks([pack], [])]
+    mask = n - 1
+    while mask:
+        arrived = [swap(g, mask) for g in gathered]
+        if mask == 1:
+            early, late = gathered[1:] + arrived[:-1], arrived[-1:]
+            if early:
+                sums = [sum_blocks(early, sums)]
+        gathered = gathered + arrived
+        mask //= 2
 
     column = lax.dynamic_index_in_dim(
         jnp.asarray(plan.column_tables()), row_tile * m + col_tile, keepdims=False
@@ -514,19 +585,21 @@
     edge_lanes = sum(s[-1] for s in shapes[1:])
     edge_shape = (up8(EDGE * planes), edge_lanes)
     a0, a1, a2, a3, edge = pl.pallas_call(
-        functools.partial(place_kernel, plan),
-        out_shape=[jax.ShapeDtypeStruct(s, F32) for s in shapes + [edge_shape]],
-        in_specs=[vmem] * (2 * n + 4),
+        functools.partial(place_kernel, plan, len(late)),
+        out_shape=[pltpu.VMEM(s, F32) for s in shapes + [edge_shape]],
+        in_specs=[vmem] * (len(late) + 5),
+        compiler_params=pltpu.CompilerParams(vmem_limit_bytes=16 << 20),
         out_specs=[vmem] * 5,
         scratch_shapes=[
-            pltpu.VMEM((2 * n * S_DEV, area), BF),
+            pltpu.VMEM((2 * len(late) * S_DEV, area), BF),
+            pltpu.VMEM((planes, plan.slots, area), F32),
             pltpu.VMEM((plan.rows, TS), F32),
             pltpu.VMEM((planes, size[1] + 8, plan.rows), F32),
             pltpu.VMEM((planes, size[2] + 8, plan.rows), F32),
             pltpu.VMEM((planes, size[3] + 8, plan.rows), F32),
         ],
         name="place",
-    )(*[b for b, _ in gathered], *[s for _, s in gathered], column, row1, row2, row3)
+    )(*[on_chip(v) for v in late + sums], column, row1, row2, row3)
 
     pairs = []
     for t in range(n):
@@ -556,12 +629,17 @@
             pltpu.VMEM((2 * bands, (plan.rows >> 1) // TS, size[1], TS), F32),
             pltpu.VMEM((2 * bands, plan.rows // TS, size[0], TS), F32),
         ],
+        compiler_params=pltpu.CompilerParams(vmem_limit_bytes=16 << 20),
         name="blend",
     )(
-        flags, a0, a1, a2, a3, edge,
+        flags, *[on_chip(v) for v in (a0, a1, a2, a3, edge)],
         jnp.asarray(grow1.astype(BF)), jnp.asarray(grow2.astype(BF)), jnp.asarray(grow3.astype(BF)),
     )
     return out[:, None]
+
+
+def strip_step(*arguments):
+    return strip_local(*arguments)
 
 
 def use_strips(n, m):
@@ -578,9 +656,9 @@
         P(("region", "ty"), "tx"),
         P(("region", "ty"), "tx"),
     )
-    body = strip_local if use_strips(mesh.shape["tx"], mesh.shape["ty"]) else local
+    strips = use_strips(mesh.shape["tx"], mesh.shape["ty"])
     return jax.shard_map(
-        body,
+        strip_step if strips else local,
         mesh=mesh,
         in_specs=placed,
         out_specs=P("band", ("region", "ty"), "tx", None),

time: 44.6 us -> 31.7 us (0.71)
  starting transfers between devices: 18.5 us -> 10.5 us
  local copies, waits for them, and re-layouts: 3.43 us -> 0.88 us
  Pallas kernels: 8.92 us -> 6.82 us
  other arithmetic: 0.6 us -> 0.08 us
  waiting for transfers between devices: 12.1 us -> 12.6 us
    ppermute x6 -> x3, starting transfers between devices: 17 us -> 8.93 us  [swap(): return lax.ppermute(value, 'tx', [(i, i ^ mask) for i in range(n)])]
    unnamed x14 -> x12, local copies, waits for them, and re-layouts: 1.97 us -> 0.03 us
    pallas_call x2 -> x4, Pallas kernels: 6.1 us -> 4.69 us  [the longest x1 2.63 us: strip_local(): pl.pallas_call(functools.partial(place_kernel, plan, len(late)), out_shap...]
    pallas_call x1, Pallas kernels: 2.82 us -> 2.14 us  [strip_local(): pl.pallas_call(functools.partial(blend_kernel, plan), out_shape=jax.Shape...]
    squeeze x1, local copies, waits for them, and re-layouts: 1.46 us -> 0.84 us  [strip_local(): lax.dynamic_index_in_dim(jnp.asarray(plan.column_tables()), row_tile * m...]
    convert_element_type x1, other arithmetic: 0.6 us -> 0.08 us  [strip_local(): flags = jnp.stack([first & (col_tile > 0), last & (col_tile < m - 1), fir...]
    ppermute x6 -> x3, waiting for transfers between devices: 9.9 us -> 10 us  [swap(): return lax.ppermute(value, 'tx', [(i, i ^ mask) for i in range(n)])]
  transfers between devices with their start and end apart: 7 -> 4, of which waited for: 4 -> 3; matrix products, arithmetic and copies ran while one was open for 5% -> 3% of each run, Pallas kernels for 3% -> 3%
where the time goes in v2:
time: 31.7 us; the launch traced here: 31.6 us
  waiting for transfers between devices  12.6 us (40%)
  starting transfers between devices  10.5 us (33%)
  Pallas kernels  6.82 us (22%)
  local copies, waits for them, and re-layouts  0.88 us (3%)
  between operations  0.74 us (2%)
    ppermute x3, waiting for transfers between devices, swap(): return lax.ppermute(value, 'tx', [(i, i ^ mask) for i in range(n)])  10 us
    ppermute x3, starting transfers between devices, swap(): return lax.ppermute(value, 'tx', [(i, i ^ mask) for i in range(n)])  8.93 us
    pallas_call x1, Pallas kernels, strip_local(): pl.pallas_call(functools.partial(place_kernel, plan, len(late)), out_shap...  2.63 us
    ppermute x1, waiting for transfers between devices, strip_local(): edge = lax.ppermute(edge, ('tx', 'ty'), pairs)  2.52 us
    pallas_call x1, Pallas kernels, strip_local(): pl.pallas_call(functools.partial(blend_kernel, plan), out_shape=jax.Shape...  2.14 us
    ppermute x1, starting transfers between devices, strip_local(): edge = lax.ppermute(edge, ('tx', 'ty'), pairs)  1.55 us
    pallas_call x2, Pallas kernels, sum_blocks(): pl.pallas_call(functools.partial(sum_kernel, plan, count), out_shape=pltp...  1.04 us
    pallas_call x1, Pallas kernels, strip_local(): pl.pallas_call(functools.partial(pack_kernel, plan), out_shape=pltpu.VMEM...  1.01 us
  transfers between devices with their start and end apart: 4, of which 3 were waited for; matrix products, arithmetic and copies ran while one was open for 3% of the time, Pallas kernels for 3%

profile of v2, /device:TPU:0, one launch (start us, length us, event | category | flops | bytes accessed | tf_op | source)
XLA Modules:
  0.0 31.6 jit_solution(12357219752033401605)
XLA Ops:
  0.7 1.0 %pack.1.refs_0_ = bf16[456,256]{1,0:T(8,128)(2,1)S(1)} custom-call(s32[1,1]{1,0:T(1,128)S(6)} %copy.16.count_ref, bf16[384,256]{1,0:T(8,128)(2,1)} %bitcast.15, bf16[64,256]{1,0:T(8,128)(2,1)} %bitcast.16, s32[1,64]{1,0:T(1,128)} %dest_ref.1, s32[1,64]{1,0:T(1,128)} %offset_ref.1), custom_call_target="tpu_custom_call" | custom-call | tf_op jit(solution)/shard_map/pack/pallas_call | solution.py:520
  1.7 5.1 %collective-permute-start = (bf16[456,256]{1,0:T(8,128)(2,1)S(1)}, bf16[456,256]{1,0:T(8,128)(2,1)S(1)}, u32[]{:S(2)}, u32[]{:S(2)}) collective-permute-start(bf16[456,256]{1,0:T(8,128)(2,1)S(1)} %pack.1.refs_0_), channel_id=1, source_target_pairs={{0,12},{4,8},{8,4},{12,0},{1,13},{5,9},{9,5},{13,1},{2,14},{6,10},... | collective-permute-start | bytes 700424 | tf_op jit(solution)/shard_map/ppermute | solution.py:535
  6.8 0.0 collective-permute-start.2
  6.8 6.6 %collective-permute-done.refs_0_ = bf16[456,256]{1,0:T(8,128)(2,1)S(1)} collective-permute-done((bf16[456,256]{1,0:T(8,128)(2,1)S(1)}, bf16[456,256]{1,0:T(8,128)(2,1)S(1)}, u32[]{:S(2)}, u32[]{:S(2)}) %collective-permute-start) | collective-permute-done | bytes 233504 | tf_op jit(solution)/shard_map/ppermute | solution.py:535
  13.4 3.8 %collective-permute-start.1 = (bf16[456,256]{1,0:T(8,128)(2,1)S(1)}, bf16[456,256]{1,0:T(8,128)(2,1)S(1)}, u32[]{:S(2)}, u32[]{:S(2)}) collective-permute-start(bf16[456,256]{1,0:T(8,128)(2,1)S(1)} %collective-permute-done.refs_0_), channel_id=1, source_target_pairs={{0,4},{4,0},{8,12},{12,8},{1,5},{5,1},{9,13},{13,9},{2,6},{6,2},{1... | collective-permute-start | bytes 700424 | tf_op jit(solution)/shard_map/ppermute | solution.py:535
  17.2 0.4 %shard_map.118.refs_2_ = f32[7,256,256]{2,1,0:T(8,128)S(1)} custom-call(bf16[456,256]{1,0:T(8,128)(2,1)S(1)} %pack.1.refs_0_), custom_call_target="tpu_custom_call" | custom-call | flops 117440512 | bytes 1835008 | tf_op jit(solution)/shard_map/pallas_call | solution.py:540
  17.7 0.8 %dynamic-slice_bitcast_fusion.refs_2_ = bf16[120,256]{1,0:T(8,128)(2,1)S(1)} fusion(bf16[8,120,256]{2,1,0:T(8,128)(2,1)} %constant.36.clone, s32[]{:T(128)S(6)} %select_n.4), kind=kLoop, calls=%fused_computation | loop fusion | bytes 122884 | tf_op jit(solution)/shard_map/jit(dynamic_index_in_dim)/squeeze | solution.py:567
  18.5 0.0 copy-start.1
  18.5 0.0 copy-start.2
  18.5 0.0 copy-start.3
  18.5 0.0 collective-permute-done.2.refs_1_
  18.6 0.6 %shard_map.119.refs_1_ = f32[7,256,256]{2,1,0:T(8,128)S(1)} custom-call(bf16[456,256]{1,0:T(8,128)(2,1)S(1)} %collective-permute-done.refs_0_, bf16[456,256]{1,0:T(8,128)(2,1)S(1)} %collective-permute-done.2.refs_1_, f32[7,256,256]{2,1,0:T(8,128)S(1)} %shard_map.118.refs_2_), custom_call_target="tpu_custom_call", output_to_operand_aliasing={{}: (2, {})} | custom-call | flops 234881024 | bytes 1835008 | tf_op jit(solution)/shard_map/pallas_call | solution.py:540
  19.2 0.0 copy-start
  19.2 0.0 copy-start.4
  19.2 0.0 copy-start.5
  19.2 3.4 %collective-permute-done.1.refs_0_ = bf16[456,256]{1,0:T(8,128)(2,1)S(1)} collective-permute-done((bf16[456,256]{1,0:T(8,128)(2,1)S(1)}, bf16[456,256]{1,0:T(8,128)(2,1)S(1)}, u32[]{:S(2)}, u32[]{:S(2)}) %collective-permute-start.1) | collective-permute-done | bytes 233504 | tf_op jit(solution)/shard_map/ppermute | solution.py:535
  22.6 0.0 copy-done.1
  22.6 0.0 copy-done.2
  22.6 0.0 copy-done.3
  22.6 2.6 %place.1 = (f32[7,32,512]{2,1,0:T(8,128)S(1)}, f32[7,24,256]{2,1,0:T(8,128)S(1)}, f32[7,16,128]{2,1,0:T(8,128)S(1)}, f32[7,8,128]{2,1,0:T(8,128)S(1)}, f32[24,512]{1,0:T(8,128)S(1)}) custom-call(bf16[456,256]{1,0:T(8,128)(2,1)S(1)} %collective-permute-done.1.refs_0_, f32[7,256,256]{2,1,0:T(8,128)S(1)} %shard_map.119.refs_1_, ...), custom_call_target="tpu_custom_call" | custom-call | tf_op jit(solution)/shard_map/place/pallas_call | solution.py:587
  25.3 1.6 %collective-permute-start.3 = (f32[24,512]{1,0:T(8,128)S(1)}, f32[24,512]{1,0:T(8,128)S(1)}, u32[]{:S(2)}, u32[]{:S(2)}) collective-permute-start(f32[24,512]{1,0:T(8,128)S(1)} %get-tuple-element.14), channel_id=1, source_target_pairs={{0,2},{2,0},{4,6},{6,4},{8,10},{10,8},{12,14},{14,12},{1,3},{3,1},... | collective-permute-start | bytes 147464 | tf_op jit(solution)/shard_map/ppermute | solution.py:609
  26.8 0.1 add_convert_fusion.flag_ref
  26.9 2.5 %collective-permute-done.3.edge_ref = f32[24,512]{1,0:T(8,128)S(1)} collective-permute-done((f32[24,512]{1,0:T(8,128)S(1)}, f32[24,512]{1,0:T(8,128)S(1)}, u32[]{:S(2)}, u32[]{:S(2)}) %collective-permute-start.3) | collective-permute-done | bytes 49184 | tf_op jit(solution)/shard_map/ppermute | solution.py:609
  29.4 0.0 copy-done
  29.4 0.0 copy-done.4
  29.4 0.0 copy-done.5
  29.4 2.1 %blend.1 = bf16[6,32,512]{2,1,0:T(8,128)(2,1)} custom-call(s32[4]{0:T(128)S(1)} %add_convert_fusion.flag_ref, f32[7,32,512]{2,1,0:T(8,128)S(1)} %get-tuple-element.10.a0_ref, f32[7,24,256]{2,1,0:T(8,128)S(1)} %get-tuple-element.11.a1_ref, f32[7,16,128]{2,1,0:T(8,128)S(1)} %get-tuple-element.12.a2_ref, f32[7,8,128]{2,1,0:T(8,128)S(1)} %get-tuple-element.13.a3_ref, ...), custom_call_target="tpu_custom_call" | custom-call | tf_op jit(solution)/shard_map/blend/pallas_call | solution.py:619
Async XLA Ops:
  1.7 11.8 %collective-permute-start = (bf16[456,256]{1,0:T(8,128)(2,1)S(1)}, bf16[456,256]{1,0:T(8,128)(2,1)S(1)}, u32[]{:S(2)}, u32[]{:S(2)}) collective-permute-start(bf16[456,256]{1,0:T(8,128)(2,1)S(1)} %pack.1.refs_0_), channel_id=1, source_target_pairs={{0,12},{4,8},{8,4},{12,0},{1,13},{5,9},{9,5},{13,1},{2,14},{6,10},... | collective-permute-start | bytes 700424 | tf_op jit(solution)/shard_map/ppermute | solution.py:535
  6.8 11.7 %collective-permute-start.2 = (bf16[456,256]{1,0:T(8,128)(2,1)S(1)}, bf16[456,256]{1,0:T(8,128)(2,1)S(1)}, u32[]{:S(2)}, u32[]{:S(2)}) collective-permute-start(bf16[456,256]{1,0:T(8,128)(2,1)S(1)} %pack.1.refs_0_), channel_id=1, source_target_pairs={{0,4},{4,0},{8,12},{12,8},{1,5},{5,1},{9,13},{13,9},{2,6},{6,2},{1... | collective-permute-start | bytes 700424 | tf_op jit(solution)/shard_map/ppermute | solution.py:535
  13.4 9.2 %collective-permute-start.1 = (bf16[456,256]{1,0:T(8,128)(2,1)S(1)}, bf16[456,256]{1,0:T(8,128)(2,1)S(1)}, u32[]{:S(2)}, u32[]{:S(2)}) collective-permute-start(bf16[456,256]{1,0:T(8,128)(2,1)S(1)} %collective-permute-done.refs_0_), channel_id=1, source_target_pairs={{0,4},{4,0},{8,12},{12,8},{1,5},{5,1},{9,13},{13,9},{2,6},{6,2},{1... | collective-permute-start | bytes 700424 | tf_op jit(solution)/shard_map/ppermute | solution.py:535
  18.5 4.1 %copy-start.1 = (bf16[512,256]{1,0:T(8,128)(2,1)S(1)}, bf16[512,256]{1,0:T(8,128)(2,1)}, u32[]{:S(2)}) copy-start(bf16[512,256]{1,0:T(8,128)(2,1)} %constant.37.clone.refs_3_) | copy-start | bytes 786436
  18.5 4.1 %copy-start.2 = (bf16[2,512,128]{2,1,0:T(8,128)(2,1)S(1)}, bf16[2,512,128]{2,1,0:T(8,128)(2,1)}, u32[]{:S(2)}) copy-start(bf16[2,512,128]{2,1,0:T(8,128)(2,1)} %constant.39.clone.refs_5_) | copy-start | bytes 786436
  18.5 4.1 %copy-start.3 = (bf16[512,128]{1,0:T(8,128)(2,1)S(1)}, bf16[512,128]{1,0:T(8,128)(2,1)}, u32[]{:S(2)}) copy-start(bf16[512,128]{1,0:T(8,128)(2,1)} %constant.38.clone.refs_4_) | copy-start | bytes 393220
  19.2 10.3 %copy-start = (bf16[256,512]{1,0:T(8,128)(2,1)S(1)}, bf16[256,512]{1,0:T(8,128)(2,1)}, u32[]{:S(2)}) copy-start(bf16[256,512]{1,0:T(8,128)(2,1)} %constant.40.clone.grow1_ref) | copy-start | bytes 786436
  19.2 10.3 %copy-start.4 = (bf16[128,256]{1,0:T(8,128)(2,1)S(1)}, bf16[128,256]{1,0:T(8,128)(2,1)}, u32[]{:S(2)}) copy-start(bf16[128,256]{1,0:T(8,128)(2,1)} %constant.41.clone.grow2_ref) | copy-start | bytes 196612
  19.2 10.2 %copy-start.5 = (bf16[128,128]{1,0:T(8,128)(2,1)S(1)}, bf16[128,128]{1,0:T(8,128)(2,1)}, u32[]{:S(2)}) copy-start(bf16[128,128]{1,0:T(8,128)(2,1)} %constant.42.clone.grow3_ref) | copy-start | bytes 98308
  25.3 4.2 %collective-permute-start.3 = (f32[24,512]{1,0:T(8,128)S(1)}, f32[24,512]{1,0:T(8,128)S(1)}, u32[]{:S(2)}, u32[]{:S(2)}) collective-permute-start(f32[24,512]{1,0:T(8,128)S(1)} %get-tuple-element.14), channel_id=1, source_target_pairs={{0,2},{2,0},{4,6},{6,4},{8,10},{10,8},{12,14},{14,12},{1,3},{3,1},... | collective-permute-start | bytes 147464 | tf_op jit(solution)/shard_map/ppermute | solution.py:609

commit v3 on v2

--- a/solution.py
+++ b/solution.py
@@ -184,6 +184,7 @@
 F32 = jnp.float32
 EDGE = 3
 CODE_ROWS = 8
+DEAD = -1024
 
 
 def up8(v):
@@ -244,6 +245,10 @@
         self.low_at = self.main
         self.low_edge_at = self.main + self.size[3]
         self.total = self.main + self.size[3] + 8
+        self.weight_at = bands // 2 * BS * BS
+        self.code_at = self.weight_at + BS * BS // 2
+        order = np.arange(self.rows)
+        self.row_of = order % self.slot_rows * BS + order // self.slot_rows
 
     def column_tables(self):
         n, m, w = self.n, self.m, self.strip
@@ -287,17 +292,15 @@
     )
 
 
-def pack_kernel(plan, count_ref, scenes_ref, cloud_ref, dest_ref, offset_ref, out_ref, dest, offset, sems):
-    rows = plan.bands * S_DEV
+def pack_kernel(plan, count_ref, scenes_ref, cloud_ref, dest_ref, offset_ref, out_ref, raw, cloud, dest,
+                offset, sems):
+    rows = 2 * S_DEV
+    pairs = plan.bands // 2
     copies = [
         pltpu.make_async_copy(source, target, sems.at[k])
         for k, (source, target) in enumerate(
-            (
-                (dest_ref, dest),
-                (offset_ref, offset),
-                (cloud_ref, out_ref.at[pl.ds(rows, S_DEV)]),
-                (scenes_ref, out_ref.at[pl.ds(0, rows)]),
-            )
+            [(dest_ref, dest), (offset_ref, offset), (cloud_ref, cloud)]
+            + [(scenes_ref.at[pl.ds(q * rows, rows)], raw.at[pl.ds(q * rows, rows)]) for q in range(pairs)]
         )
     ]
     for copy in copies:
@@ -308,50 +311,95 @@
     slot = offset[...]
     code = (slot % per_row) * plan.slot_rows + dest[...] * per_row + slot // per_row
     live = lax.broadcasted_iota(jnp.int32, (1, S_DEV), 1) < count_ref[0, 0]
-    code = jnp.where(live, code, -1).astype(F32)
-    rows += S_DEV
-    tail = out_ref.shape[0] - rows
-    out_ref[rows:, :] = jnp.full((tail, BS * BS), -1.0, BF)
-    out_ref[rows:, :S_DEV] = jnp.broadcast_to(code, (tail, S_DEV)).astype(BF)
-    for copy in copies[2:]:
-        copy.wait()
-
-
-def landing_of(plan, packs):
-    tail = slice((plan.bands + 1) * S_DEV, (plan.bands + 1) * S_DEV + CODE_ROWS)
-    codes = packs[0][tail, :].astype(F32)
-    for p in range(1, len(packs)):
-        codes = jnp.maximum(codes, pltpu.roll(packs[p][tail, :].astype(F32), S_DEV * p, 1))
-    blocks = len(packs) * S_DEV
-    slot = lax.broadcasted_iota(jnp.int32, (plan.slots, blocks), 0).astype(F32)
-    landing = jnp.where(slot == codes[:1, :blocks], 1.0, 0.0).astype(BF)
-    return jnp.concatenate([landing, landing], axis=1)
-
-
-def slot_sums(plan, packs, landing2, prod_ref, f):
-    blocks = len(packs) * S_DEV
-    weights = pl.ds(plan.bands * S_DEV, S_DEV)
-    for p, pack in enumerate(packs):
-        weight = pack[weights, :]
-        if f == plan.bands:
-            prod_ref[pl.ds(p * S_DEV, S_DEV), :] = weight
-            continue
-        value = pack[f * S_DEV : (f + 1) * S_DEV, :].astype(F32) * weight.astype(F32)
+    code = jnp.where(live, code, DEAD).astype(F32)
+    code = jnp.broadcast_to(jnp.concatenate([code, code], axis=1), (CODE_ROWS, rows))
+    out_ref[plan.code_at :, :] = code.astype(BF)
+    copies[2].wait()
+    half = BS * BS // 2
+    weights = jnp.concatenate([cloud[:, :half], cloud[:, half:]], axis=0)
+    out_ref[plan.weight_at : plan.code_at, :] = weights.T
+    for q in range(pairs):
+        copies[3 + q].wait()
+        out_ref[q * BS * BS : (q + 1) * BS * BS, :] = raw[q * rows : (q + 1) * rows, :].T
+
+
+def landing_of(plan, pack):
+    codes = pack[plan.code_at : plan.code_at + CODE_ROWS, :].astype(F32).T[:, :1]
+    blocks = codes.shape[0]
+    second = lax.broadcasted_iota(jnp.int32, (blocks, 1), 0) >= S_DEV
+    codes = codes + jnp.where(second, float(plan.slots), 0.0)
+    slot = lax.broadcasted_iota(jnp.int32, (blocks, 2 * plan.slots), 1).astype(F32)
+    landing = jnp.where(slot == codes, 1.0, 0.0).astype(BF)
+    return jnp.concatenate([landing, landing], axis=0)
+
+
+def slot_sums(plan, pack):
+    landing2 = landing_of(plan, pack)
+    area = BS * BS
+    blocks = 2 * S_DEV
+    both = pack[plan.weight_at : plan.code_at, :].astype(F32)
+    first = lax.broadcasted_iota(jnp.int32, both.shape, 1) < S_DEV
+    turned = pltpu.roll(both, S_DEV, 1)
+    weights = jnp.concatenate(
+        [jnp.where(first, both, turned), jnp.where(first, turned, both)], axis=0
+    )
+    result = []
+    for q in range(plan.bands // 2):
+        value = pack[q * area : (q + 1) * area, :].astype(F32) * weights
         high, low = halves(value)
-        prod_ref[pl.ds(p * S_DEV, S_DEV), :] = high
-        prod_ref[pl.ds(blocks + p * S_DEV, S_DEV), :] = low
-    used = blocks if f == plan.bands else 2 * blocks
-    return jnp.dot(landing2[:, :used], prod_ref[:used, :], preferred_element_type=F32)
+        pair = jnp.dot(
+            jnp.concatenate([high, low], axis=1), landing2, preferred_element_type=F32
+        )
+        result += [pair[:, : plan.slots], pair[:, plan.slots :]]
+    result.append(
+        jnp.dot(weights.astype(BF), landing2[:blocks, : plan.slots], preferred_element_type=F32)
+    )
+    return result
 
 
 def sum_kernel(plan, count, *refs):
     packs, rest = refs[:count], refs[count:]
-    before_ref = rest[0] if len(rest) == 3 else None
-    out_ref, prod_ref = rest[-2:]
-    landing2 = landing_of(plan, packs)
-    for f in range(plan.bands + 1):
-        sums = slot_sums(plan, packs, landing2, prod_ref, f)
-        out_ref[f] = sums if before_ref is None else before_ref[f] + sums
+    before_ref = rest[0] if len(rest) == 2 else None
+    out_ref = rest[-1]
+    for p, pack in enumerate(packs):
+        for f, sums in enumerate(slot_sums(plan, pack)):
+            if p:
+                out_ref[f] += sums
+            else:
+                out_ref[f] = sums if before_ref is None else before_ref[f] + sums
+
+
+def tile_of(plan, sums, tile_ref, tall):
+    wide = plan.slot_rows
+    ways = TS // wide
+    group = lax.broadcasted_iota(jnp.int32, (BS, TS), 1) // wide
+    for chunk in range(plan.slots // TS):
+        for r0 in range(0, BS, ways):
+            part = [
+                sums[(r0 + k) * BS : (r0 + k + 1) * BS, chunk * TS : (chunk + 1) * TS]
+                for k in range(ways)
+            ]
+            step = ways // 2
+            while step:
+                odd = (group & step) != 0
+                for i in range(ways):
+                    if i & step:
+                        continue
+                    a, b = part[i], part[i + step]
+                    if 2 * step * wide == TS:
+                        moved = pltpu.roll(jnp.where(odd, a, b), TS // 2, 1)
+                        part[i] = jnp.where(odd, moved, a)
+                        part[i + step] = jnp.where(odd, b, moved)
+                    else:
+                        part[i] = jnp.where(odd, pltpu.roll(b, step * wide, 1), a)
+                        part[i + step] = jnp.where(odd, b, pltpu.roll(a, TS - step * wide, 1))
+                step //= 2
+            at = r0 * wide
+            for k in range(ways):
+                high, low = halves(part[k])
+                row = (chunk * ways + k) * BS
+                tile_ref[row : row + BS, at : at + TS] = high
+                tile_ref[tall + row : tall + row + BS, at : at + TS] = low
 
 
 def place_kernel(plan, count, *refs):
@@ -359,39 +407,17 @@
     packs = refs[:count]
     before_ref, column_ref, row1_ref, row2_ref, row3_ref = refs[count : count + 5]
     a0_ref, a1_ref, a2_ref, a3_ref, edge_ref = refs[count + 5 : count + 10]
-    prod_ref, sums_ref, tile_ref, z1_ref, z2_ref, z3_ref = refs[count + 10 :]
-    area = BS * BS
-    landing2 = landing_of(plan, packs)
-    group = lax.broadcasted_iota(jnp.int32, (plan.slot_rows, TS), 1) // BS
-    per_row = TS // BS
+    tile_ref, z1_ref, z2_ref, z3_ref = refs[count + 10 :]
     column = column_ref[...]
+    added = [slot_sums(plan, pack) for pack in packs]
+    at, size, edge = plan.at, plan.size, plan.edge_at
     for f in range(bands + 1):
-        sums_ref[f] = before_ref[f] + slot_sums(plan, packs, landing2, prod_ref, f)
-    for f in range(bands + 1):
-        sums = sums_ref[f]
-        for half in range(area // TS):
-            part = [
-                sums[b * plan.slot_rows : (b + 1) * plan.slot_rows, half * TS : (half + 1) * TS]
-                for b in range(per_row)
-            ]
-            step = per_row // 2
-            while step:
-                odd = (group & step) != 0
-                for i in range(per_row):
-                    if i & step:
-                        continue
-                    a, b = part[i], part[i + step]
-                    part[i] = jnp.where(odd, pltpu.roll(b, step * BS, 1), a)
-                    part[i + step] = jnp.where(odd, b, pltpu.roll(a, TS - step * BS, 1))
-                step //= 2
-            for r in range(per_row):
-                tile_ref[pl.ds(half * per_row + r, plan.slot_rows, stride=BS), :] = part[r]
-        high, low = halves(tile_ref[...])
-        tile = jnp.concatenate([high, low], axis=1)
-        cols = lax.dot_general(
-            column, tile, (((1,), (1,)), ((), ())), preferred_element_type=F32
-        )
-        at, size, edge = plan.at, plan.size, plan.edge_at
+        sums = before_ref[f]
+        for one in added:
+            sums = sums + one[f]
+        tile = tile_ref.at[f % 2]
+        tile_of(plan, sums, tile, TS)
+        cols = jnp.dot(column, tile[...], preferred_element_type=F32)
         a0_ref[f] = cols[at[0] : at[1]]
         z1_ref[f, : size[1]] = cols[at[1] : at[2]]
         z1_ref[f, size[1] :] = cols[edge[1] : edge[1] + 8]
@@ -412,7 +438,7 @@
         z3.astype(BF), row3_ref[1], preferred_element_type=F32
     )
     start = 0
-    edge_ref[...] = jnp.zeros(edge_ref.shape, F32)
+    edge_ref[...] = jnp.zeros(edge_ref.shape, edge_ref.dtype)
     for z, out_ref, level in ((z1, a1_ref, 1), (z2, a2_ref, 2), (z3, a3_ref, 3)):
         lanes = z.shape[-1]
         z = z.reshape(planes, size[level] + 8, lanes)
@@ -420,7 +446,7 @@
         for f in range(planes):
             edge_ref[pl.ds(EDGE * f, EDGE), start : start + lanes] = z[
                 f, size[level] : size[level] + EDGE
-            ]
+            ].astype(edge_ref.dtype)
         start += lanes
 
 
@@ -443,7 +469,7 @@
 
 
 def blend_kernel(plan, flag_ref, a0_ref, a1_ref, a2_ref, a3_ref, edge_ref, grow1_ref, grow2_ref, grow3_ref,
-                 out_ref, g1_ref, g2_ref, g3_ref, e2_ref, e1_ref, e0_ref):
+                 natural_ref, out_ref, g1_ref, g2_ref, g3_ref, e2_ref, e1_ref, e0_ref, strip_ref, sems):
     bands = plan.bands
     planes = bands + 1
     w = plan.strip
@@ -453,7 +479,7 @@
         lanes = src.shape[-1]
         dst[...] = src[...]
         for f in range(planes):
-            edge = edge_ref[pl.ds(EDGE * f, EDGE), start : start + lanes]
+            edge = edge_ref[pl.ds(EDGE * f, EDGE), start : start + lanes].astype(F32)
             far = w >> level
             dst[f, :EDGE] += jnp.where(left > 0, edge, 0.0)
             dst[f, far : far + EDGE] += jnp.where(right > 0, edge, 0.0)
@@ -493,9 +519,15 @@
     even, odd = (a + 6.0 * b + c) * 0.125, (b + c) * 0.5
     up = weave(even, odd, e0_ref, w)
     inverse = 1.0 / (BACKGROUND + a0_ref[bands])
+    copies = []
     for f in range(bands):
         value = (a0_ref[f] - up[f]) * inverse + up[bands + f]
-        out_ref[f] = value.astype(BF)
+        value = jnp.dot(value.astype(BF), natural_ref[...], preferred_element_type=F32)
+        strip_ref[f] = value.astype(BF)
+        copies.append(pltpu.make_async_copy(strip_ref.at[f], out_ref.at[f], sems.at[f]))
+        copies[-1].start()
+    for copy in copies:
+        copy.wait()
 
 
 def on_chip(value):
@@ -519,13 +551,15 @@
     blocks = jnp.swapaxes(scenes[0], 0, 1).reshape(bands * S_DEV, area)
     pack = pl.pallas_call(
         functools.partial(pack_kernel, plan),
-        out_shape=pltpu.VMEM((planes * S_DEV + CODE_ROWS, area), BF),
+        out_shape=pltpu.VMEM((plan.code_at + CODE_ROWS, 2 * S_DEV), BF),
         in_specs=[smem] + [hbm] * 4,
         out_specs=vmem,
         scratch_shapes=[
+            pltpu.VMEM(blocks.shape, BF),
+            pltpu.VMEM(cloud[0].shape, BF),
             pltpu.VMEM(destination.shape, jnp.int32),
             pltpu.VMEM(offset.shape, jnp.int32),
-            pltpu.SemaphoreType.DMA((4,)),
+            pltpu.SemaphoreType.DMA((3 + bands // 2,)),
         ],
         compiler_params=pltpu.CompilerParams(vmem_limit_bytes=4 << 20),
         name="pack",
@@ -539,10 +573,9 @@
         operands = [on_chip(v) for v in packs + before]
         return pl.pallas_call(
             functools.partial(sum_kernel, plan, count),
-            out_shape=pltpu.VMEM((planes, plan.slots, area), F32),
+            out_shape=pltpu.VMEM((planes, area, plan.slots), F32),
             in_specs=[vmem] * len(operands),
             out_specs=vmem,
-            scratch_shapes=[pltpu.VMEM((2 * count * S_DEV, area), BF)],
             input_output_aliases={count: 0} if before else {},
             compiler_params=pltpu.CompilerParams(vmem_limit_bytes=4 << 20),
             cost_estimate=pl.CostEstimate(
@@ -568,12 +601,12 @@
         jnp.asarray(plan.column_tables()), row_tile * m + col_tile, keepdims=False
     )
     shrinks = row_shrinks(plan.rows)
-    row1 = jnp.asarray(shrinks[0].T.astype(BF))
-    row2 = jnp.asarray(shrinks[1].T.astype(BF))
+    row1 = jnp.asarray(shrinks[0].T[plan.row_of].astype(BF))
+    row2 = jnp.asarray(shrinks[1].T[plan.row_of].astype(BF))
     top = plan.rows >> 3
     wide_top = max(top, 128)
     padded = np.zeros((plan.rows, wide_top))
-    padded[:, :top] = shrinks[2].T
+    padded[:, :top] = shrinks[2].T[plan.row_of]
     row3 = jnp.asarray(np.stack(split_table(padded)))
     size = plan.size
     shapes = [
@@ -586,14 +619,12 @@
     edge_shape = (up8(EDGE * planes), edge_lanes)
     a0, a1, a2, a3, edge = pl.pallas_call(
         functools.partial(place_kernel, plan, len(late)),
-        out_shape=[pltpu.VMEM(s, F32) for s in shapes + [edge_shape]],
+        out_shape=[pltpu.VMEM(s, F32) for s in shapes] + [pltpu.VMEM(edge_shape, BF)],
         in_specs=[vmem] * (len(late) + 5),
         compiler_params=pltpu.CompilerParams(vmem_limit_bytes=16 << 20),
         out_specs=[vmem] * 5,
         scratch_shapes=[
-            pltpu.VMEM((2 * len(late) * S_DEV, area), BF),
-            pltpu.VMEM((planes, plan.slots, area), F32),
-            pltpu.VMEM((plan.rows, TS), F32),
+            pltpu.VMEM((2, 2 * TS, plan.rows), BF),
             pltpu.VMEM((planes, size[1] + 8, plan.rows), F32),
             pltpu.VMEM((planes, size[2] + 8, plan.rows), F32),
             pltpu.VMEM((planes, size[3] + 8, plan.rows), F32),
@@ -615,12 +646,13 @@
     grow3 = np.zeros((wide_top, plan.rows >> 2))
     grow3[:top] = grow_grid(top).T
     grow2 = grow_grid(plan.rows >> 2).T
-    grow1 = grow_grid(plan.rows >> 1).T
+    grow1 = grow_grid(plan.rows >> 1).T[:, plan.row_of]
+    natural = np.eye(plan.rows)[plan.row_of]
     out = pl.pallas_call(
         functools.partial(blend_kernel, plan),
         out_shape=jax.ShapeDtypeStruct((bands, size[0], plan.rows), BF),
-        in_specs=[smem] + [vmem] * 8,
-        out_specs=vmem,
+        in_specs=[smem] + [vmem] * 9,
+        out_specs=hbm,
         scratch_shapes=[
             pltpu.VMEM(shapes[1], F32),
             pltpu.VMEM(shapes[2], F32),
@@ -628,12 +660,15 @@
             pltpu.VMEM((2 * bands, (plan.rows >> 2) // TS, size[2], TS), F32),
             pltpu.VMEM((2 * bands, (plan.rows >> 1) // TS, size[1], TS), F32),
             pltpu.VMEM((2 * bands, plan.rows // TS, size[0], TS), F32),
+            pltpu.VMEM((bands, size[0], plan.rows), BF),
+            pltpu.SemaphoreType.DMA((bands,)),
         ],
         compiler_params=pltpu.CompilerParams(vmem_limit_bytes=16 << 20),
         name="blend",
     )(
         flags, *[on_chip(v) for v in (a0, a1, a2, a3, edge)],
         jnp.asarray(grow1.astype(BF)), jnp.asarray(grow2.astype(BF)), jnp.asarray(grow3.astype(BF)),
+        jnp.asarray(natural.astype(BF)),
     )
     return out[:, None]
 

time: 31.7 us -> 31.3 us (0.987)
  waiting for transfers between devices: 12.6 us -> 11.8 us
    pallas_call x1, Pallas kernels: 2.63 us -> 1.88 us  [strip_local(): pl.pallas_call(functools.partial(place_kernel, plan, len(late)), out_shap...]
    ppermute x3, waiting for transfers between devices: 10 us -> 9.55 us  [swap(): return lax.ppermute(value, 'tx', [(i, i ^ mask) for i in range(n)])]
    pallas_call x1, Pallas kernels: 2.14 us -> 2.63 us  [strip_local(): pl.pallas_call(functools.partial(blend_kernel, plan), out_shape=jax.Shape...]
    pallas_call x2, Pallas kernels: 1.04 us -> 1.44 us  [sum_blocks(): pl.pallas_call(functools.partial(sum_kernel, plan, count), out_shape=pltp...]
  transfers between devices with their start and end apart: 4 -> 4, of which waited for: 3 -> 3; matrix products, arithmetic and copies ran while one was open for 3% -> 3% of each run, Pallas kernels for 3% -> 5%
where the time goes in v3:
time: 31.3 us; the launch traced here: 31.1 us
  waiting for transfers between devices  11.8 us (38%)
  starting transfers between devices  10.5 us (34%)
  Pallas kernels  7.11 us (23%)
  local copies, waits for them, and re-layouts  0.88 us (3%)
  between operations  0.75 us (2%)
    ppermute x3, waiting for transfers between devices, swap(): return lax.ppermute(value, 'tx', [(i, i ^ mask) for i in range(n)])  9.55 us
    ppermute x3, starting transfers between devices, swap(): return lax.ppermute(value, 'tx', [(i, i ^ mask) for i in range(n)])  8.89 us
    pallas_call x1, Pallas kernels, strip_local(): pl.pallas_call(functools.partial(blend_kernel, plan), out_shape=jax.Shape...  2.63 us
    ppermute x1, waiting for transfers between devices, strip_local(): edge = lax.ppermute(edge, ('tx', 'ty'), pairs)  2.25 us
    pallas_call x1, Pallas kernels, strip_local(): pl.pallas_call(functools.partial(place_kernel, plan, len(late)), out_shap...  1.88 us
    ppermute x1, starting transfers between devices, strip_local(): edge = lax.ppermute(edge, ('tx', 'ty'), pairs)  1.56 us
    pallas_call x2, Pallas kernels, sum_blocks(): pl.pallas_call(functools.partial(sum_kernel, plan, count), out_shape=pltp...  1.44 us
    pallas_call x1, Pallas kernels, strip_local(): pl.pallas_call(functools.partial(pack_kernel, plan), out_shape=pltpu.VMEM...  1.16 us
  transfers between devices with their start and end apart: 4, of which 3 were waited for; matrix products, arithmetic and copies ran while one was open for 3% of the time, Pallas kernels for 5%

profile of v3, /device:TPU:0, one launch (start us, length us, event | category | flops | bytes accessed | tf_op | source)
XLA Modules:
  0.0 31.1 jit_solution(13036401323924491346)
XLA Ops:
  0.7 1.2 %pack.1.refs_0_ = bf16[904,128]{1,0:T(8,128)(2,1)S(1)} custom-call(s32[1,1]{1,0:T(1,128)S(6)} %copy.17.count_ref, bf16[384,256]{1,0:T(8,128)(2,1)} %bitcast.15, bf16[64,256]{1,0:T(8,128)(2,1)} %bitcast.16, s32[1,64]{1,0:T(1,128)} %dest_ref.1, s32[1,64]{1,0:T(1,128)} %offset_ref.1), custom_call_target="tpu_custom_call" | custom-call | tf_op jit(solution)/shard_map/pack/pallas_call | solution.py:552
  1.8 5.1 %collective-permute-start = (bf16[904,128]{1,0:T(8,128)(2,1)S(1)}, bf16[904,128]{1,0:T(8,128)(2,1)S(1)}, u32[]{:S(2)}, u32[]{:S(2)}) collective-permute-start(bf16[904,128]{1,0:T(8,128)(2,1)S(1)} %pack.1.refs_0_), channel_id=1, source_target_pairs={{0,12},{4,8},{8,4},{12,0},{1,13},{5,9},{9,5},{13,1},{2,14},{6,10},... | collective-permute-start | bytes 694280 | tf_op jit(solution)/shard_map/ppermute | solution.py:569
  7.0 0.0 collective-permute-start.2
  7.0 6.6 %collective-permute-done.refs_0_ = bf16[904,128]{1,0:T(8,128)(2,1)S(1)} collective-permute-done((bf16[904,128]{1,0:T(8,128)(2,1)S(1)}, bf16[904,128]{1,0:T(8,128)(2,1)S(1)}, u32[]{:S(2)}, u32[]{:S(2)}) %collective-permute-start) | collective-permute-done | bytes 231456 | tf_op jit(solution)/shard_map/ppermute | solution.py:569
  13.5 3.7 %collective-permute-start.1 = (bf16[904,128]{1,0:T(8,128)(2,1)S(1)}, bf16[904,128]{1,0:T(8,128)(2,1)S(1)}, u32[]{:S(2)}, u32[]{:S(2)}) collective-permute-start(bf16[904,128]{1,0:T(8,128)(2,1)S(1)} %collective-permute-done.refs_0_), channel_id=1, source_target_pairs={{0,4},{4,0},{8,12},{12,8},{1,5},{5,1},{9,13},{13,9},{2,6},{6,2},{1... | collective-permute-start | bytes 694280 | tf_op jit(solution)/shard_map/ppermute | solution.py:569
  17.3 0.6 %shard_map.127.refs_2_ = f32[7,256,256]{2,1,0:T(8,128)S(1)} custom-call(bf16[904,128]{1,0:T(8,128)(2,1)S(1)} %pack.1.refs_0_), custom_call_target="tpu_custom_call" | custom-call | flops 117440512 | bytes 1835008 | tf_op jit(solution)/shard_map/pallas_call | solution.py:574
  17.9 0.8 %dynamic-slice_bitcast_fusion.refs_2_ = bf16[120,256]{1,0:T(8,128)(2,1)S(1)} fusion(bf16[8,120,256]{2,1,0:T(8,128)(2,1)} %constant.38.clone, s32[]{:T(128)S(6)} %select_n.4), kind=kLoop, calls=%fused_computation | loop fusion | bytes 122884 | tf_op jit(solution)/shard_map/jit(dynamic_index_in_dim)/squeeze | solution.py:600
  18.7 0.0 copy-start.1
  18.7 0.0 copy-start.2
  18.7 0.0 copy-start.4
  18.7 0.0 collective-permute-done.2.refs_1_
  18.7 0.9 %shard_map.128.refs_1_ = f32[7,256,256]{2,1,0:T(8,128)S(1)} custom-call(bf16[904,128]{1,0:T(8,128)(2,1)S(1)} %collective-permute-done.refs_0_, bf16[904,128]{1,0:T(8,128)(2,1)S(1)} %collective-permute-done.2.refs_1_, f32[7,256,256]{2,1,0:T(8,128)S(1)} %shard_map.127.refs_2_), custom_call_target="tpu_custom_call", output_to_operand_aliasing={{}: (2, {})} | custom-call | flops 234881024 | bytes 1835008 | tf_op jit(solution)/shard_map/pallas_call | solution.py:574
  19.6 0.0 copy-start
  19.6 0.0 copy-start.3
  19.6 0.0 copy-start.5
  19.6 0.0 copy-start.6
  19.7 3.0 %collective-permute-done.1.refs_0_ = bf16[904,128]{1,0:T(8,128)(2,1)S(1)} collective-permute-done((bf16[904,128]{1,0:T(8,128)(2,1)S(1)}, bf16[904,128]{1,0:T(8,128)(2,1)S(1)}, u32[]{:S(2)}, u32[]{:S(2)}) %collective-permute-start.1) | collective-permute-done | bytes 231456 | tf_op jit(solution)/shard_map/ppermute | solution.py:569
  22.6 0.0 copy-done.1
  22.6 0.0 copy-done.2
  22.6 0.0 copy-done.4
  22.6 1.9 %place.1 = (f32[7,32,512]{2,1,0:T(8,128)S(1)}, f32[7,24,256]{2,1,0:T(8,128)S(1)}, f32[7,16,128]{2,1,0:T(8,128)S(1)}, f32[7,8,128]{2,1,0:T(8,128)S(1)}, bf16[24,512]{1,0:T(8,128)(2,1)S(1)}) custom-call(bf16[904,128]{1,0:T(8,128)(2,1)S(1)} %collective-permute-done.1.refs_0_, f32[7,256,256]{2,1,0:T(8,128)S(1)} %shard_map.128.refs_1_, ...), custom_call_target="tpu_custom_call" | custom-call | tf_op jit(solution)/shard_map/place/pallas_call | solution.py:620
  24.5 1.6 %collective-permute-start.3 = (bf16[24,512]{1,0:T(8,128)(2,1)S(1)}, bf16[24,512]{1,0:T(8,128)(2,1)S(1)}, u32[]{:S(2)}, u32[]{:S(2)}) collective-permute-start(bf16[24,512]{1,0:T(8,128)(2,1)S(1)} %get-tuple-element.14), channel_id=1, source_target_pairs={{0,2},{2,0},{4,6},{6,4},{8,10},{10,8},{12,14},{14,12},{1,3},{3,1},... | collective-permute-start | bytes 73736 | tf_op jit(solution)/shard_map/ppermute | solution.py:640
  26.1 0.1 add_convert_fusion.flag_ref
  26.2 2.2 %collective-permute-done.3.edge_ref = bf16[24,512]{1,0:T(8,128)(2,1)S(1)} collective-permute-done((bf16[24,512]{1,0:T(8,128)(2,1)S(1)}, bf16[24,512]{1,0:T(8,128)(2,1)S(1)}, u32[]{:S(2)}, u32[]{:S(2)}) %collective-permute-start.3) | collective-permute-done | bytes 24608 | tf_op jit(solution)/shard_map/ppermute | solution.py:640
  28.4 0.0 copy-done
  28.4 0.0 copy-done.3
  28.4 0.0 copy-done.5
  28.4 0.0 copy-done.6
  28.4 2.6 %blend.1 = bf16[6,32,512]{2,1,0:T(8,128)(2,1)} custom-call(s32[4]{0:T(128)S(1)} %add_convert_fusion.flag_ref, f32[7,32,512]{2,1,0:T(8,128)S(1)} %get-tuple-element.10.a0_ref, f32[7,24,256]{2,1,0:T(8,128)S(1)} %get-tuple-element.11.a1_ref, f32[7,16,128]{2,1,0:T(8,128)S(1)} %get-tuple-element.12.a2_ref, f32[7,8,128]{2,1,0:T(8,128)S(1)} %get-tuple-element.13.a3_ref, ...), custom_call_target="tpu_custom_call" | custom-call | tf_op jit(solution)/shard_map/blend/pallas_call | solution.py:651
Async XLA Ops:
  1.8 11.7 %collective-permute-start = (bf16[904,128]{1,0:T(8,128)(2,1)S(1)}, bf16[904,128]{1,0:T(8,128)(2,1)S(1)}, u32[]{:S(2)}, u32[]{:S(2)}) collective-permute-start(bf16[904,128]{1,0:T(8,128)(2,1)S(1)} %pack.1.refs_0_), channel_id=1, source_target_pairs={{0,12},{4,8},{8,4},{12,0},{1,13},{5,9},{9,5},{13,1},{2,14},{6,10},... | collective-permute-start | bytes 694280 | tf_op jit(solution)/shard_map/ppermute | solution.py:569
  7.0 11.8 %collective-permute-start.2 = (bf16[904,128]{1,0:T(8,128)(2,1)S(1)}, bf16[904,128]{1,0:T(8,128)(2,1)S(1)}, u32[]{:S(2)}, u32[]{:S(2)}) collective-permute-start(bf16[904,128]{1,0:T(8,128)(2,1)S(1)} %pack.1.refs_0_), channel_id=1, source_target_pairs={{0,4},{4,0},{8,12},{12,8},{1,5},{5,1},{9,13},{13,9},{2,6},{6,2},{1... | collective-permute-start | bytes 694280 | tf_op jit(solution)/shard_map/ppermute | solution.py:569
  13.5 9.1 %collective-permute-start.1 = (bf16[904,128]{1,0:T(8,128)(2,1)S(1)}, bf16[904,128]{1,0:T(8,128)(2,1)S(1)}, u32[]{:S(2)}, u32[]{:S(2)}) collective-permute-start(bf16[904,128]{1,0:T(8,128)(2,1)S(1)} %collective-permute-done.refs_0_), channel_id=1, source_target_pairs={{0,4},{4,0},{8,12},{12,8},{1,5},{5,1},{9,13},{13,9},{2,6},{6,2},{1... | collective-permute-start | bytes 694280 | tf_op jit(solution)/shard_map/ppermute | solution.py:569
  18.7 3.9 %copy-start.1 = (bf16[512,256]{1,0:T(8,128)(2,1)S(1)}, bf16[512,256]{1,0:T(8,128)(2,1)}, u32[]{:S(2)}) copy-start(bf16[512,256]{1,0:T(8,128)(2,1)} %constant.39.clone.refs_3_) | copy-start | bytes 786436
  18.7 3.9 %copy-start.2 = (bf16[2,512,128]{2,1,0:T(8,128)(2,1)S(1)}, bf16[2,512,128]{2,1,0:T(8,128)(2,1)}, u32[]{:S(2)}) copy-start(bf16[2,512,128]{2,1,0:T(8,128)(2,1)} %constant.41.clone.refs_5_) | copy-start | bytes 786436
  18.7 3.9 %copy-start.4 = (bf16[512,128]{1,0:T(8,128)(2,1)S(1)}, bf16[512,128]{1,0:T(8,128)(2,1)}, u32[]{:S(2)}) copy-start(bf16[512,128]{1,0:T(8,128)(2,1)} %constant.40.clone.refs_4_) | copy-start | bytes 393220
  19.6 8.8 %copy-start = (bf16[512,512]{1,0:T(8,128)(2,1)S(1)}, bf16[512,512]{1,0:T(8,128)(2,1)}, u32[]{:S(2)}) copy-start(bf16[512,512]{1,0:T(8,128)(2,1)} %constant.45.clone.natural_ref) | copy-start | bytes 1572868
  19.6 8.8 %copy-start.3 = (bf16[256,512]{1,0:T(8,128)(2,1)S(1)}, bf16[256,512]{1,0:T(8,128)(2,1)}, u32[]{:S(2)}) copy-start(bf16[256,512]{1,0:T(8,128)(2,1)} %constant.42.clone.grow1_ref) | copy-start | bytes 786436
  19.6 8.8 %copy-start.5 = (bf16[128,256]{1,0:T(8,128)(2,1)S(1)}, bf16[128,256]{1,0:T(8,128)(2,1)}, u32[]{:S(2)}) copy-start(bf16[128,256]{1,0:T(8,128)(2,1)} %constant.43.clone.grow2_ref) | copy-start | bytes 196612
  19.6 8.8 %copy-start.6 = (bf16[128,128]{1,0:T(8,128)(2,1)S(1)}, bf16[128,128]{1,0:T(8,128)(2,1)}, u32[]{:S(2)}) copy-start(bf16[128,128]{1,0:T(8,128)(2,1)} %constant.44.clone.grow3_ref) | copy-start | bytes 98308
  24.5 3.9 %collective-permute-start.3 = (bf16[24,512]{1,0:T(8,128)(2,1)S(1)}, bf16[24,512]{1,0:T(8,128)(2,1)S(1)}, u32[]{:S(2)}, u32[]{:S(2)}) collective-permute-start(bf16[24,512]{1,0:T(8,128)(2,1)S(1)} %get-tuple-element.14), channel_id=1, source_target_pairs={{0,2},{2,0},{4,6},{6,4},{8,10},{10,8},{12,14},{14,12},{1,3},{3,1},... | collective-permute-start | bytes 73736 | tf_op jit(solution)/shard_map/ppermute | solution.py:640

commit v4 on v3

--- a/solution.py
+++ b/solution.py
@@ -240,11 +240,11 @@
         self.at = [0]
         for size in self.size:
             self.at.append(self.at[-1] + size)
-        self.edge_at = [None] + [self.at[LEVELS] + 8 * k for k in range(LEVELS - 1)]
-        self.main = self.at[LEVELS] + 8 * (LEVELS - 1)
-        self.low_at = self.main
-        self.low_edge_at = self.main + self.size[3]
-        self.total = self.main + self.size[3] + 8
+        self.low_at = self.at[LEVELS]
+        self.main = self.low_at + self.size[3]
+        self.edge_at = [None] + [self.main + 8 * k for k in range(LEVELS - 1)]
+        self.total = self.main + 8 * (LEVELS - 1)
+        self.near = TS // self.slot_rows * BS
         self.weight_at = bands // 2 * BS * BS
         self.code_at = self.weight_at + BS * BS // 2
         order = np.arange(self.rows)
@@ -272,11 +272,11 @@
                     for k in range(EDGE):
                         o = base + k
                         if 0 <= o < width >> level:
-                            tables[t, j, self.edge_at[level] + k] = grids[level][o, j * TS : (j + 1) * TS]
+                            row = grids[level][o, j * TS : (j + 1) * TS]
+                            row = row[TS - self.near :] if 2 * t < n else row[: self.near]
+                            tables[t, j, self.edge_at[level] + k, : self.near] = row
         high, low = split_table(tables)
-        high[:, :, self.low_at : self.low_at + self.size[3]] = low[:, :, self.at[3] : self.at[4]]
-        edge = self.edge_at[3]
-        high[:, :, self.low_edge_at : self.low_edge_at + 8] = low[:, :, edge : edge + 8]
+        high[:, :, self.low_at : self.main] = low[:, :, self.at[3] : self.at[4]]
         return np.concatenate([high, high], axis=-1).reshape(n * m, self.total, 2 * TS)
 
 
@@ -357,97 +357,107 @@
     return result
 
 
-def sum_kernel(plan, count, *refs):
-    packs, rest = refs[:count], refs[count:]
-    before_ref = rest[0] if len(rest) == 2 else None
-    out_ref = rest[-1]
-    for p, pack in enumerate(packs):
-        for f, sums in enumerate(slot_sums(plan, pack)):
-            if p:
-                out_ref[f] += sums
-            else:
-                out_ref[f] = sums if before_ref is None else before_ref[f] + sums
-
-
-def tile_of(plan, sums, tile_ref, tall):
+def sum_kernel(plan, pack, out_ref):
+    for f, sums in enumerate(slot_sums(plan, pack)):
+        out_ref[f] = sums
+
+
+def turn(plan, part):
     wide = plan.slot_rows
     ways = TS // wide
     group = lax.broadcasted_iota(jnp.int32, (BS, TS), 1) // wide
+    step = ways // 2
+    while step:
+        odd = (group & step) != 0
+        for i in range(ways):
+            if i & step:
+                continue
+            a, b = part[i], part[i + step]
+            if 2 * step * wide == TS:
+                moved = pltpu.roll(jnp.where(odd, a, b), TS // 2, 1)
+                part[i] = jnp.where(odd, moved, a)
+                part[i + step] = jnp.where(odd, b, moved)
+            else:
+                part[i] = jnp.where(odd, pltpu.roll(b, step * wide, 1), a)
+                part[i + step] = jnp.where(odd, b, pltpu.roll(a, TS - step * wide, 1))
+        step //= 2
+    return part
+
+
+def first_kernel(plan, far, near, before_ref, column_ref, row1_ref, row2_ref, row3_ref,
+                 out_ref, near_ref, far_ref, tile_ref, z_ref):
+    planes = plan.bands + 1
+    right = 2 * lax.axis_index("tx") < plan.n
+    edge_table = column_ref[plan.main :, : plan.near]
+    ways = TS // plan.slot_rows
+    rows = plan.rows
+    far_sums, near_sums = slot_sums(plan, far), slot_sums(plan, near)
+    for f in range(planes):
+        sums = before_ref[f] + far_sums[f] + near_sums[f]
+        out_ref[f] = sums
+        for which, one in enumerate((sums, far_sums[f])):
+            side = jnp.where(right, one[:, plan.slots - TS :], one[:, :TS])
+            tile = tile_ref.at[2 * (f % 2) + which]
+            for r0 in range(0, BS, ways):
+                part = [side[(r0 + k) * BS : (r0 + k + 1) * BS] for k in range(ways)]
+                for k, value in enumerate(turn(plan, part)):
+                    at = r0 * plan.slot_rows
+                    tile[k * BS : (k + 1) * BS, at : at + TS] = value.astype(BF)
+            cols = jnp.dot(edge_table, tile[...], preferred_element_type=F32)
+            for level in range(1, LEVELS):
+                z_ref[level - 1, which * planes + f] = cols[8 * level - 8 : 8 * level]
+    start = 0
+    for ref in (near_ref, far_ref):
+        ref[...] = jnp.zeros(ref.shape, ref.dtype)
+    for level, table in ((1, row1_ref[...]), (2, row2_ref[...]), (3, row3_ref[0])):
+        lanes = table.shape[1]
+        z = z_ref[level - 1].reshape(2 * planes * 8, rows).astype(BF)
+        z = jnp.dot(z, table, preferred_element_type=F32).reshape(2 * planes, 8, lanes)
+        for which, ref in enumerate((near_ref, far_ref)):
+            for f in range(planes):
+                ref[pl.ds(EDGE * f, EDGE), start : start + lanes] = z[which * planes + f, :EDGE].astype(BF)
+        start += lanes
+
+
+def tile_of(plan, sums, tile_ref, tall):
+    ways = TS // plan.slot_rows
     for chunk in range(plan.slots // TS):
         for r0 in range(0, BS, ways):
             part = [
                 sums[(r0 + k) * BS : (r0 + k + 1) * BS, chunk * TS : (chunk + 1) * TS]
                 for k in range(ways)
             ]
-            step = ways // 2
-            while step:
-                odd = (group & step) != 0
-                for i in range(ways):
-                    if i & step:
-                        continue
-                    a, b = part[i], part[i + step]
-                    if 2 * step * wide == TS:
-                        moved = pltpu.roll(jnp.where(odd, a, b), TS // 2, 1)
-                        part[i] = jnp.where(odd, moved, a)
-                        part[i + step] = jnp.where(odd, b, moved)
-                    else:
-                        part[i] = jnp.where(odd, pltpu.roll(b, step * wide, 1), a)
-                        part[i + step] = jnp.where(odd, b, pltpu.roll(a, TS - step * wide, 1))
-                step //= 2
-            at = r0 * wide
-            for k in range(ways):
-                high, low = halves(part[k])
+            at = r0 * plan.slot_rows
+            for k, value in enumerate(turn(plan, part)):
+                high, low = halves(value)
                 row = (chunk * ways + k) * BS
                 tile_ref[row : row + BS, at : at + TS] = high
                 tile_ref[tall + row : tall + row + BS, at : at + TS] = low
 
 
-def place_kernel(plan, count, *refs):
-    bands = plan.bands
-    packs = refs[:count]
-    before_ref, column_ref, row1_ref, row2_ref, row3_ref = refs[count : count + 5]
-    a0_ref, a1_ref, a2_ref, a3_ref, edge_ref = refs[count + 5 : count + 10]
-    tile_ref, z1_ref, z2_ref, z3_ref = refs[count + 10 :]
-    column = column_ref[...]
-    added = [slot_sums(plan, pack) for pack in packs]
-    at, size, edge = plan.at, plan.size, plan.edge_at
-    for f in range(bands + 1):
-        sums = before_ref[f]
-        for one in added:
-            sums = sums + one[f]
+def place_kernel(plan, pack, before_ref, column_ref, row1_ref, row2_ref, row3_ref,
+                 a0_ref, a1_ref, a2_ref, a3_ref, tile_ref, z1_ref, z2_ref, z3_ref):
+    column = column_ref[: plan.main, :]
+    at, size = plan.at, plan.size
+    planes = plan.bands + 1
+    for f, last in enumerate(slot_sums(plan, pack)):
         tile = tile_ref.at[f % 2]
-        tile_of(plan, sums, tile, TS)
+        tile_of(plan, before_ref[f] + last, tile, TS)
         cols = jnp.dot(column, tile[...], preferred_element_type=F32)
         a0_ref[f] = cols[at[0] : at[1]]
-        z1_ref[f, : size[1]] = cols[at[1] : at[2]]
-        z1_ref[f, size[1] :] = cols[edge[1] : edge[1] + 8]
-        z2_ref[f, : size[2]] = cols[at[2] : at[3]]
-        z2_ref[f, size[2] :] = cols[edge[2] : edge[2] + 8]
-        z3_ref[f, : size[3]] = (
-            cols[at[3] : at[4]] + cols[plan.low_at : plan.low_at + size[3]]
-        )
-        z3_ref[f, size[3] :] = (
-            cols[edge[3] : edge[3] + 8] + cols[plan.low_edge_at : plan.low_edge_at + 8]
-        )
-    planes = bands + 1
+        z1_ref[f] = cols[at[1] : at[2]]
+        z2_ref[f] = cols[at[2] : at[3]]
+        z3_ref[f] = cols[at[3] : at[4]] + cols[plan.low_at : plan.main]
     rows = plan.rows
-    z1 = dot2(z1_ref[...].reshape(planes * (size[1] + 8), rows), row1_ref[...])
-    z2 = dot2(z2_ref[...].reshape(planes * (size[2] + 8), rows), row2_ref[...])
-    z3 = z3_ref[...].reshape(planes * (size[3] + 8), rows)
+    z1 = dot2(z1_ref[...].reshape(planes * size[1], rows), row1_ref[...])
+    z2 = dot2(z2_ref[...].reshape(planes * size[2], rows), row2_ref[...])
+    z3 = z3_ref[...].reshape(planes * size[3], rows)
     z3 = dot2(z3, row3_ref[0]) + jnp.dot(
         z3.astype(BF), row3_ref[1], preferred_element_type=F32
     )
-    start = 0
-    edge_ref[...] = jnp.zeros(edge_ref.shape, edge_ref.dtype)
-    for z, out_ref, level in ((z1, a1_ref, 1), (z2, a2_ref, 2), (z3, a3_ref, 3)):
-        lanes = z.shape[-1]
-        z = z.reshape(planes, size[level] + 8, lanes)
-        out_ref[...] = z[:, : size[level]]
-        for f in range(planes):
-            edge_ref[pl.ds(EDGE * f, EDGE), start : start + lanes] = z[
-                f, size[level] : size[level] + EDGE
-            ].astype(edge_ref.dtype)
-        start += lanes
+    a1_ref[...] = z1.reshape(a1_ref.shape)
+    a2_ref[...] = z2.reshape(a2_ref.shape)
+    a3_ref[...] = z3.reshape(a3_ref.shape)
 
 
 def grow_columns(value, outputs):
@@ -468,28 +478,30 @@
     return jnp.concatenate([ref[:, chunk] for chunk in range(lanes // TS)], axis=-1)
 
 
-def blend_kernel(plan, flag_ref, a0_ref, a1_ref, a2_ref, a3_ref, edge_ref, grow1_ref, grow2_ref, grow3_ref,
+def blend_kernel(plan, a0_ref, a1_ref, a2_ref, a3_ref, near_ref, far_ref, grow1_ref, grow2_ref, grow3_ref,
                  natural_ref, out_ref, g1_ref, g2_ref, g3_ref, e2_ref, e1_ref, e0_ref, strip_ref, sems):
     bands = plan.bands
     planes = bands + 1
     w = plan.strip
-    left, right = flag_ref[0], flag_ref[1]
+    row_tile, col_tile = lax.axis_index("tx"), lax.axis_index("ty")
+    first, last = row_tile == 0, row_tile == plan.n - 1
+    left, right = first & (col_tile > 0), last & (col_tile < plan.m - 1)
+    first, last = first & (col_tile == 0), last & (col_tile == plan.m - 1)
+    edges = near_ref[...].astype(F32) + far_ref[...].astype(F32)
     start = 0
     for level, (src, dst) in enumerate(((a1_ref, g1_ref), (a2_ref, g2_ref), (a3_ref, g3_ref)), 1):
         lanes = src.shape[-1]
         dst[...] = src[...]
         for f in range(planes):
-            edge = edge_ref[pl.ds(EDGE * f, EDGE), start : start + lanes].astype(F32)
+            edge = edges[EDGE * f : EDGE * (f + 1), start : start + lanes]
             far = w >> level
-            dst[f, :EDGE] += jnp.where(left > 0, edge, 0.0)
-            dst[f, far : far + EDGE] += jnp.where(right > 0, edge, 0.0)
+            dst[f, :EDGE] += jnp.where(left, edge, 0.0)
+            dst[f, far : far + EDGE] += jnp.where(right, edge, 0.0)
         start += lanes
-    first = flag_ref[2]
-    last = flag_ref[3]
 
     def inside(level, columns):
         column = lax.broadcasted_iota(jnp.int32, (columns, 1), 0) - 1
-        keep = ((column >= 0) | (first == 0)) & ((column < (w >> level)) | (last == 0))
+        keep = ((column >= 0) | ~first) & ((column < (w >> level)) | ~last)
         return keep.astype(F32)
 
     top = g3_ref[...]
@@ -520,11 +532,17 @@
     up = weave(even, odd, e0_ref, w)
     inverse = 1.0 / (BACKGROUND + a0_ref[bands])
     copies = []
-    for f in range(bands):
-        value = (a0_ref[f] - up[f]) * inverse + up[bands + f]
-        value = jnp.dot(value.astype(BF), natural_ref[...], preferred_element_type=F32)
-        strip_ref[f] = value.astype(BF)
-        copies.append(pltpu.make_async_copy(strip_ref.at[f], out_ref.at[f], sems.at[f]))
+    part = bands // 2
+    for f in range(0, bands, part):
+        value = (a0_ref[f : f + part] - up[f : f + part]) * inverse + up[bands + f : bands + f + part]
+        value = value.astype(BF).reshape(part * w, plan.rows)
+        value = jnp.dot(value, natural_ref[...], preferred_element_type=F32)
+        strip_ref[pl.ds(f, part)] = value.astype(BF).reshape(part, w, plan.rows)
+        copies.append(
+            pltpu.make_async_copy(
+                strip_ref.at[pl.ds(f, part)], out_ref.at[pl.ds(f, part)], sems.at[len(copies)]
+            )
+        )
         copies[-1].start()
     for copy in copies:
         copy.wait()
@@ -565,37 +583,16 @@
         name="pack",
     )(counts, *[off_chip(v) for v in (blocks, cloud[0], destination, offset)])
 
-    def swap(value, mask):
-        return lax.ppermute(value, "tx", [(i, i ^ mask) for i in range(n)])
-
-    def sum_blocks(packs, before):
-        count = len(packs)
-        operands = [on_chip(v) for v in packs + before]
+    def call(kernel, operands, outputs, scratch=(), flops=0, out_specs=None):
         return pl.pallas_call(
-            functools.partial(sum_kernel, plan, count),
-            out_shape=pltpu.VMEM((planes, area, plan.slots), F32),
+            functools.partial(kernel, plan),
+            out_shape=outputs,
             in_specs=[vmem] * len(operands),
-            out_specs=vmem,
-            input_output_aliases={count: 0} if before else {},
-            compiler_params=pltpu.CompilerParams(vmem_limit_bytes=4 << 20),
-            cost_estimate=pl.CostEstimate(
-                flops=4 * planes * plan.slots * area * count * S_DEV,
-                bytes_accessed=planes * plan.slots * area * 4,
-                transcendentals=0,
-            ),
-        )(*operands)
-
-    gathered = [pack]
-    sums = [sum_blocks([pack], [])]
-    mask = n - 1
-    while mask:
-        arrived = [swap(g, mask) for g in gathered]
-        if mask == 1:
-            early, late = gathered[1:] + arrived[:-1], arrived[-1:]
-            if early:
-                sums = [sum_blocks(early, sums)]
-        gathered = gathered + arrived
-        mask //= 2
+            out_specs=out_specs or jax.tree.map(lambda _: vmem, outputs),
+            scratch_shapes=list(scratch),
+            compiler_params=pltpu.CompilerParams(vmem_limit_bytes=16 << 20),
+            cost_estimate=pl.CostEstimate(flops=flops, bytes_accessed=1 << 20, transcendentals=0),
+        )(*[on_chip(v) for v in operands])
 
     column = lax.dynamic_index_in_dim(
         jnp.asarray(plan.column_tables()), row_tile * m + col_tile, keepdims=False
@@ -608,6 +605,7 @@
     padded = np.zeros((plan.rows, wide_top))
     padded[:, :top] = shrinks[2].T[plan.row_of]
     row3 = jnp.asarray(np.stack(split_table(padded)))
+    tables = [column, row1, row2, row3]
     size = plan.size
     shapes = [
         (planes, size[0], plan.rows),
@@ -615,45 +613,50 @@
         (planes, size[2], plan.rows >> 2),
         (planes, size[3], wide_top),
     ]
-    edge_lanes = sum(s[-1] for s in shapes[1:])
-    edge_shape = (up8(EDGE * planes), edge_lanes)
-    a0, a1, a2, a3, edge = pl.pallas_call(
-        functools.partial(place_kernel, plan, len(late)),
-        out_shape=[pltpu.VMEM(s, F32) for s in shapes] + [pltpu.VMEM(edge_shape, BF)],
-        in_specs=[vmem] * (len(late) + 5),
-        compiler_params=pltpu.CompilerParams(vmem_limit_bytes=16 << 20),
-        out_specs=[vmem] * 5,
-        scratch_shapes=[
-            pltpu.VMEM((2, 2 * TS, plan.rows), BF),
-            pltpu.VMEM((planes, size[1] + 8, plan.rows), F32),
-            pltpu.VMEM((planes, size[2] + 8, plan.rows), F32),
-            pltpu.VMEM((planes, size[3] + 8, plan.rows), F32),
+    edge_shape = (up8(EDGE * planes), sum(s[-1] for s in shapes[1:]))
+    sums_shape = pltpu.VMEM((planes, area, plan.slots), F32)
+    work = 2 * planes * area * plan.slots * 2 * S_DEV
+
+    across = [(i, n - 1 - i) for i in range(n)]
+    beside = [(i, i ^ 1) for i in range(n)]
+    far = lax.ppermute(pack, "tx", across)
+    near = lax.ppermute(pack, "tx", beside)
+    sums = call(sum_kernel, [pack], sums_shape, flops=work)
+    late = lax.ppermute(far, "tx", beside)
+    sums, edge_near, edge_far = call(
+        first_kernel,
+        [far, near, sums] + tables,
+        [sums_shape, pltpu.VMEM(edge_shape, BF), pltpu.VMEM(edge_shape, BF)],
+        [
+            pltpu.VMEM((4, plan.near, plan.rows), BF),
+            pltpu.VMEM((LEVELS - 1, 2 * planes, 8, plan.rows), F32),
         ],
-        name="place",
-    )(*[on_chip(v) for v in late + sums], column, row1, row2, row3)
-
-    pairs = []
-    for t in range(n):
-        for j in range(m):
-            other = (j + 1) % m if 2 * t < n else (j - 1) % m
-            pairs.append((t * m + j, t * m + other))
-    edge = lax.ppermute(edge, ("tx", "ty"), pairs)
-
-    first, last = row_tile == 0, row_tile == n - 1
-    flags = jnp.stack(
-        [first & (col_tile > 0), last & (col_tile < m - 1), first & (col_tile == 0), last & (col_tile == m - 1)]
-    ).astype(jnp.int32)
+        flops=4 * work,
+    )
+    turns = [
+        (t * m + j, (j + 1) % m if 2 * t < n else (j - 1) % m) for t in range(n) for j in range(m)
+    ]
+    edge_near = lax.ppermute(edge_near, ("tx", "ty"), [(k, k // m * m + j) for k, j in turns])
+    edge_far = lax.ppermute(edge_far, ("tx", "ty"), [(k, (k // m ^ 1) * m + j) for k, j in turns])
+    levels = call(
+        place_kernel,
+        [late, sums] + tables,
+        [pltpu.VMEM(s, F32) for s in shapes],
+        [pltpu.VMEM((2, 2 * TS, plan.rows), BF)]
+        + [pltpu.VMEM((planes, s, plan.rows), F32) for s in size[1:]],
+        flops=4 * work,
+    )
     grow3 = np.zeros((wide_top, plan.rows >> 2))
     grow3[:top] = grow_grid(top).T
     grow2 = grow_grid(plan.rows >> 2).T
     grow1 = grow_grid(plan.rows >> 1).T[:, plan.row_of]
     natural = np.eye(plan.rows)[plan.row_of]
-    out = pl.pallas_call(
-        functools.partial(blend_kernel, plan),
-        out_shape=jax.ShapeDtypeStruct((bands, size[0], plan.rows), BF),
-        in_specs=[smem] + [vmem] * 9,
-        out_specs=hbm,
-        scratch_shapes=[
+    out = call(
+        blend_kernel,
+        [*levels, edge_near, edge_far]
+        + [jnp.asarray(table.astype(BF)) for table in (grow1, grow2, grow3, natural)],
+        jax.ShapeDtypeStruct((bands, size[0], plan.rows), BF),
+        [
             pltpu.VMEM(shapes[1], F32),
             pltpu.VMEM(shapes[2], F32),
             pltpu.VMEM(shapes[3], F32),
@@ -661,14 +664,10 @@
             pltpu.VMEM((2 * bands, (plan.rows >> 1) // TS, size[1], TS), F32),
             pltpu.VMEM((2 * bands, plan.rows // TS, size[0], TS), F32),
             pltpu.VMEM((bands, size[0], plan.rows), BF),
-            pltpu.SemaphoreType.DMA((bands,)),
+            pltpu.SemaphoreType.DMA((2,)),
         ],
-        compiler_params=pltpu.CompilerParams(vmem_limit_bytes=16 << 20),
-        name="blend",
-    )(
-        flags, *[on_chip(v) for v in (a0, a1, a2, a3, edge)],
-        jnp.asarray(grow1.astype(BF)), jnp.asarray(grow2.astype(BF)), jnp.asarray(grow3.astype(BF)),
-        jnp.asarray(natural.astype(BF)),
+        flops=4 * work,
+        out_specs=hbm,
     )
     return out[:, None]
 
@@ -678,9 +677,8 @@
 
 
 def use_strips(n, m):
-    power = n & (n - 1) == 0
     spread = max(2, 2 * S_DEV // n)
-    return power and 2 <= n and TS // n >= 32 and m >= 2 and S_DEV <= 2 * spread
+    return n == 4 and TS // n >= 32 and m >= 2 and S_DEV <= 2 * spread
 
 
 def solution(mesh):

time: 31.3 us -> 28.7 us (0.917)
  waiting for transfers between devices: 11.8 us -> 8.6 us
  starting transfers between devices: 10.5 us -> 11.4 us
    ppermute x4 -> x5, waiting for transfers between devices: 11.8 us -> 8.6 us  [the longest x1 6.57 us: strip_local(): far = lax.ppermute(pack, 'tx', across)]
    ppermute x4 -> x5, starting transfers between devices: 10.5 us -> 11.4 us  [the longest x1 5.14 us: strip_local(): far = lax.ppermute(pack, 'tx', across)]
  transfers between devices with their start and end apart: 4 -> 5, of which waited for: 3 -> 2; matrix products, arithmetic and copies ran while one was open for 3% -> 3% of each run, Pallas kernels for 5% -> 14%
where the time goes in v4:
time: 28.7 us; the launch traced here: 28.5 us
  starting transfers between devices  11.4 us (40%)
  waiting for transfers between devices  8.6 us (30%)
  Pallas kernels  6.87 us (24%)
  local copies, waits for them, and re-layouts  0.87 us (3%)
  between operations  0.82 us (3%)
    ppermute x1, waiting for transfers between devices, strip_local(): far = lax.ppermute(pack, 'tx', across)  6.57 us
    pallas_call x4, Pallas kernels, call(): pl.pallas_call(functools.partial(kernel, plan), out_shape=outputs, in_spe...  5.71 us
    ppermute x1, starting transfers between devices, strip_local(): far = lax.ppermute(pack, 'tx', across)  5.14 us
    ppermute x1, starting transfers between devices, strip_local(): late = lax.ppermute(far, 'tx', beside)  3.75 us
    ppermute x1, waiting for transfers between devices, strip_local(): lax.ppermute(edge_far, ('tx', 'ty'), [(k, (k // m ^ 1) * m + j) for k, j...  2.02 us
    ppermute x1, starting transfers between devices, strip_local(): lax.ppermute(edge_near, ('tx', 'ty'), [(k, k // m * m + j) for k, j in tu...  1.55 us
    pallas_call x1, Pallas kernels, strip_local(): pl.pallas_call(functools.partial(pack_kernel, plan), out_shape=pltpu.VMEM...  1.16 us
    ppermute x1, starting transfers between devices, strip_local(): lax.ppermute(edge_far, ('tx', 'ty'), [(k, (k // m ^ 1) * m + j) for k, j...  0.94 us
  transfers between devices with their start and end apart: 5, of which 2 were waited for; matrix products, arithmetic and copies ran while one was open for 3% of the time, Pallas kernels for 14%

profile of v4, /device:TPU:0, one launch (start us, length us, event | category | flops | bytes accessed | tf_op | source)
XLA Modules:
  0.0 28.5 jit_solution(9291694395899871628)
XLA Ops:
  0.0 0.0 copy-start
  0.0 0.0 copy-start.3
  0.0 0.0 copy-start.1
  0.7 1.2 %pack.1 = bf16[904,128]{1,0:T(8,128)(2,1)S(1)} custom-call(s32[1,1]{1,0:T(1,128)S(6)} %copy.15.count_ref, bf16[384,256]{1,0:T(8,128)(2,1)} %bitcast.11, bf16[64,256]{1,0:T(8,128)(2,1)} %bitcast.12, s32[1,64]{1,0:T(1,128)} %dest_ref.1, s32[1,64]{1,0:T(1,128)} %offset_ref.1), custom_call_target="tpu_custom_call" | custom-call | tf_op jit(solution)/shard_map/pack/pallas_call | solution.py:570
  1.9 5.1 %collective-permute-start = (bf16[904,128]{1,0:T(8,128)(2,1)S(1)}, bf16[904,128]{1,0:T(8,128)(2,1)S(1)}, u32[]{:S(2)}, u32[]{:S(2)}) collective-permute-start(bf16[904,128]{1,0:T(8,128)(2,1)S(1)} %pack.1), channel_id=1, source_target_pairs={{0,12},{4,8},{8,4},{12,0},{1,13},{5,9},{9,5},{13,1},{2,14},{6,10},... | collective-permute-start | bytes 694280 | tf_op jit(solution)/shard_map/ppermute | solution.py:622
  7.0 0.0 collective-permute-start.2
  7.0 6.6 %collective-permute-done.far = bf16[904,128]{1,0:T(8,128)(2,1)S(1)} collective-permute-done((bf16[904,128]{1,0:T(8,128)(2,1)S(1)}, bf16[904,128]{1,0:T(8,128)(2,1)S(1)}, u32[]{:S(2)}, u32[]{:S(2)}) %collective-permute-start) | collective-permute-done | bytes 231456 | tf_op jit(solution)/shard_map/ppermute | solution.py:622
  13.6 3.7 %collective-permute-start.1 = (bf16[904,128]{1,0:T(8,128)(2,1)S(1)}, bf16[904,128]{1,0:T(8,128)(2,1)S(1)}, u32[]{:S(2)}, u32[]{:S(2)}) collective-permute-start(bf16[904,128]{1,0:T(8,128)(2,1)S(1)} %collective-permute-done.far), channel_id=1, source_target_pairs={{0,4},{4,0},{8,12},{12,8},{1,5},{5,1},{9,13},{13,9},{2,6},{6,2},{1... | collective-permute-start | bytes 694280 | tf_op jit(solution)/shard_map/ppermute | solution.py:625
  17.4 0.6 %shard_map.127.before_ref = f32[7,256,256]{2,1,0:T(8,128)S(1)} custom-call(bf16[904,128]{1,0:T(8,128)(2,1)S(1)} %pack.1), custom_call_target="tpu_custom_call" | custom-call | flops 117440512 | bytes 1048576 | tf_op jit(solution)/shard_map/pallas_call | solution.py:587
  17.9 0.8 %dynamic-slice_bitcast_fusion.column_ref = bf16[112,256]{1,0:T(8,128)(2,1)S(1)} fusion(bf16[8,112,256]{2,1,0:T(8,128)(2,1)} %constant.33.clone, s32[]{:T(128)S(6)} %select_n.4), kind=kLoop, calls=%fused_computation | loop fusion | bytes 114692 | tf_op jit(solution)/shard_map/jit(dynamic_index_in_dim)/squeeze | solution.py:597
  18.8 0.0 collective-permute-done.2.near
  18.8 0.0 copy-done
  18.8 0.0 copy-done.3
  18.8 0.0 copy-done.1
  18.8 1.6 %shard_map.128 = (f32[7,256,256]{2,1,0:T(8,128)S(1)}, bf16[24,512]{1,0:T(8,128)(2,1)S(1)}, bf16[24,512]{1,0:T(8,128)(2,1)S(1)}) custom-call(bf16[904,128]{1,0:T(8,128)(2,1)S(1)} %collective-permute-done.far, bf16[904,128]{1,0:T(8,128)(2,1)S(1)} %collective-permute-done.2.near, f32[7,256,256]{2,1,0:T(8,128)S(1)} %shard_map.127.before_ref, ...), custom_call_target="tpu_custom_call" | custom-call | flops 469762048 | bytes 1048576 | tf_op jit(solution)/shard_map/pallas_call | solution.py:587
  20.4 0.0 copy-start.2
  20.4 0.0 copy-start.4
  20.4 0.0 copy-start.5
  20.5 0.0 copy-start.6
  20.5 1.6 %collective-permute-start.3 = (bf16[24,512]{1,0:T(8,128)(2,1)S(1)}, bf16[24,512]{1,0:T(8,128)(2,1)S(1)}, u32[]{:S(2)}, u32[]{:S(2)}) collective-permute-start(bf16[24,512]{1,0:T(8,128)(2,1)S(1)} %get-tuple-element.17), channel_id=1, source_target_pairs={{0,2},{2,0},{4,6},{6,4},{8,10},{10,8},{12,14},{14,12},{1,3},{3,1},... | collective-permute-start | bytes 73736 | tf_op jit(solution)/shard_map/ppermute | solution.py:639
  22.0 0.9 %collective-permute-start.4 = (bf16[24,512]{1,0:T(8,128)(2,1)S(1)}, bf16[24,512]{1,0:T(8,128)(2,1)S(1)}, u32[]{:S(2)}, u32[]{:S(2)}) collective-permute-start(bf16[24,512]{1,0:T(8,128)(2,1)S(1)} %get-tuple-element.18), channel_id=1, source_target_pairs={{0,6},{2,4},{4,2},{6,0},{8,14},{10,12},{12,10},{14,8},{1,7},{3,5},... | collective-permute-start | bytes 73736 | tf_op jit(solution)/shard_map/ppermute | solution.py:640
  23.0 0.0 collective-permute-done.1.pack
  23.0 1.7 %shard_map.129 = (f32[7,32,512]{2,1,0:T(8,128)S(1)}, f32[7,24,256]{2,1,0:T(8,128)S(1)}, f32[7,16,128]{2,1,0:T(8,128)S(1)}, f32[7,8,128]{2,1,0:T(8,128)S(1)}) custom-call(bf16[904,128]{1,0:T(8,128)(2,1)S(1)} %collective-permute-done.1.pack, f32[7,256,256]{2,1,0:T(8,128)S(1)} %get-tuple-element.12.before_ref, ...), custom_call_target="tpu_custom_call" | custom-call | flops 469762048 | bytes 1048576 | tf_op jit(solution)/shard_map/pallas_call | solution.py:587
  24.7 0.0 collective-permute-done.3.near_ref
  24.7 2.0 %collective-permute-done.4.far_ref = bf16[24,512]{1,0:T(8,128)(2,1)S(1)} collective-permute-done((bf16[24,512]{1,0:T(8,128)(2,1)S(1)}, bf16[24,512]{1,0:T(8,128)(2,1)S(1)}, u32[]{:S(2)}, u32[]{:S(2)}) %collective-permute-start.4) | collective-permute-done | bytes 24608 | tf_op jit(solution)/shard_map/ppermute | solution.py:640
  26.7 0.0 copy-done.2
  26.8 0.0 copy-done.4
  26.8 0.0 copy-done.5
  26.8 0.0 copy-done.6
  26.8 1.8 %shard_map.130 = bf16[6,32,512]{2,1,0:T(8,128)(2,1)} custom-call(f32[7,32,512]{2,1,0:T(8,128)S(1)} %get-tuple-element.13.a0_ref, f32[7,24,256]{2,1,0:T(8,128)S(1)} %get-tuple-element.14.a1_ref, f32[7,16,128]{2,1,0:T(8,128)S(1)} %get-tuple-element.15.a2_ref, f32[7,8,128]{2,1,0:T(8,128)S(1)} %get-tuple-element.16.a3_ref, ...), custom_call_target="tpu_custom_call" | custom-call | flops 469762048 | bytes 1048576 | tf_op jit(solution)/shard_map/pallas_call | solution.py:587
Async XLA Ops:
  0.0 18.8 %copy-start = (bf16[512,256]{1,0:T(8,128)(2,1)S(1)}, bf16[512,256]{1,0:T(8,128)(2,1)}, u32[]{:S(2)}) copy-start(bf16[512,256]{1,0:T(8,128)(2,1)} %constant.34.clone.row1_ref) | copy-start | bytes 786436
  0.0 18.8 %copy-start.3 = (bf16[512,128]{1,0:T(8,128)(2,1)S(1)}, bf16[512,128]{1,0:T(8,128)(2,1)}, u32[]{:S(2)}) copy-start(bf16[512,128]{1,0:T(8,128)(2,1)} %constant.35.clone.row2_ref) | copy-start | bytes 393220
  0.0 18.8 %copy-start.1 = (bf16[2,512,128]{2,1,0:T(8,128)(2,1)S(1)}, bf16[2,512,128]{2,1,0:T(8,128)(2,1)}, u32[]{:S(2)}) copy-start(bf16[2,512,128]{2,1,0:T(8,128)(2,1)} %constant.36.clone.row3_ref) | copy-start | bytes 786436
  1.9 11.7 %collective-permute-start = (bf16[904,128]{1,0:T(8,128)(2,1)S(1)}, bf16[904,128]{1,0:T(8,128)(2,1)S(1)}, u32[]{:S(2)}, u32[]{:S(2)}) collective-permute-start(bf16[904,128]{1,0:T(8,128)(2,1)S(1)} %pack.1), channel_id=1, source_target_pairs={{0,12},{4,8},{8,4},{12,0},{1,13},{5,9},{9,5},{13,1},{2,14},{6,10},... | collective-permute-start | bytes 694280 | tf_op jit(solution)/shard_map/ppermute | solution.py:622
  7.0 11.7 %collective-permute-start.2 = (bf16[904,128]{1,0:T(8,128)(2,1)S(1)}, bf16[904,128]{1,0:T(8,128)(2,1)S(1)}, u32[]{:S(2)}, u32[]{:S(2)}) collective-permute-start(bf16[904,128]{1,0:T(8,128)(2,1)S(1)} %pack.1), channel_id=1, source_target_pairs={{0,4},{4,0},{8,12},{12,8},{1,5},{5,1},{9,13},{13,9},{2,6},{6,2},{1... | collective-permute-start | bytes 694280 | tf_op jit(solution)/shard_map/ppermute | solution.py:623
  13.6 9.4 %collective-permute-start.1 = (bf16[904,128]{1,0:T(8,128)(2,1)S(1)}, bf16[904,128]{1,0:T(8,128)(2,1)S(1)}, u32[]{:S(2)}, u32[]{:S(2)}) collective-permute-start(bf16[904,128]{1,0:T(8,128)(2,1)S(1)} %collective-permute-done.far), channel_id=1, source_target_pairs={{0,4},{4,0},{8,12},{12,8},{1,5},{5,1},{9,13},{13,9},{2,6},{6,2},{1... | collective-permute-start | bytes 694280 | tf_op jit(solution)/shard_map/ppermute | solution.py:625
  20.4 6.3 %copy-start.2 = (bf16[512,512]{1,0:T(8,128)(2,1)S(1)}, bf16[512,512]{1,0:T(8,128)(2,1)}, u32[]{:S(2)}) copy-start(bf16[512,512]{1,0:T(8,128)(2,1)} %constant.40.clone.natural_ref) | copy-start | bytes 1572868
  20.4 6.3 %copy-start.4 = (bf16[256,512]{1,0:T(8,128)(2,1)S(1)}, bf16[256,512]{1,0:T(8,128)(2,1)}, u32[]{:S(2)}) copy-start(bf16[256,512]{1,0:T(8,128)(2,1)} %constant.37.clone.grow1_ref) | copy-start | bytes 786436
  20.4 6.3 %copy-start.5 = (bf16[128,256]{1,0:T(8,128)(2,1)S(1)}, bf16[128,256]{1,0:T(8,128)(2,1)}, u32[]{:S(2)}) copy-start(bf16[128,256]{1,0:T(8,128)(2,1)} %constant.38.clone.grow2_ref) | copy-start | bytes 196612
  20.5 6.3 %copy-start.6 = (bf16[128,128]{1,0:T(8,128)(2,1)S(1)}, bf16[128,128]{1,0:T(8,128)(2,1)}, u32[]{:S(2)}) copy-start(bf16[128,128]{1,0:T(8,128)(2,1)} %constant.39.clone.grow3_ref) | copy-start | bytes 98308
  20.5 4.3 %collective-permute-start.3 = (bf16[24,512]{1,0:T(8,128)(2,1)S(1)}, bf16[24,512]{1,0:T(8,128)(2,1)S(1)}, u32[]{:S(2)}, u32[]{:S(2)}) collective-permute-start(bf16[24,512]{1,0:T(8,128)(2,1)S(1)} %get-tuple-element.17), channel_id=1, source_target_pairs={{0,2},{2,0},{4,6},{6,4},{8,10},{10,8},{12,14},{14,12},{1,3},{3,1},... | collective-permute-start | bytes 73736 | tf_op jit(solution)/shard_map/ppermute | solution.py:639
  22.0 4.7 %collective-permute-start.4 = (bf16[24,512]{1,0:T(8,128)(2,1)S(1)}, bf16[24,512]{1,0:T(8,128)(2,1)S(1)}, u32[]{:S(2)}, u32[]{:S(2)}) collective-permute-start(bf16[24,512]{1,0:T(8,128)(2,1)S(1)} %get-tuple-element.18), channel_id=1, source_target_pairs={{0,6},{2,4},{4,2},{6,0},{8,14},{10,12},{12,10},{14,8},{1,7},{3,5},... | collective-permute-start | bytes 73736 | tf_op jit(solution)/shard_map/ppermute | solution.py:640

commit v5 on v4

--- a/solution.py
+++ b/solution.py
@@ -242,13 +242,16 @@
             self.at.append(self.at[-1] + size)
         self.low_at = self.at[LEVELS]
         self.main = self.low_at + self.size[3]
-        self.edge_at = [None] + [self.main + 8 * k for k in range(LEVELS - 1)]
-        self.total = self.main + 8 * (LEVELS - 1)
-        self.near = TS // self.slot_rows * BS
-        self.weight_at = bands // 2 * BS * BS
-        self.code_at = self.weight_at + BS * BS // 2
+        self.edge_rows = 8 * (LEVELS - 1)
+        self.total = self.main + 2 * self.edge_rows
+        self.near = 2 * BS
+        self.half = BS * BS // 2
+        self.weight_at = bands * self.half
+        self.code_at = self.weight_at + self.half
         order = np.arange(self.rows)
-        self.row_of = order % self.slot_rows * BS + order // self.slot_rows
+        wide = self.slot_rows
+        u, half, v = order // (4 * wide), order // (2 * wide) % 2, order // wide % 2
+        self.row_of = order % wide * BS + half * (BS // 2) + 2 * u + v
 
     def column_tables(self):
         n, m, w = self.n, self.m, self.strip
@@ -263,18 +266,15 @@
                         o = base + k
                         if 0 <= o < width >> level:
                             tables[t, j, self.at[level] + k] = grids[level][o, j * TS : (j + 1) * TS]
-                    if level == 0:
-                        continue
-                    if 2 * t < n:
-                        base = ((j + 1) * TS >> level) - 1
-                    else:
-                        base = (j * TS >> level) - 1
-                    for k in range(EDGE):
-                        o = base + k
-                        if 0 <= o < width >> level:
-                            row = grids[level][o, j * TS : (j + 1) * TS]
-                            row = row[TS - self.near :] if 2 * t < n else row[: self.near]
-                            tables[t, j, self.edge_at[level] + k, : self.near] = row
+                    for which, target in enumerate((t, t ^ n // 2)):
+                        right = 2 * target < n
+                        base = ((j + 1 if right else j) * TS >> level) - 1
+                        at = self.main + which * self.edge_rows + 8 * (level - 1)
+                        for k in range(EDGE if level else 0):
+                            if 0 <= base + k < width >> level:
+                                row = grids[level][base + k, j * TS : (j + 1) * TS]
+                                row = row[TS - self.near :] if right else row[: self.near]
+                                tables[t, j, at + k, : self.near] = row
         high, low = split_table(tables)
         high[:, :, self.low_at : self.main] = low[:, :, self.at[3] : self.at[4]]
         return np.concatenate([high, high], axis=-1).reshape(n * m, self.total, 2 * TS)
@@ -292,15 +292,19 @@
     )
 
 
-def pack_kernel(plan, count_ref, scenes_ref, cloud_ref, dest_ref, offset_ref, out_ref, raw, cloud, dest,
+def pack_kernel(plan, count_ref, scenes_ref, cloud_ref, dest_ref, offset_ref, out_ref, raw, dest,
                 offset, sems):
     rows = 2 * S_DEV
-    pairs = plan.bands // 2
+    half = plan.half
     copies = [
         pltpu.make_async_copy(source, target, sems.at[k])
         for k, (source, target) in enumerate(
-            [(dest_ref, dest), (offset_ref, offset), (cloud_ref, cloud)]
-            + [(scenes_ref.at[pl.ds(q * rows, rows)], raw.at[pl.ds(q * rows, rows)]) for q in range(pairs)]
+            (
+                (dest_ref, dest),
+                (offset_ref, offset),
+                (cloud_ref, raw.at[plan.bands]),
+                (scenes_ref, raw.at[pl.ds(0, plan.bands)]),
+            )
         )
     ]
     for copy in copies:
@@ -314,141 +318,139 @@
     code = jnp.where(live, code, DEAD).astype(F32)
     code = jnp.broadcast_to(jnp.concatenate([code, code], axis=1), (CODE_ROWS, rows))
     out_ref[plan.code_at :, :] = code.astype(BF)
-    copies[2].wait()
-    half = BS * BS // 2
-    weights = jnp.concatenate([cloud[:, :half], cloud[:, half:]], axis=0)
-    out_ref[plan.weight_at : plan.code_at, :] = weights.T
-    for q in range(pairs):
-        copies[3 + q].wait()
-        out_ref[q * BS * BS : (q + 1) * BS * BS, :] = raw[q * rows : (q + 1) * rows, :].T
+    for f in (plan.bands, *range(plan.bands)):
+        if f == plan.bands:
+            copies[2].wait()
+        elif f == 0:
+            copies[3].wait()
+        block = raw[f]
+        block = jnp.concatenate([block[:, :half], block[:, half:]], axis=0)
+        out_ref[f * half : (f + 1) * half, :] = block.T
+
+
+def load_kernel(plan, column_ref, *refs):
+    count = (len(refs) - 2) // 2
+    sources, targets, sems = refs[:count], refs[count:-1], refs[-1]
+    mine = lax.axis_index("tx") * plan.m + lax.axis_index("ty")
+    copies = [
+        pltpu.make_async_copy(source, target, sems.at[k])
+        for k, (source, target) in enumerate(zip((column_ref.at[mine], *sources), targets))
+    ]
+    for copy in copies:
+        copy.start()
+    for copy in copies:
+        copy.wait()
 
 
 def landing_of(plan, pack):
     codes = pack[plan.code_at : plan.code_at + CODE_ROWS, :].astype(F32).T[:, :1]
     blocks = codes.shape[0]
+    pair = float(2 * plan.slot_rows)
     second = lax.broadcasted_iota(jnp.int32, (blocks, 1), 0) >= S_DEV
-    codes = codes + jnp.where(second, float(plan.slots), 0.0)
+    codes = codes + pair * jnp.floor(codes / pair) + jnp.where(second, pair, 0.0)
     slot = lax.broadcasted_iota(jnp.int32, (blocks, 2 * plan.slots), 1).astype(F32)
     landing = jnp.where(slot == codes, 1.0, 0.0).astype(BF)
     return jnp.concatenate([landing, landing], axis=0)
 
 
-def slot_sums(plan, pack):
-    landing2 = landing_of(plan, pack)
-    area = BS * BS
-    blocks = 2 * S_DEV
-    both = pack[plan.weight_at : plan.code_at, :].astype(F32)
-    first = lax.broadcasted_iota(jnp.int32, both.shape, 1) < S_DEV
-    turned = pltpu.roll(both, S_DEV, 1)
-    weights = jnp.concatenate(
-        [jnp.where(first, both, turned), jnp.where(first, turned, both)], axis=0
-    )
-    result = []
-    for q in range(plan.bands // 2):
-        value = pack[q * area : (q + 1) * area, :].astype(F32) * weights
-        high, low = halves(value)
-        pair = jnp.dot(
-            jnp.concatenate([high, low], axis=1), landing2, preferred_element_type=F32
-        )
-        result += [pair[:, : plan.slots], pair[:, plan.slots :]]
-    result.append(
-        jnp.dot(weights.astype(BF), landing2[:blocks, : plan.slots], preferred_element_type=F32)
-    )
-    return result
-
-
-def sum_kernel(plan, pack, out_ref):
-    for f, sums in enumerate(slot_sums(plan, pack)):
-        out_ref[f] = sums
-
-
-def turn(plan, part):
+def slot_sums(plan, pack, prod_ref):
+    weight = pack[plan.weight_at : plan.code_at, :]
+    half, blocks = plan.half, 2 * S_DEV
+    for f in range(plan.bands):
+        rows = pl.ds(f * half, half)
+        high, low = halves(pack[f * half : (f + 1) * half, :].astype(F32) * weight.astype(F32))
+        prod_ref[rows, :blocks] = high
+        prod_ref[rows, blocks:] = low
+    rows = pl.ds(plan.weight_at, half)
+    prod_ref[rows, :blocks] = weight
+    prod_ref[rows, blocks:] = jnp.zeros_like(weight)
+    return jnp.dot(prod_ref[...], landing_of(plan, pack), preferred_element_type=F32)
+
+
+def turn(plan, a, b):
     wide = plan.slot_rows
-    ways = TS // wide
-    group = lax.broadcasted_iota(jnp.int32, (BS, TS), 1) // wide
-    step = ways // 2
-    while step:
-        odd = (group & step) != 0
-        for i in range(ways):
-            if i & step:
-                continue
-            a, b = part[i], part[i + step]
-            if 2 * step * wide == TS:
-                moved = pltpu.roll(jnp.where(odd, a, b), TS // 2, 1)
-                part[i] = jnp.where(odd, moved, a)
-                part[i + step] = jnp.where(odd, b, moved)
-            else:
-                part[i] = jnp.where(odd, pltpu.roll(b, step * wide, 1), a)
-                part[i + step] = jnp.where(odd, b, pltpu.roll(a, TS - step * wide, 1))
-        step //= 2
-    return part
+    odd = lax.broadcasted_iota(jnp.int32, a.shape, 1) // wide % 2 == 1
+    return jnp.where(odd, pltpu.roll(b, wide, 1), a), jnp.where(odd, b, pltpu.roll(a, TS - wide, 1))
+
+
+def edge_of(plan, side_ref, table, row_refs, out_ref, tile_ref, z_ref):
+    planes = plan.bands + 1
+    rows = plan.rows
+    for f in range(planes):
+        tile = tile_ref.at[f % 2]
+        for u in range(BS // 4):
+            at = f * plan.half + 2 * u * BS
+            pair = turn(plan, side_ref[at : at + BS], side_ref[at + BS : at + 2 * BS])
+            for k, value in enumerate(pair):
+                tile[k * BS : (k + 1) * BS, u * TS : (u + 1) * TS] = value.astype(BF)
+        cols = jnp.dot(table, tile[...], preferred_element_type=F32)
+        for level in range(LEVELS - 1):
+            z_ref[level, f] = cols[8 * level : 8 * level + 8]
+    start = 0
+    out_ref[...] = jnp.zeros(out_ref.shape, out_ref.dtype)
+    for level, ref in enumerate(row_refs):
+        row_table = ref[...] if len(ref.shape) == 2 else ref[0]
+        lanes = row_table.shape[1]
+        z = z_ref[level].reshape(planes * 8, rows).astype(BF)
+        z = jnp.dot(z, row_table, preferred_element_type=F32).reshape(planes, 8, lanes)
+        for f in range(planes):
+            out_ref[pl.ds(EDGE * f, EDGE), start : start + lanes] = z[f, :EDGE].astype(BF)
+        start += lanes
+
+
+def side_of(plan, sums, right):
+    return jnp.where(right, sums[:, 2 * plan.slots - TS :], sums[:, :TS])
+
+
+def own_kernel(plan, pack, column_ref, row1_ref, row2_ref, row3_ref,
+               out_ref, edge_ref, prod_ref, side_ref, tile_ref, z_ref):
+    right = 2 * (lax.axis_index("tx") ^ plan.n // 2) < plan.n
+    sums = slot_sums(plan, pack, prod_ref)
+    out_ref[...] = sums
+    side_ref[...] = side_of(plan, sums, right)
+    table = column_ref[plan.main + plan.edge_rows :, : plan.near]
+    edge_of(plan, side_ref, table, (row1_ref, row2_ref, row3_ref), edge_ref, tile_ref, z_ref)
 
 
 def first_kernel(plan, far, near, before_ref, column_ref, row1_ref, row2_ref, row3_ref,
-                 out_ref, near_ref, far_ref, tile_ref, z_ref):
-    planes = plan.bands + 1
+                 out_ref, edge_ref, prod_ref, side_ref, tile_ref, z_ref):
     right = 2 * lax.axis_index("tx") < plan.n
-    edge_table = column_ref[plan.main :, : plan.near]
-    ways = TS // plan.slot_rows
-    rows = plan.rows
-    far_sums, near_sums = slot_sums(plan, far), slot_sums(plan, near)
-    for f in range(planes):
-        sums = before_ref[f] + far_sums[f] + near_sums[f]
-        out_ref[f] = sums
-        for which, one in enumerate((sums, far_sums[f])):
-            side = jnp.where(right, one[:, plan.slots - TS :], one[:, :TS])
-            tile = tile_ref.at[2 * (f % 2) + which]
-            for r0 in range(0, BS, ways):
-                part = [side[(r0 + k) * BS : (r0 + k + 1) * BS] for k in range(ways)]
-                for k, value in enumerate(turn(plan, part)):
-                    at = r0 * plan.slot_rows
-                    tile[k * BS : (k + 1) * BS, at : at + TS] = value.astype(BF)
-            cols = jnp.dot(edge_table, tile[...], preferred_element_type=F32)
-            for level in range(1, LEVELS):
-                z_ref[level - 1, which * planes + f] = cols[8 * level - 8 : 8 * level]
-    start = 0
-    for ref in (near_ref, far_ref):
-        ref[...] = jnp.zeros(ref.shape, ref.dtype)
-    for level, table in ((1, row1_ref[...]), (2, row2_ref[...]), (3, row3_ref[0])):
-        lanes = table.shape[1]
-        z = z_ref[level - 1].reshape(2 * planes * 8, rows).astype(BF)
-        z = jnp.dot(z, table, preferred_element_type=F32).reshape(2 * planes, 8, lanes)
-        for which, ref in enumerate((near_ref, far_ref)):
-            for f in range(planes):
-                ref[pl.ds(EDGE * f, EDGE), start : start + lanes] = z[which * planes + f, :EDGE].astype(BF)
-        start += lanes
-
-
-def tile_of(plan, sums, tile_ref, tall):
-    ways = TS // plan.slot_rows
-    for chunk in range(plan.slots // TS):
-        for r0 in range(0, BS, ways):
-            part = [
-                sums[(r0 + k) * BS : (r0 + k + 1) * BS, chunk * TS : (chunk + 1) * TS]
-                for k in range(ways)
-            ]
-            at = r0 * plan.slot_rows
-            for k, value in enumerate(turn(plan, part)):
+    one = slot_sums(plan, far, prod_ref.at[0])
+    sums = before_ref[...] + one + slot_sums(plan, near, prod_ref.at[1])
+    out_ref[...] = sums
+    side_ref[...] = side_of(plan, sums, right)
+    table = column_ref[plan.main : plan.main + plan.edge_rows, : plan.near]
+    edge_of(plan, side_ref, table, (row1_ref, row2_ref, row3_ref), edge_ref, tile_ref, z_ref)
+
+
+def tile_of(plan, sums, at, tile_ref):
+    for pair in range(2 * plan.slots // TS):
+        lanes = slice(pair * TS, (pair + 1) * TS)
+        for u in range(BS // 4):
+            row = at + 2 * u * BS
+            both = turn(plan, sums[row : row + BS, lanes], sums[row + BS : row + 2 * BS, lanes])
+            for k, value in enumerate(both):
                 high, low = halves(value)
-                row = (chunk * ways + k) * BS
-                tile_ref[row : row + BS, at : at + TS] = high
-                tile_ref[tall + row : tall + row + BS, at : at + TS] = low
+                row = (2 * pair + k) * BS
+                tile_ref[row : row + BS, u * TS : (u + 1) * TS] = high
+                tile_ref[TS + row : TS + row + BS, u * TS : (u + 1) * TS] = low
 
 
 def place_kernel(plan, pack, before_ref, column_ref, row1_ref, row2_ref, row3_ref,
-                 a0_ref, a1_ref, a2_ref, a3_ref, tile_ref, z1_ref, z2_ref, z3_ref):
+                 a0_ref, a1_ref, a2_ref, a3_ref, prod_ref, sums_ref, tile_ref, z1_ref, z2_ref, z3_ref):
     column = column_ref[: plan.main, :]
     at, size = plan.at, plan.size
     planes = plan.bands + 1
-    for f, last in enumerate(slot_sums(plan, pack)):
+    rows = plan.rows
+    sums_ref[...] = before_ref[...] + slot_sums(plan, pack, prod_ref)
+    for f in range(planes):
         tile = tile_ref.at[f % 2]
-        tile_of(plan, before_ref[f] + last, tile, TS)
+        tile_of(plan, sums_ref, f * plan.half, tile)
         cols = jnp.dot(column, tile[...], preferred_element_type=F32)
         a0_ref[f] = cols[at[0] : at[1]]
         z1_ref[f] = cols[at[1] : at[2]]
         z2_ref[f] = cols[at[2] : at[3]]
         z3_ref[f] = cols[at[3] : at[4]] + cols[plan.low_at : plan.main]
-    rows = plan.rows
     z1 = dot2(z1_ref[...].reshape(planes * size[1], rows), row1_ref[...])
     z2 = dot2(z2_ref[...].reshape(planes * size[2], rows), row2_ref[...])
     z3 = z3_ref[...].reshape(planes * size[3], rows)
@@ -524,12 +526,12 @@
         blend = (current[:bands] - up[:bands]) * inverse + up[bands:]
         blend = blend * inside(level, blend.shape[1])
     stacked = jnp.concatenate([g1_ref[:bands], blend], axis=0)
-    k, c, r = stacked.shape
-    wide = dot2(stacked.reshape(k * c, r), grow1_ref[...]).reshape(k, c, plan.rows)
     half = w // 2
-    a, b, c = wide[:, :half], wide[:, 1 : half + 1], wide[:, 2 : half + 2]
+    a, b, c = stacked[:, :half], stacked[:, 1 : half + 1], stacked[:, 2 : half + 2]
     even, odd = (a + 6.0 * b + c) * 0.125, (b + c) * 0.5
-    up = weave(even, odd, e0_ref, w)
+    tall = weave(even, odd, e0_ref, w)
+    up = dot2(tall.reshape(2 * bands * w, tall.shape[-1]), grow1_ref[...])
+    up = up.reshape(2 * bands, w, plan.rows)
     inverse = 1.0 / (BACKGROUND + a0_ref[bands])
     copies = []
     part = bands // 2
@@ -558,7 +560,6 @@
 
 def strip_local(scenes, cloud, destination, offset, counts):
     n, m = lax.axis_size("tx"), lax.axis_size("ty")
-    row_tile, col_tile = lax.axis_index("tx"), lax.axis_index("ty")
     bands = scenes.shape[2]
     plan = Plan(n, m, bands)
     planes = bands + 1
@@ -566,18 +567,17 @@
     vmem = pl.BlockSpec(memory_space=pltpu.VMEM)
     smem = pl.BlockSpec(memory_space=pltpu.SMEM)
     hbm = pl.BlockSpec(memory_space=pl.ANY)
-    blocks = jnp.swapaxes(scenes[0], 0, 1).reshape(bands * S_DEV, area)
+    blocks = jnp.swapaxes(scenes[0], 0, 1)
     pack = pl.pallas_call(
         functools.partial(pack_kernel, plan),
         out_shape=pltpu.VMEM((plan.code_at + CODE_ROWS, 2 * S_DEV), BF),
         in_specs=[smem] + [hbm] * 4,
         out_specs=vmem,
         scratch_shapes=[
-            pltpu.VMEM(blocks.shape, BF),
-            pltpu.VMEM(cloud[0].shape, BF),
+            pltpu.VMEM((planes, S_DEV, area), BF),
             pltpu.VMEM(destination.shape, jnp.int32),
             pltpu.VMEM(offset.shape, jnp.int32),
-            pltpu.SemaphoreType.DMA((3 + bands // 2,)),
+            pltpu.SemaphoreType.DMA((4,)),
         ],
         compiler_params=pltpu.CompilerParams(vmem_limit_bytes=4 << 20),
         name="pack",
@@ -594,18 +594,31 @@
             cost_estimate=pl.CostEstimate(flops=flops, bytes_accessed=1 << 20, transcendentals=0),
         )(*[on_chip(v) for v in operands])
 
-    column = lax.dynamic_index_in_dim(
-        jnp.asarray(plan.column_tables()), row_tile * m + col_tile, keepdims=False
-    )
     shrinks = row_shrinks(plan.rows)
-    row1 = jnp.asarray(shrinks[0].T[plan.row_of].astype(BF))
-    row2 = jnp.asarray(shrinks[1].T[plan.row_of].astype(BF))
+    row1 = shrinks[0].T[plan.row_of]
+    row2 = shrinks[1].T[plan.row_of]
     top = plan.rows >> 3
     wide_top = max(top, 128)
     padded = np.zeros((plan.rows, wide_top))
     padded[:, :top] = shrinks[2].T[plan.row_of]
-    row3 = jnp.asarray(np.stack(split_table(padded)))
-    tables = [column, row1, row2, row3]
+    row3 = np.stack(split_table(padded))
+    grow3 = np.zeros((wide_top, plan.rows >> 2))
+    grow3[:top] = grow_grid(top).T
+    grow2 = grow_grid(plan.rows >> 2).T
+    grow1 = grow_grid(plan.rows >> 1).T[:, plan.row_of]
+    natural = np.eye(plan.rows)[plan.row_of]
+    constants = [plan.column_tables(), row1, row2, row3, grow1, grow2, grow3, natural]
+    constants = [off_chip(jnp.asarray(table.astype(BF))) for table in constants]
+    loaded = pl.pallas_call(
+        functools.partial(load_kernel, plan),
+        out_shape=[pltpu.VMEM(c.shape[k == 0 :], BF) for k, c in enumerate(constants)],
+        in_specs=[hbm] * len(constants),
+        out_specs=[vmem] * len(constants),
+        scratch_shapes=[pltpu.SemaphoreType.DMA((len(constants),))],
+        compiler_params=pltpu.CompilerParams(vmem_limit_bytes=4 << 20),
+        name="load",
+    )(*constants)
+    tables, grows = list(loaded[:4]), list(loaded[4:])
     size = plan.size
     shapes = [
         (planes, size[0], plan.rows),
@@ -614,47 +627,61 @@
         (planes, size[3], wide_top),
     ]
     edge_shape = (up8(EDGE * planes), sum(s[-1] for s in shapes[1:]))
-    sums_shape = pltpu.VMEM((planes, area, plan.slots), F32)
+    sums_shape = pltpu.VMEM((planes * plan.half, 2 * plan.slots), F32)
+    prod_shape = (planes * plan.half, 4 * S_DEV)
     work = 2 * planes * area * plan.slots * 2 * S_DEV
 
     across = [(i, n - 1 - i) for i in range(n)]
     beside = [(i, i ^ 1) for i in range(n)]
     far = lax.ppermute(pack, "tx", across)
     near = lax.ppermute(pack, "tx", beside)
-    sums = call(sum_kernel, [pack], sums_shape, flops=work)
+    edge_work = [
+        pltpu.VMEM((planes * plan.half, TS), F32),
+        pltpu.VMEM((2, plan.near, plan.rows), BF),
+        pltpu.VMEM((LEVELS - 1, planes, 8, plan.rows), F32),
+    ]
+    sums_and_edge = [sums_shape, pltpu.VMEM(edge_shape, BF)]
+    sums, edge_far = call(
+        own_kernel,
+        [pack] + tables,
+        sums_and_edge,
+        [pltpu.VMEM(prod_shape, BF)] + edge_work,
+        flops=work,
+    )
+
+    def over(value, shift):
+        pairs = []
+        for t in range(n):
+            for j in range(m):
+                target = t ^ shift
+                pairs.append((t * m + j, target * m + (j + 1 if 2 * target < n else j - 1) % m))
+        return lax.ppermute(value, ("tx", "ty"), pairs)
+
+    edge_far = over(edge_far, n // 2)
     late = lax.ppermute(far, "tx", beside)
-    sums, edge_near, edge_far = call(
+    sums, edge_near = call(
         first_kernel,
         [far, near, sums] + tables,
-        [sums_shape, pltpu.VMEM(edge_shape, BF), pltpu.VMEM(edge_shape, BF)],
-        [
-            pltpu.VMEM((4, plan.near, plan.rows), BF),
-            pltpu.VMEM((LEVELS - 1, 2 * planes, 8, plan.rows), F32),
-        ],
+        sums_and_edge,
+        [pltpu.VMEM((2, *prod_shape), BF)] + edge_work,
         flops=4 * work,
     )
-    turns = [
-        (t * m + j, (j + 1) % m if 2 * t < n else (j - 1) % m) for t in range(n) for j in range(m)
-    ]
-    edge_near = lax.ppermute(edge_near, ("tx", "ty"), [(k, k // m * m + j) for k, j in turns])
-    edge_far = lax.ppermute(edge_far, ("tx", "ty"), [(k, (k // m ^ 1) * m + j) for k, j in turns])
+    edge_near = over(edge_near, 0)
     levels = call(
         place_kernel,
         [late, sums] + tables,
         [pltpu.VMEM(s, F32) for s in shapes],
-        [pltpu.VMEM((2, 2 * TS, plan.rows), BF)]
+        [
+            pltpu.VMEM(prod_shape, BF),
+            pltpu.VMEM(sums_shape.shape, F32),
+            pltpu.VMEM((2, 2 * TS, plan.rows), BF),
+        ]
         + [pltpu.VMEM((planes, s, plan.rows), F32) for s in size[1:]],
         flops=4 * work,
     )
-    grow3 = np.zeros((wide_top, plan.rows >> 2))
-    grow3[:top] = grow_grid(top).T
-    grow2 = grow_grid(plan.rows >> 2).T
-    grow1 = grow_grid(plan.rows >> 1).T[:, plan.row_of]
-    natural = np.eye(plan.rows)[plan.row_of]
     out = call(
         blend_kernel,
-        [*levels, edge_near, edge_far]
-        + [jnp.asarray(table.astype(BF)) for table in (grow1, grow2, grow3, natural)],
+        [*levels, edge_near, edge_far, *grows],
         jax.ShapeDtypeStruct((bands, size[0], plan.rows), BF),
         [
             pltpu.VMEM(shapes[1], F32),
@@ -662,7 +689,7 @@
             pltpu.VMEM(shapes[3], F32),
             pltpu.VMEM((2 * bands, (plan.rows >> 2) // TS, size[2], TS), F32),
             pltpu.VMEM((2 * bands, (plan.rows >> 1) // TS, size[1], TS), F32),
-            pltpu.VMEM((2 * bands, plan.rows // TS, size[0], TS), F32),
+            pltpu.VMEM((2 * bands, (plan.rows >> 1) // TS, size[0], TS), F32),
             pltpu.VMEM((bands, size[0], plan.rows), BF),
             pltpu.SemaphoreType.DMA((2,)),
         ],

time: 28.7 us -> 28.8 us (level)
  Pallas kernels: 6.87 us -> 8.1 us
  local copies, waits for them, and re-layouts: 0.87 us -> 0 us
    pallas_call x0 -> x1, Pallas kernels: none -> 1.49 us  [strip_local(): pl.pallas_call(functools.partial(load_kernel, plan), out_shape=[pltpu.VME...]
    squeeze x1 -> x0, local copies, waits for them, and re-layouts: 0.83 us -> none  [strip_local(): lax.dynamic_index_in_dim(jnp.asarray(plan.column_tables()), row_tile * m...]
  transfers between devices with their start and end apart: 5 -> 5, of which waited for: 2 -> 3; matrix products, arithmetic and copies ran while one was open for 3% -> 0% of each run, Pallas kernels for 14% -> 18%
where the time goes in v5:
time: 28.8 us; the launch traced here: 28.6 us
  starting transfers between devices  11.5 us (40%)
  waiting for transfers between devices  8.32 us (29%)
  Pallas kernels  8.1 us (28%)
  between operations  0.69 us (2%)
    ppermute x1, waiting for transfers between devices, strip_local(): far = lax.ppermute(pack, 'tx', across)  6.57 us
    pallas_call x4, Pallas kernels, call(): pl.pallas_call(functools.partial(kernel, plan), out_shape=outputs, in_spe...  5.5 us
    ppermute x1, starting transfers between devices, strip_local(): far = lax.ppermute(pack, 'tx', across)  5.14 us
    ppermute x1, starting transfers between devices, strip_local(): late = lax.ppermute(far, 'tx', beside)  3.75 us
    ppermute x2, starting transfers between devices, over(): return lax.ppermute(value, ('tx', 'ty'), pairs)  2.61 us
    ppermute x2, waiting for transfers between devices, over(): return lax.ppermute(value, ('tx', 'ty'), pairs)  1.74 us
    pallas_call x1, Pallas kernels, strip_local(): pl.pallas_call(functools.partial(load_kernel, plan), out_shape=[pltpu.VME...  1.49 us
    pallas_call x1, Pallas kernels, strip_local(): pl.pallas_call(functools.partial(pack_kernel, plan), out_shape=pltpu.VMEM...  1.12 us
  transfers between devices with their start and end apart: 5, of which 3 were waited for; matrix products, arithmetic and copies ran while one was open for 0% of the time, Pallas kernels for 18%

profile of v5, /device:TPU:0, one launch (start us, length us, event | category | flops | bytes accessed | tf_op | source)
XLA Modules:
  0.0 28.6 jit_solution(8986404108978738196)
XLA Ops:
  0.7 1.1 %pack.1 = bf16[904,128]{1,0:T(8,128)(2,1)S(1)} custom-call(s32[1,1]{1,0:T(1,128)S(6)} %copy.15.count_ref, bf16[6,64,256]{2,1,0:T(8,128)(2,1)} %bitcast.7, bf16[64,256]{1,0:T(8,128)(2,1)} %bitcast.8, s32[1,64]{1,0:T(1,128)} %dest_ref.1, s32[1,64]{1,0:T(1,128)} %offset_ref.1), custom_call_target="tpu_custom_call" | custom-call | tf_op jit(solution)/shard_map/pack/pallas_call | solution.py:571
  1.8 5.1 %collective-permute-start = (bf16[904,128]{1,0:T(8,128)(2,1)S(1)}, bf16[904,128]{1,0:T(8,128)(2,1)S(1)}, u32[]{:S(2)}, u32[]{:S(2)}) collective-permute-start(bf16[904,128]{1,0:T(8,128)(2,1)S(1)} %pack.1), channel_id=1, source_target_pairs={{0,12},{4,8},{8,4},{12,0},{1,13},{5,9},{9,5},{13,1},{2,14},{6,10},... | collective-permute-start | bytes 694280 | tf_op jit(solution)/shard_map/ppermute | solution.py:636
  6.9 0.0 collective-permute-start.2
  6.9 6.6 %collective-permute-done.far = bf16[904,128]{1,0:T(8,128)(2,1)S(1)} collective-permute-done((bf16[904,128]{1,0:T(8,128)(2,1)S(1)}, bf16[904,128]{1,0:T(8,128)(2,1)S(1)}, u32[]{:S(2)}, u32[]{:S(2)}) %collective-permute-start) | collective-permute-done | bytes 231456 | tf_op jit(solution)/shard_map/ppermute | solution.py:636
  13.5 3.7 %collective-permute-start.1 = (bf16[904,128]{1,0:T(8,128)(2,1)S(1)}, bf16[904,128]{1,0:T(8,128)(2,1)S(1)}, u32[]{:S(2)}, u32[]{:S(2)}) collective-permute-start(bf16[904,128]{1,0:T(8,128)(2,1)S(1)} %collective-permute-done.far), channel_id=1, source_target_pairs={{0,4},{4,0},{8,12},{12,8},{1,5},{5,1},{9,13},{13,9},{2,6},{6,2},{1... | collective-permute-start | bytes 694280 | tf_op jit(solution)/shard_map/ppermute | solution.py:661
  17.2 1.5 %load.1 = (bf16[136,256]{1,0:T(8,128)(2,1)S(1)}, bf16[512,256]{1,0:T(8,128)(2,1)S(1)}, bf16[512,128]{1,0:T(8,128)(2,1)S(1)}, bf16[2,512,128]{2,1,0:T(8,128)(2,1)...) custom-call(bf16[8,136,256]{2,1,0:T(8,128)(2,1)} %constant.16.clone., ...), custom_call_target="tpu_custom_call" | custom-call | tf_op jit(solution)/shard_map/load/pallas_call | solution.py:612
  18.7 1.0 %shard_map.127 = (f32[896,512]{1,0:T(8,128)S(1)}, bf16[24,512]{1,0:T(8,128)(2,1)S(1)}) custom-call(bf16[904,128]{1,0:T(8,128)(2,1)S(1)} %pack.1, bf16[136,256]{1,0:T(8,128)(2,1)S(1)} %get-tuple-element.21.column_ref, bf16[512,256]{1,0:T(8,128)(2,1)S(1)} %get-tuple-element.22.row1_ref, bf16[512,128]{1,0:T(8,128)(2,1)S(1)} %get-tuple-element.23.row2_ref, ...), custom_call_target="tpu_custom_call" | custom-call | flops 117440512 | bytes 1048576 | tf_op jit(solution)/shard_map/pallas_call | solution.py:587
  19.7 2.0 %collective-permute-start.4 = (bf16[24,512]{1,0:T(8,128)(2,1)S(1)}, bf16[24,512]{1,0:T(8,128)(2,1)S(1)}, u32[]{:S(2)}, u32[]{:S(2)}) collective-permute-start(bf16[24,512]{1,0:T(8,128)(2,1)S(1)} %get-tuple-element.32), channel_id=1, source_target_pairs={{0,10},{2,8},{4,14},{6,12},{8,2},{10,0},{12,6},{14,4},{1,11},{3,9}... | collective-permute-start | bytes 73736 | tf_op jit(solution)/shard_map/ppermute | solution.py:658
  21.7 0.0 collective-permute-done.2.near
  21.7 1.2 %shard_map.128 = (f32[896,512]{1,0:T(8,128)S(1)}, bf16[24,512]{1,0:T(8,128)(2,1)S(1)}) custom-call(bf16[904,128]{1,0:T(8,128)(2,1)S(1)} %collective-permute-done.far, bf16[904,128]{1,0:T(8,128)(2,1)S(1)} %collective-permute-done.2.near, f32[896,512]{1,0:T(8,128)S(1)} %get-tuple-element.25.before_ref, bf16[136,256]{1,0:T(8,128)(2,1)S(1)} %get-tuple-element.21.column_ref, ...), custom_call_target="tpu_custom_call" | custom-call | flops 469762048 | bytes 1048576 | tf_op jit(solution)/shard_map/pallas_call | solution.py:587
  23.0 0.6 %collective-permute-start.3 = (bf16[24,512]{1,0:T(8,128)(2,1)S(1)}, bf16[24,512]{1,0:T(8,128)(2,1)S(1)}, u32[]{:S(2)}, u32[]{:S(2)}) collective-permute-start(bf16[24,512]{1,0:T(8,128)(2,1)S(1)} %get-tuple-element.31), channel_id=1, source_target_pairs={{0,2},{2,0},{4,6},{6,4},{8,10},{10,8},{12,14},{14,12},{1,3},{3,1},... | collective-permute-start | bytes 73736 | tf_op jit(solution)/shard_map/ppermute | solution.py:658
  23.6 0.0 collective-permute-done.1.pack
  23.6 1.5 %shard_map.129 = (f32[7,32,512]{2,1,0:T(8,128)S(1)}, f32[7,24,256]{2,1,0:T(8,128)S(1)}, f32[7,16,128]{2,1,0:T(8,128)S(1)}, f32[7,8,128]{2,1,0:T(8,128)S(1)}) custom-call(bf16[904,128]{1,0:T(8,128)(2,1)S(1)} %collective-permute-done.1.pack, f32[896,512]{1,0:T(8,128)S(1)} %get-tuple-element.26.before_ref, bf16[136,256]{1,0:T(8,128)(2,1)S(1)} %get-tuple-element.21.column_ref, ...), custom_call_target="tpu_custom_call" | custom-call | flops 469762048 | bytes 1048576 | tf_op jit(solution)/shard_map/pallas_call | solution.py:587
  25.1 0.3 %collective-permute-done.4.far_ref = bf16[24,512]{1,0:T(8,128)(2,1)S(1)} collective-permute-done((bf16[24,512]{1,0:T(8,128)(2,1)S(1)}, bf16[24,512]{1,0:T(8,128)(2,1)S(1)}, u32[]{:S(2)}, u32[]{:S(2)}) %collective-permute-start.4) | collective-permute-done | bytes 24608 | tf_op jit(solution)/shard_map/ppermute | solution.py:658
  25.4 1.4 %collective-permute-done.3.near_ref = bf16[24,512]{1,0:T(8,128)(2,1)S(1)} collective-permute-done((bf16[24,512]{1,0:T(8,128)(2,1)S(1)}, bf16[24,512]{1,0:T(8,128)(2,1)S(1)}, u32[]{:S(2)}, u32[]{:S(2)}) %collective-permute-start.3) | collective-permute-done | bytes 24608 | tf_op jit(solution)/shard_map/ppermute | solution.py:658
  26.9 1.8 %shard_map.130 = bf16[6,32,512]{2,1,0:T(8,128)(2,1)} custom-call(f32[7,32,512]{2,1,0:T(8,128)S(1)} %get-tuple-element.27.a0_ref, f32[7,24,256]{2,1,0:T(8,128)S(1)} %get-tuple-element.28.a1_ref, f32[7,16,128]{2,1,0:T(8,128)S(1)} %get-tuple-element.29.a2_ref, f32[7,8,128]{2,1,0:T(8,128)S(1)} %get-tuple-element.30.a3_ref, ...), custom_call_target="tpu_custom_call" | custom-call | flops 469762048 | bytes 1048576 | tf_op jit(solution)/shard_map/pallas_call | solution.py:587
Async XLA Ops:
  1.8 11.7 %collective-permute-start = (bf16[904,128]{1,0:T(8,128)(2,1)S(1)}, bf16[904,128]{1,0:T(8,128)(2,1)S(1)}, u32[]{:S(2)}, u32[]{:S(2)}) collective-permute-start(bf16[904,128]{1,0:T(8,128)(2,1)S(1)} %pack.1), channel_id=1, source_target_pairs={{0,12},{4,8},{8,4},{12,0},{1,13},{5,9},{9,5},{13,1},{2,14},{6,10},... | collective-permute-start | bytes 694280 | tf_op jit(solution)/shard_map/ppermute | solution.py:636
  6.9 14.8 %collective-permute-start.2 = (bf16[904,128]{1,0:T(8,128)(2,1)S(1)}, bf16[904,128]{1,0:T(8,128)(2,1)S(1)}, u32[]{:S(2)}, u32[]{:S(2)}) collective-permute-start(bf16[904,128]{1,0:T(8,128)(2,1)S(1)} %pack.1), channel_id=1, source_target_pairs={{0,4},{4,0},{8,12},{12,8},{1,5},{5,1},{9,13},{13,9},{2,6},{6,2},{1... | collective-permute-start | bytes 694280 | tf_op jit(solution)/shard_map/ppermute | solution.py:637
  13.5 10.1 %collective-permute-start.1 = (bf16[904,128]{1,0:T(8,128)(2,1)S(1)}, bf16[904,128]{1,0:T(8,128)(2,1)S(1)}, u32[]{:S(2)}, u32[]{:S(2)}) collective-permute-start(bf16[904,128]{1,0:T(8,128)(2,1)S(1)} %collective-permute-done.far), channel_id=1, source_target_pairs={{0,4},{4,0},{8,12},{12,8},{1,5},{5,1},{9,13},{13,9},{2,6},{6,2},{1... | collective-permute-start | bytes 694280 | tf_op jit(solution)/shard_map/ppermute | solution.py:661
  19.7 5.7 %collective-permute-start.4 = (bf16[24,512]{1,0:T(8,128)(2,1)S(1)}, bf16[24,512]{1,0:T(8,128)(2,1)S(1)}, u32[]{:S(2)}, u32[]{:S(2)}) collective-permute-start(bf16[24,512]{1,0:T(8,128)(2,1)S(1)} %get-tuple-element.32), channel_id=1, source_target_pairs={{0,10},{2,8},{4,14},{6,12},{8,2},{10,0},{12,6},{14,4},{1,11},{3,9}... | collective-permute-start | bytes 73736 | tf_op jit(solution)/shard_map/ppermute | solution.py:658
  23.0 3.9 %collective-permute-start.3 = (bf16[24,512]{1,0:T(8,128)(2,1)S(1)}, bf16[24,512]{1,0:T(8,128)(2,1)S(1)}, u32[]{:S(2)}, u32[]{:S(2)}) collective-permute-start(bf16[24,512]{1,0:T(8,128)(2,1)S(1)} %get-tuple-element.31), channel_id=1, source_target_pairs={{0,2},{2,0},{4,6},{6,4},{8,10},{10,8},{12,14},{14,12},{1,3},{3,1},... | collective-permute-start | bytes 73736 | tf_op jit(solution)/shard_map/ppermute | solution.py:658

commit v6 on v5

--- a/solution.py
+++ b/solution.py
@@ -292,8 +292,12 @@
     )
 
 
-def pack_kernel(plan, count_ref, scenes_ref, cloud_ref, dest_ref, offset_ref, out_ref, raw, dest,
-                offset, sems):
+def turned(plan, block):
+    return jnp.concatenate([block[:, : plan.half], block[:, plan.half :]], axis=0).T
+
+
+def pack_kernel(plan, count_ref, scenes_ref, cloud_ref, dest_ref, offset_ref, out_ref, note_ref, raw,
+                dest, offset, sems):
     rows = 2 * S_DEV
     half = plan.half
     copies = [
@@ -323,9 +327,8 @@
             copies[2].wait()
         elif f == 0:
             copies[3].wait()
-        block = raw[f]
-        block = jnp.concatenate([block[:, :half], block[:, half:]], axis=0)
-        out_ref[f * half : (f + 1) * half, :] = block.T
+        out_ref[f * half : (f + 1) * half, :] = turned(plan, raw[f])
+    note_ref[...] = out_ref[plan.weight_at :, :]
 
 
 def load_kernel(plan, column_ref, *refs):
@@ -342,8 +345,8 @@
         copy.wait()
 
 
-def landing_of(plan, pack):
-    codes = pack[plan.code_at : plan.code_at + CODE_ROWS, :].astype(F32).T[:, :1]
+def landing_of(plan, codes):
+    codes = codes.astype(F32).T[:, :1]
     blocks = codes.shape[0]
     pair = float(2 * plan.slot_rows)
     second = lax.broadcasted_iota(jnp.int32, (blocks, 1), 0) >= S_DEV
@@ -353,18 +356,22 @@
     return jnp.concatenate([landing, landing], axis=0)
 
 
-def slot_sums(plan, pack, prod_ref):
-    weight = pack[plan.weight_at : plan.code_at, :]
+def slot_sums(plan, scenes, note, prod_ref):
     half, blocks = plan.half, 2 * S_DEV
+    weight = note[:half, :]
     for f in range(plan.bands):
         rows = pl.ds(f * half, half)
-        high, low = halves(pack[f * half : (f + 1) * half, :].astype(F32) * weight.astype(F32))
+        if len(scenes.shape) == 3:
+            value = turned(plan, scenes[f])
+        else:
+            value = scenes[f * half : (f + 1) * half, :]
+        high, low = halves(value.astype(F32) * weight.astype(F32))
         prod_ref[rows, :blocks] = high
         prod_ref[rows, blocks:] = low
     rows = pl.ds(plan.weight_at, half)
     prod_ref[rows, :blocks] = weight
     prod_ref[rows, blocks:] = jnp.zeros_like(weight)
-    return jnp.dot(prod_ref[...], landing_of(plan, pack), preferred_element_type=F32)
+    return jnp.dot(prod_ref[...], landing_of(plan, note[half:, :]), preferred_element_type=F32)
 
 
 def turn(plan, a, b):
@@ -373,7 +380,11 @@
     return jnp.where(odd, pltpu.roll(b, wide, 1), a), jnp.where(odd, b, pltpu.roll(a, TS - wide, 1))
 
 
-def edge_of(plan, side_ref, table, row_refs, out_ref, tile_ref, z_ref):
+def twin_sum(value):
+    return value + pltpu.roll(value, value.shape[-1] // 2, value.ndim - 1)
+
+
+def edge_of(plan, side_ref, table, row1_ref, row23_ref, out_ref, tile_ref, z1_ref, z23_ref):
     planes = plan.bands + 1
     rows = plan.rows
     for f in range(planes):
@@ -384,43 +395,46 @@
             for k, value in enumerate(pair):
                 tile[k * BS : (k + 1) * BS, u * TS : (u + 1) * TS] = value.astype(BF)
         cols = jnp.dot(table, tile[...], preferred_element_type=F32)
-        for level in range(LEVELS - 1):
-            z_ref[level, f] = cols[8 * level : 8 * level + 8]
-    start = 0
+        z1_ref[f] = cols[:8]
+        z23_ref[f] = cols[8:]
     out_ref[...] = jnp.zeros(out_ref.shape, out_ref.dtype)
-    for level, ref in enumerate(row_refs):
-        row_table = ref[...] if len(ref.shape) == 2 else ref[0]
-        lanes = row_table.shape[1]
-        z = z_ref[level].reshape(planes * 8, rows).astype(BF)
-        z = jnp.dot(z, row_table, preferred_element_type=F32).reshape(planes, 8, lanes)
-        for f in range(planes):
-            out_ref[pl.ds(EDGE * f, EDGE), start : start + lanes] = z[f, :EDGE].astype(BF)
-        start += lanes
+    z1 = z1_ref[...].reshape(planes * 8, rows).astype(BF)
+    z1 = jnp.dot(z1, row1_ref[...], preferred_element_type=F32).reshape(planes, 8, rows // 2)
+    z23 = z23_ref[...].reshape(planes * 16, rows).astype(BF)
+    z23 = jnp.dot(z23, row23_ref[...], preferred_element_type=F32).reshape(planes, 16, rows // 2)
+    second = rows // 2 + rows // 4
+    for f in range(planes):
+        at = pl.ds(EDGE * f, EDGE)
+        out_ref[at, : rows // 2] = z1[f, :EDGE].astype(BF)
+        out_ref[at, rows // 2 : second] = z23[f, :EDGE, : rows // 4].astype(BF)
+        top = twin_sum(z23[f, 8:, rows // 4 :])
+        out_ref[at, second:] = top[:EDGE].astype(BF)
 
 
 def side_of(plan, sums, right):
     return jnp.where(right, sums[:, 2 * plan.slots - TS :], sums[:, :TS])
 
 
-def own_kernel(plan, pack, column_ref, row1_ref, row2_ref, row3_ref,
-               out_ref, edge_ref, prod_ref, side_ref, tile_ref, z_ref):
+def own_kernel(plan, pack, column_ref, row1_ref, row23_ref,
+               out_ref, edge_ref, prod_ref, side_ref, tile_ref, z1_ref, z23_ref):
     right = 2 * (lax.axis_index("tx") ^ plan.n // 2) < plan.n
-    sums = slot_sums(plan, pack, prod_ref)
+    sums = slot_sums(plan, pack, pack.at[pl.ds(plan.weight_at, plan.half + CODE_ROWS)], prod_ref)
     out_ref[...] = sums
     side_ref[...] = side_of(plan, sums, right)
     table = column_ref[plan.main + plan.edge_rows :, : plan.near]
-    edge_of(plan, side_ref, table, (row1_ref, row2_ref, row3_ref), edge_ref, tile_ref, z_ref)
-
-
-def first_kernel(plan, far, near, before_ref, column_ref, row1_ref, row2_ref, row3_ref,
-                 out_ref, edge_ref, prod_ref, side_ref, tile_ref, z_ref):
+    edge_of(plan, side_ref, table, row1_ref, row23_ref, edge_ref, tile_ref, z1_ref, z23_ref)
+
+
+def first_kernel(plan, far, note, near, before_ref, column_ref, row1_ref, row23_ref,
+                 out_ref, edge_ref, prod_ref, side_ref, tile_ref, z1_ref, z23_ref):
     right = 2 * lax.axis_index("tx") < plan.n
-    one = slot_sums(plan, far, prod_ref.at[0])
-    sums = before_ref[...] + one + slot_sums(plan, near, prod_ref.at[1])
+    near_note = near.at[pl.ds(plan.weight_at, plan.half + CODE_ROWS)]
+    sums = slot_sums(plan, near, near_note, prod_ref.at[0])
+    sums = before_ref[...] + sums + slot_sums(plan, far, note, prod_ref.at[1])
     out_ref[...] = sums
     side_ref[...] = side_of(plan, sums, right)
     table = column_ref[plan.main : plan.main + plan.edge_rows, : plan.near]
-    edge_of(plan, side_ref, table, (row1_ref, row2_ref, row3_ref), edge_ref, tile_ref, z_ref)
+    edge_of(plan, side_ref, table, row1_ref, row23_ref, edge_ref, tile_ref, z1_ref, z23_ref)
 
 
 def tile_of(plan, sums, at, tile_ref):
@@ -436,30 +450,28 @@
                 tile_ref[TS + row : TS + row + BS, u * TS : (u + 1) * TS] = low
 
 
-def place_kernel(plan, pack, before_ref, column_ref, row1_ref, row2_ref, row3_ref,
-                 a0_ref, a1_ref, a2_ref, a3_ref, prod_ref, sums_ref, tile_ref, z1_ref, z2_ref, z3_ref):
+def place_kernel(plan, late, note, before_ref, column_ref, row1_ref, row23_ref,
+                 a0_ref, a1_ref, a2_ref, a3_ref, prod_ref, sums_ref, tile_ref, z1_ref, z23_ref):
     column = column_ref[: plan.main, :]
     at, size = plan.at, plan.size
     planes = plan.bands + 1
     rows = plan.rows
-    sums_ref[...] = before_ref[...] + slot_sums(plan, pack, prod_ref)
+    sums_ref[...] = before_ref[...] + slot_sums(plan, late, note, prod_ref)
     for f in range(planes):
         tile = tile_ref.at[f % 2]
         tile_of(plan, sums_ref, f * plan.half, tile)
         cols = jnp.dot(column, tile[...], preferred_element_type=F32)
         a0_ref[f] = cols[at[0] : at[1]]
         z1_ref[f] = cols[at[1] : at[2]]
-        z2_ref[f] = cols[at[2] : at[3]]
-        z3_ref[f] = cols[at[3] : at[4]] + cols[plan.low_at : plan.main]
+        z23_ref[f, : size[2]] = cols[at[2] : at[3]]
+        z23_ref[f, size[2] :] = cols[at[3] : at[4]] + cols[plan.low_at : plan.main]
     z1 = dot2(z1_ref[...].reshape(planes * size[1], rows), row1_ref[...])
-    z2 = dot2(z2_ref[...].reshape(planes * size[2], rows), row2_ref[...])
-    z3 = z3_ref[...].reshape(planes * size[3], rows)
-    z3 = dot2(z3, row3_ref[0]) + jnp.dot(
-        z3.astype(BF), row3_ref[1], preferred_element_type=F32
-    )
     a1_ref[...] = z1.reshape(a1_ref.shape)
-    a2_ref[...] = z2.reshape(a2_ref.shape)
-    a3_ref[...] = z3.reshape(a3_ref.shape)
+    z23 = dot2(z23_ref[...].reshape(planes * (size[2] + size[3]), rows), row23_ref[...])
+    z23 = z23.reshape(planes, size[2] + size[3], rows // 2)
+    a2_ref[...] = z23[:, : size[2], : rows // 4]
+    for f in range(planes):
+        a3_ref[f] = twin_sum(z23[f, size[2] :, rows // 4 :])
 
 
 def grow_columns(value, outputs):
@@ -568,20 +580,6 @@
     smem = pl.BlockSpec(memory_space=pltpu.SMEM)
     hbm = pl.BlockSpec(memory_space=pl.ANY)
     blocks = jnp.swapaxes(scenes[0], 0, 1)
-    pack = pl.pallas_call(
-        functools.partial(pack_kernel, plan),
-        out_shape=pltpu.VMEM((plan.code_at + CODE_ROWS, 2 * S_DEV), BF),
-        in_specs=[smem] + [hbm] * 4,
-        out_specs=vmem,
-        scratch_shapes=[
-            pltpu.VMEM((planes, S_DEV, area), BF),
-            pltpu.VMEM(destination.shape, jnp.int32),
-            pltpu.VMEM(offset.shape, jnp.int32),
-            pltpu.SemaphoreType.DMA((4,)),
-        ],
-        compiler_params=pltpu.CompilerParams(vmem_limit_bytes=4 << 20),
-        name="pack",
-    )(counts, *[off_chip(v) for v in (blocks, cloud[0], destination, offset)])
 
     def call(kernel, operands, outputs, scratch=(), flops=0, out_specs=None):
         return pl.pallas_call(
@@ -598,16 +596,14 @@
     row1 = shrinks[0].T[plan.row_of]
     row2 = shrinks[1].T[plan.row_of]
     top = plan.rows >> 3
-    wide_top = max(top, 128)
-    padded = np.zeros((plan.rows, wide_top))
-    padded[:, :top] = shrinks[2].T[plan.row_of]
-    row3 = np.stack(split_table(padded))
+    wide_top = 2 * top
+    row23 = np.concatenate([row2, *split_table(shrinks[2].T[plan.row_of])], axis=1)
     grow3 = np.zeros((wide_top, plan.rows >> 2))
     grow3[:top] = grow_grid(top).T
     grow2 = grow_grid(plan.rows >> 2).T
     grow1 = grow_grid(plan.rows >> 1).T[:, plan.row_of]
     natural = np.eye(plan.rows)[plan.row_of]
-    constants = [plan.column_tables(), row1, row2, row3, grow1, grow2, grow3, natural]
+    constants = [plan.column_tables(), row1, row23, grow1, grow2, grow3, natural]
     constants = [off_chip(jnp.asarray(table.astype(BF))) for table in constants]
     loaded = pl.pallas_call(
         functools.partial(load_kernel, plan),
@@ -618,7 +614,7 @@
         compiler_params=pltpu.CompilerParams(vmem_limit_bytes=4 << 20),
         name="load",
     )(*constants)
-    tables, grows = list(loaded[:4]), list(loaded[4:])
+    tables, grows = list(loaded[:3]), list(loaded[3:])
     size = plan.size
     shapes = [
         (planes, size[0], plan.rows),
@@ -633,12 +629,32 @@
 
     across = [(i, n - 1 - i) for i in range(n)]
     beside = [(i, i ^ 1) for i in range(n)]
-    far = lax.ppermute(pack, "tx", across)
+    far = lax.ppermute(blocks, "tx", across)
+    pack, note = pl.pallas_call(
+        functools.partial(pack_kernel, plan),
+        out_shape=[
+            pltpu.VMEM((plan.code_at + CODE_ROWS, 2 * S_DEV), BF),
+            pltpu.VMEM((plan.half + CODE_ROWS, 2 * S_DEV), BF),
+        ],
+        in_specs=[smem] + [hbm] * 4,
+        out_specs=[vmem] * 2,
+        scratch_shapes=[
+            pltpu.VMEM((planes, S_DEV, area), BF),
+            pltpu.VMEM(destination.shape, jnp.int32),
+            pltpu.VMEM(offset.shape, jnp.int32),
+            pltpu.SemaphoreType.DMA((4,)),
+        ],
+        compiler_params=pltpu.CompilerParams(vmem_limit_bytes=4 << 20),
+        name="pack",
+    )(counts, *[off_chip(v) for v in (blocks, cloud[0], destination, offset)])
+
+    far_note = lax.ppermute(note, "tx", across)
     near = lax.ppermute(pack, "tx", beside)
     edge_work = [
         pltpu.VMEM((planes * plan.half, TS), F32),
         pltpu.VMEM((2, plan.near, plan.rows), BF),
-        pltpu.VMEM((LEVELS - 1, planes, 8, plan.rows), F32),
+        pltpu.VMEM((planes, 8, plan.rows), F32),
+        pltpu.VMEM((planes, 16, plan.rows), F32),
     ]
     sums_and_edge = [sums_shape, pltpu.VMEM(edge_shape, BF)]
     sums, edge_far = call(
@@ -659,9 +675,10 @@
 
     edge_far = over(edge_far, n // 2)
     late = lax.ppermute(far, "tx", beside)
+    late_note = lax.ppermute(far_note, "tx", beside)
     sums, edge_near = call(
         first_kernel,
-        [far, near, sums] + tables,
+        [far, far_note, near, sums] + tables,
         sums_and_edge,
         [pltpu.VMEM((2, *prod_shape), BF)] + edge_work,
         flops=4 * work,
@@ -669,14 +686,15 @@
     edge_near = over(edge_near, 0)
     levels = call(
         place_kernel,
-        [late, sums] + tables,
+        [late, late_note, sums] + tables,
         [pltpu.VMEM(s, F32) for s in shapes],
         [
             pltpu.VMEM(prod_shape, BF),
             pltpu.VMEM(sums_shape.shape, F32),
             pltpu.VMEM((2, 2 * TS, plan.rows), BF),
-        ]
-        + [pltpu.VMEM((planes, s, plan.rows), F32) for s in size[1:]],
+            pltpu.VMEM((planes, size[1], plan.rows), F32),
+            pltpu.VMEM((planes, size[2] + size[3], plan.rows), F32),
+        ],
         flops=4 * work,
     )
     out = call(

time: 28.8 us -> 29.1 us (1.010)
  starting transfers between devices: 11.5 us -> 12.3 us
  waiting for transfers between devices: 8.32 us -> 7.77 us
    ppermute x1 -> x3, starting transfers between devices: 5.14 us -> 8.18 us  [the longest x1 5.08 us: strip_local(): far = lax.ppermute(blocks, 'tx', across)]
    ppermute x2, starting transfers between devices: 2.61 us -> 1.04 us  [over(): return lax.ppermute(value, ('tx', 'ty'), pairs)]
    ppermute x2, waiting for transfers between devices: 1.74 us -> 0.4 us  [over(): return lax.ppermute(value, ('tx', 'ty'), pairs)]
    ppermute x1 -> x3, waiting for transfers between devices: 6.57 us -> 7.36 us  [the longest x1 4.15 us: strip_local(): far = lax.ppermute(blocks, 'tx', across)]
    ppermute x1, starting transfers between devices: 3.75 us -> 3.03 us  [strip_local(): late = lax.ppermute(far, 'tx', beside)]
  transfers between devices with their start and end apart: 5 -> 7, of which waited for: 3 -> 4; matrix products, arithmetic and copies ran while one was open for 0% -> 0% of each run, Pallas kernels for 18% -> 22%
where the time goes in v6:
time: 29.1 us; the launch traced here: 28.9 us
  starting transfers between devices  12.3 us (42%)
  Pallas kernels  8.15 us (28%)
  waiting for transfers between devices  7.77 us (27%)
  between operations  0.7 us (2%)
    pallas_call x4, Pallas kernels, call(): pl.pallas_call(functools.partial(kernel, plan), out_shape=outputs, in_spe...  5.61 us
    ppermute x1, starting transfers between devices, strip_local(): far = lax.ppermute(blocks, 'tx', across)  5.08 us
    ppermute x1, waiting for transfers between devices, strip_local(): far = lax.ppermute(blocks, 'tx', across)  4.15 us
    ppermute x1, starting transfers between devices, strip_local(): late = lax.ppermute(far, 'tx', beside)  3.03 us
    ppermute x1, starting transfers between devices, strip_local(): far_note = lax.ppermute(note, 'tx', across)  2.47 us
    ppermute x1, waiting for transfers between devices, strip_local(): far_note = lax.ppermute(note, 'tx', across)  2.2 us
    pallas_call x1, Pallas kernels, strip_local(): pl.pallas_call(functools.partial(load_kernel, plan), out_shape=[pltpu.VME...  1.41 us
    pallas_call x1, Pallas kernels, strip_local(): pl.pallas_call(functools.partial(pack_kernel, plan), out_shape=[pltpu.VME...  1.12 us
  transfers between devices with their start and end apart: 7, of which 4 were waited for; matrix products, arithmetic and copies ran while one was open for 0% of the time, Pallas kernels for 22%

profile of v6, /device:TPU:0, one launch (start us, length us, event | category | flops | bytes accessed | tf_op | source)
XLA Modules:
  0.0 28.9 jit_solution(18076154070307062728)
XLA Ops:
  0.0 5.1 %collective-permute-start = (bf16[6,64,256]{2,1,0:T(8,128)(2,1)}, bf16[6,64,256]{2,1,0:T(8,128)(2,1)S(1)}, u32[]{:S(2)}, u32[]{:S(2)}) collective-permute-start(bf16[6,64,256]{2,1,0:T(8,128)(2,1)} %bitcast.7), channel_id=1, source_target_pairs={{0,12},{4,8},{8,4},{12,0},{1,13},{5,9},{9,5},{13,1},{2,14},{6,10},... | collective-permute-start | bytes 589832 | tf_op jit(solution)/shard_map/ppermute | solution.py:632
  5.7 1.1 %pack.1 = (bf16[904,128]{1,0:T(8,128)(2,1)S(1)}, bf16[136,128]{1,0:T(8,128)(2,1)S(1)}) custom-call(s32[1,1]{1,0:T(1,128)S(6)} %copy.14.count_ref, bf16[6,64,256]{2,1,0:T(8,128)(2,1)} %bitcast.8, bf16[64,256]{1,0:T(8,128)(2,1)} %bitcast.9, s32[1,64]{1,0:T(1,128)} %dest_ref.1, s32[1,64]{1,0:T(1,128)} %offset_ref.1), custom_call_target="tpu_custom_call" | custom-call | tf_op jit(solution)/shard_map/pack/pallas_call | solution.py:633
  6.9 0.1 collective-permute-start.4
  6.9 4.1 %collective-permute-done.far = bf16[6,64,256]{2,1,0:T(8,128)(2,1)S(1)} collective-permute-done((bf16[6,64,256]{2,1,0:T(8,128)(2,1)}, bf16[6,64,256]{2,1,0:T(8,128)(2,1)S(1)}, u32[]{:S(2)}, u32[]{:S(2)}) %collective-permute-start) | collective-permute-done | bytes 196640 | tf_op jit(solution)/shard_map/ppermute | solution.py:632
  11.1 3.0 %collective-permute-start.1 = (bf16[6,64,256]{2,1,0:T(8,128)(2,1)S(1)}, bf16[6,64,256]{2,1,0:T(8,128)(2,1)S(1)}, u32[]{:S(2)}, u32[]{:S(2)}) collective-permute-start(bf16[6,64,256]{2,1,0:T(8,128)(2,1)S(1)} %collective-permute-done.far), channel_id=1, source_target_pairs={{0,4},{4,0},{8,12},{12,8},{1,5},{5,1},{9,13},{13,9},{2,6},{6,2},{1... | collective-permute-start | bytes 589832 | tf_op jit(solution)/shard_map/ppermute | solution.py:677
  14.1 2.5 %collective-permute-start.2 = (bf16[136,128]{1,0:T(8,128)(2,1)S(1)}, bf16[136,128]{1,0:T(8,128)(2,1)S(1)}, u32[]{:S(2)}, u32[]{:S(2)}) collective-permute-start(bf16[136,128]{1,0:T(8,128)(2,1)S(1)} %get-tuple-element.22), channel_id=1, source_target_pairs={{0,12},{4,8},{8,4},{12,0},{1,13},{5,9},{9,5},{13,1},{2,14},{6,10},... | collective-permute-start | bytes 104456 | tf_op jit(solution)/shard_map/ppermute | solution.py:651
  16.6 1.4 %load.1 = (bf16[136,256]{1,0:T(8,128)(2,1)S(1)}, bf16[512,256]{1,0:T(8,128)(2,1)S(1)}, bf16[512,256]{1,0:T(8,128)(2,1)S(1)}, bf16[256,512]{1,0:T(8,128)(2,1)S(1)...) custom-call(bf16[8,136,256]{2,1,0:T(8,128)(2,1)} %constant.14.clone.column_ref, ...), custom_call_target="tpu_custom_call" | custom-call | tf_op jit(solution)/shard_map/load/pallas_call | solution.py:608
  18.0 1.1 %shard_map.118 = (f32[896,512]{1,0:T(8,128)S(1)}, bf16[24,512]{1,0:T(8,128)(2,1)S(1)}) custom-call(bf16[904,128]{1,0:T(8,128)(2,1)S(1)} %get-tuple-element.23.pack, bf16[136,256]{1,0:T(8,128)(2,1)S(1)} %get-tuple-element.24.column_ref, bf16[512,256]{1,0:T(8,128)(2,1)S(1)} %get-tuple-element.25.row1_ref, bf16[512,256]{1,0:T(8,128)(2,1)S(1)} %get-tuple-element.26.row23_ref), custom_call_target="tpu_custom_call" | custom-call | flops 117440512 | bytes 1048576 | tf_op jit(solution)/shard_map/pallas_call | solution.py:585
  19.1 0.1 collective-permute-start.6
  19.2 2.2 %collective-permute-done.2.note = bf16[136,128]{1,0:T(8,128)(2,1)S(1)} collective-permute-done((bf16[136,128]{1,0:T(8,128)(2,1)S(1)}, bf16[136,128]{1,0:T(8,128)(2,1)S(1)}, u32[]{:S(2)}, u32[]{:S(2)}) %collective-permute-start.2) | collective-permute-done | bytes 34848 | tf_op jit(solution)/shard_map/ppermute | solution.py:651
  21.4 0.6 %collective-permute-start.3 = (bf16[136,128]{1,0:T(8,128)(2,1)S(1)}, bf16[136,128]{1,0:T(8,128)(2,1)S(1)}, u32[]{:S(2)}, u32[]{:S(2)}) collective-permute-start(bf16[136,128]{1,0:T(8,128)(2,1)S(1)} %collective-permute-done.2.note), channel_id=1, source_target_pairs={{0,4},{4,0},{8,12},{12,8},{1,5},{5,1},{9,13},{13,9},{2,6},{6,2},{1... | collective-permute-start | bytes 104456 | tf_op jit(solution)/shard_map/ppermute | solution.py:678
  22.0 0.0 collective-permute-done.4.near
  22.0 1.3 %shard_map.119 = (f32[896,512]{1,0:T(8,128)S(1)}, bf16[24,512]{1,0:T(8,128)(2,1)S(1)}) custom-call(bf16[6,64,256]{2,1,0:T(8,128)(2,1)S(1)} %collective-permute-done.far, bf16[136,128]{1,0:T(8,128)(2,1)S(1)} %collective-permute-done.2.note, bf16[904,128]{1,0:T(8,128)(2,1)S(1)} %collective-permute-done.4.near, f32[896,512]{1,0:T(8,128)S(1)} %get-tuple-element.27.before_ref, ...), custom_call_target="tpu_custom_call" | custom-call | flops 469762048 | bytes 1048576 | tf_op jit(solution)/shard_map/pallas_call | solution.py:585
  23.3 1.0 %collective-permute-start.5 = (bf16[24,512]{1,0:T(8,128)(2,1)S(1)}, bf16[24,512]{1,0:T(8,128)(2,1)S(1)}, u32[]{:S(2)}, u32[]{:S(2)}) collective-permute-start(bf16[24,512]{1,0:T(8,128)(2,1)S(1)} %get-tuple-element.33), channel_id=1, source_target_pairs={{0,2},{2,0},{4,6},{6,4},{8,10},{10,8},{12,14},{14,12},{1,3},{3,1},... | collective-permute-start | bytes 73736 | tf_op jit(solution)/shard_map/ppermute | solution.py:674
  24.3 1.0 %collective-permute-done.3.note = bf16[136,128]{1,0:T(8,128)(2,1)S(1)} collective-permute-done((bf16[136,128]{1,0:T(8,128)(2,1)S(1)}, bf16[136,128]{1,0:T(8,128)(2,1)S(1)}, u32[]{:S(2)}, u32[]{:S(2)}) %collective-permute-start.3) | collective-permute-done | bytes 34848 | tf_op jit(solution)/shard_map/ppermute | solution.py:678
  25.3 0.0 collective-permute-done.1.late
  25.3 1.5 %shard_map.120 = (f32[7,32,512]{2,1,0:T(8,128)S(1)}, f32[7,24,256]{2,1,0:T(8,128)S(1)}, f32[7,16,128]{2,1,0:T(8,128)S(1)}, f32[7,8,128]{2,1,0:T(8,128)S(1)}) custom-call(bf16[6,64,256]{2,1,0:T(8,128)(2,1)S(1)} %collective-permute-done.1.late, bf16[136,128]{1,0:T(8,128)(2,1)S(1)} %collective-permute-done.3.note, f32[896,512]{1,0:T(8,128)S(1)} %get-tuple-element.28.before_ref, ...), custom_call_target="tpu_custom_call" | custom-call | flops 469762048 | bytes 1048576 | tf_op jit(solution)/shard_map/pallas_call | solution.py:585
  26.8 0.0 collective-permute-done.6.far_ref
  26.8 0.4 %collective-permute-done.5.near_ref = bf16[24,512]{1,0:T(8,128)(2,1)S(1)} collective-permute-done((bf16[24,512]{1,0:T(8,128)(2,1)S(1)}, bf16[24,512]{1,0:T(8,128)(2,1)S(1)}, u32[]{:S(2)}, u32[]{:S(2)}) %collective-permute-start.5) | collective-permute-done | bytes 24608 | tf_op jit(solution)/shard_map/ppermute | solution.py:674
  27.2 1.7 %shard_map.121 = bf16[6,32,512]{2,1,0:T(8,128)(2,1)} custom-call(f32[7,32,512]{2,1,0:T(8,128)S(1)} %get-tuple-element.29.a0_ref, f32[7,24,256]{2,1,0:T(8,128)S(1)} %get-tuple-element.30.a1_ref, f32[7,16,128]{2,1,0:T(8,128)S(1)} %get-tuple-element.31.a2_ref, f32[7,8,128]{2,1,0:T(8,128)S(1)} %get-tuple-element.32.a3_ref, ...), custom_call_target="tpu_custom_call" | custom-call | flops 469762048 | bytes 1048576 | tf_op jit(solution)/shard_map/pallas_call | solution.py:585
Async XLA Ops:
  0.0 11.1 %collective-permute-start = (bf16[6,64,256]{2,1,0:T(8,128)(2,1)}, bf16[6,64,256]{2,1,0:T(8,128)(2,1)S(1)}, u32[]{:S(2)}, u32[]{:S(2)}) collective-permute-start(bf16[6,64,256]{2,1,0:T(8,128)(2,1)} %bitcast.7), channel_id=1, source_target_pairs={{0,12},{4,8},{8,4},{12,0},{1,13},{5,9},{9,5},{13,1},{2,14},{6,10},... | collective-permute-start | bytes 589832 | tf_op jit(solution)/shard_map/ppermute | solution.py:632
  6.9 15.1 %collective-permute-start.4 = (bf16[904,128]{1,0:T(8,128)(2,1)S(1)}, bf16[904,128]{1,0:T(8,128)(2,1)S(1)}, u32[]{:S(2)}, u32[]{:S(2)}) collective-permute-start(bf16[904,128]{1,0:T(8,128)(2,1)S(1)} %get-tuple-element.23.pack), channel_id=1, source_target_pairs={{0,4},{4,0},{8,12},{12,8},{1,5},{5,1},{9,13},{13,9},{2,6},{6,2},{1... | collective-permute-start | bytes 694280 | tf_op jit(solution)/shard_map/ppermute | solution.py:652
  11.1 14.2 %collective-permute-start.1 = (bf16[6,64,256]{2,1,0:T(8,128)(2,1)S(1)}, bf16[6,64,256]{2,1,0:T(8,128)(2,1)S(1)}, u32[]{:S(2)}, u32[]{:S(2)}) collective-permute-start(bf16[6,64,256]{2,1,0:T(8,128)(2,1)S(1)} %collective-permute-done.far), channel_id=1, source_target_pairs={{0,4},{4,0},{8,12},{12,8},{1,5},{5,1},{9,13},{13,9},{2,6},{6,2},{1... | collective-permute-start | bytes 589832 | tf_op jit(solution)/shard_map/ppermute | solution.py:677
  14.1 7.2 %collective-permute-start.2 = (bf16[136,128]{1,0:T(8,128)(2,1)S(1)}, bf16[136,128]{1,0:T(8,128)(2,1)S(1)}, u32[]{:S(2)}, u32[]{:S(2)}) collective-permute-start(bf16[136,128]{1,0:T(8,128)(2,1)S(1)} %get-tuple-element.22), channel_id=1, source_target_pairs={{0,12},{4,8},{8,4},{12,0},{1,13},{5,9},{9,5},{13,1},{2,14},{6,10},... | collective-permute-start | bytes 104456 | tf_op jit(solution)/shard_map/ppermute | solution.py:651
  19.1 7.7 %collective-permute-start.6 = (bf16[24,512]{1,0:T(8,128)(2,1)S(1)}, bf16[24,512]{1,0:T(8,128)(2,1)S(1)}, u32[]{:S(2)}, u32[]{:S(2)}) collective-permute-start(bf16[24,512]{1,0:T(8,128)(2,1)S(1)} %get-tuple-element.34), channel_id=1, source_target_pairs={{0,10},{2,8},{4,14},{6,12},{8,2},{10,0},{12,6},{14,4},{1,11},{3,9}... | collective-permute-start | bytes 73736 | tf_op jit(solution)/shard_map/ppermute | solution.py:674
  21.4 3.9 %collective-permute-start.3 = (bf16[136,128]{1,0:T(8,128)(2,1)S(1)}, bf16[136,128]{1,0:T(8,128)(2,1)S(1)}, u32[]{:S(2)}, u32[]{:S(2)}) collective-permute-start(bf16[136,128]{1,0:T(8,128)(2,1)S(1)} %collective-permute-done.2.note), channel_id=1, source_target_pairs={{0,4},{4,0},{8,12},{12,8},{1,5},{5,1},{9,13},{13,9},{2,6},{6,2},{1... | collective-permute-start | bytes 104456 | tf_op jit(solution)/shard_map/ppermute | solution.py:678
  23.3 3.9 %collective-permute-start.5 = (bf16[24,512]{1,0:T(8,128)(2,1)S(1)}, bf16[24,512]{1,0:T(8,128)(2,1)S(1)}, u32[]{:S(2)}, u32[]{:S(2)}) collective-permute-start(bf16[24,512]{1,0:T(8,128)(2,1)S(1)} %get-tuple-element.33), channel_id=1, source_target_pairs={{0,2},{2,0},{4,6},{6,4},{8,10},{10,8},{12,14},{14,12},{1,3},{3,1},... | collective-permute-start | bytes 73736 | tf_op jit(solution)/shard_map/ppermute | solution.py:674

commit v7 on v6

--- a/solution.py
+++ b/solution.py
@@ -518,37 +518,33 @@
         keep = ((column >= 0) | ~first) & ((column < (w >> level)) | ~last)
         return keep.astype(F32)
 
-    top = g3_ref[...]
-    blend = top[:bands] / (BACKGROUND + top[bands:])
-    for level, cur_ref, below_ref, grow_ref, up_ref in (
-        (2, g2_ref, g3_ref, grow3_ref, e2_ref),
-        (1, g1_ref, g2_ref, grow2_ref, e1_ref),
-    ):
-        stacked = jnp.concatenate([below_ref[:bands], blend], axis=0)
-        k, c, r = stacked.shape
-        wide = dot2(stacked.reshape(k * c, r), grow_ref[...])
+    def grown(level, value, up_ref):
+        k, c, r = value.shape
+        if level == 0:
+            half = w // 2
+            x, y, z = value[:, :half], value[:, 1 : half + 1], value[:, 2 : half + 2]
+            tall = weave((x + 6.0 * y + z) * 0.125, (y + z) * 0.5, up_ref, w)
+            return dot2(tall.reshape(k * w, r), grow1_ref[...]).reshape(k, w, plan.rows)
+        grow_ref = (grow2_ref, grow3_ref)[level - 1]
+        wide = dot2(value.reshape(k * c, r), grow_ref[...])
         wide = wide.reshape(k, c, wide.shape[-1])
-        pairs = up8(plan.held[level]) // 2
-        pairs = min(pairs, c - 2)
-        even, odd = grow_columns(wide, 2 * pairs)
-        size = cur_ref.shape[1]
-        up = weave(even, odd, up_ref, size)
-        current = cur_ref[...]
-        inverse = 1.0 / (BACKGROUND + current[bands])
-        blend = (current[:bands] - up[:bands]) * inverse + up[bands:]
-        blend = blend * inside(level, blend.shape[1])
-    stacked = jnp.concatenate([g1_ref[:bands], blend], axis=0)
-    half = w // 2
-    a, b, c = stacked[:, :half], stacked[:, 1 : half + 1], stacked[:, 2 : half + 2]
-    even, odd = (a + 6.0 * b + c) * 0.125, (b + c) * 0.5
-    tall = weave(even, odd, e0_ref, w)
-    up = dot2(tall.reshape(2 * bands * w, tall.shape[-1]), grow1_ref[...])
-    up = up.reshape(2 * bands, w, plan.rows)
-    inverse = 1.0 / (BACKGROUND + a0_ref[bands])
+        pairs = min(up8(plan.held[level]) // 2, c - 2)
+        return weave(*grow_columns(wide, 2 * pairs), up_ref, plan.size[level])
+
+    e2a_ref, e1a_ref, e0a_ref = (ref.at[pl.ds(0, bands)] for ref in (e2_ref, e1_ref, e0_ref))
+    e2b_ref, e1b_ref, e0b_ref = (ref.at[pl.ds(bands, bands)] for ref in (e2_ref, e1_ref, e0_ref))
+    inverses = [1.0 / (BACKGROUND + ref[bands]) for ref in (a0_ref, g1_ref, g2_ref, g3_ref)]
+    blend = g3_ref[:bands] * inverses[3]
+    detail2 = (g2_ref[:bands] - grown(2, g3_ref[:bands], e2a_ref)) * inverses[2]
+    blend = (detail2 + grown(2, blend, e2b_ref)) * inside(2, plan.size[2])
+    detail1 = (g1_ref[:bands] - grown(1, g2_ref[:bands], e1a_ref)) * inverses[1]
+    blend = (detail1 + grown(1, blend, e1b_ref)) * inside(1, plan.size[1])
+    detail0 = (a0_ref[:bands] - grown(0, g1_ref[:bands], e0a_ref)) * inverses[0]
+    up = grown(0, blend, e0b_ref)
     copies = []
     part = bands // 2
     for f in range(0, bands, part):
-        value = (a0_ref[f : f + part] - up[f : f + part]) * inverse + up[bands + f : bands + f + part]
+        value = detail0[f : f + part] + up[f : f + part]
         value = value.astype(BF).reshape(part * w, plan.rows)
         value = jnp.dot(value, natural_ref[...], preferred_element_type=F32)
         strip_ref[pl.ds(f, part)] = value.astype(BF).reshape(part, w, plan.rows)

time: 29.1 us -> 29 us (level)
  no operation moved by 1% of the time
where the time goes in v7:
time: 29 us; the launch traced here: 28.8 us
  starting transfers between devices  12.3 us (42%)
  Pallas kernels  8.05 us (28%)
  waiting for transfers between devices  7.77 us (27%)
  between operations  0.7 us (2%)
    pallas_call x4, Pallas kernels, call(): pl.pallas_call(functools.partial(kernel, plan), out_shape=outputs, in_spe...  5.52 us
    ppermute x1, starting transfers between devices, strip_local(): far = lax.ppermute(blocks, 'tx', across)  5.08 us
    ppermute x1, waiting for transfers between devices, strip_local(): far = lax.ppermute(blocks, 'tx', across)  4.15 us
    ppermute x1, starting transfers between devices, strip_local(): late = lax.ppermute(far, 'tx', beside)  3.03 us
    ppermute x1, starting transfers between devices, strip_local(): far_note = lax.ppermute(note, 'tx', across)  2.47 us
    ppermute x1, waiting for transfers between devices, strip_local(): far_note = lax.ppermute(note, 'tx', across)  2.2 us
    pallas_call x1, Pallas kernels, strip_local(): pl.pallas_call(functools.partial(load_kernel, plan), out_shape=[pltpu.VME...  1.41 us
    pallas_call x1, Pallas kernels, strip_local(): pl.pallas_call(functools.partial(pack_kernel, plan), out_shape=[pltpu.VME...  1.12 us
  transfers between devices with their start and end apart: 7, of which 4 were waited for; matrix products, arithmetic and copies ran while one was open for 0% of the time, Pallas kernels for 22%

profile of v7, /device:TPU:0, one launch (start us, length us, event | category | flops | bytes accessed | tf_op | source)
XLA Modules:
  0.0 28.8 jit_solution(12200623375567418668)
XLA Ops:
  0.0 5.1 %collective-permute-start = (bf16[6,64,256]{2,1,0:T(8,128)(2,1)}, bf16[6,64,256]{2,1,0:T(8,128)(2,1)S(1)}, u32[]{:S(2)}, u32[]{:S(2)}) collective-permute-start(bf16[6,64,256]{2,1,0:T(8,128)(2,1)} %bitcast.7), channel_id=1, source_target_pairs={{0,12},{4,8},{8,4},{12,0},{1,13},{5,9},{9,5},{13,1},{2,14},{6,10},... | collective-permute-start | bytes 589832 | tf_op jit(solution)/shard_map/ppermute | solution.py:628
  5.7 1.1 %pack.1 = (bf16[904,128]{1,0:T(8,128)(2,1)S(1)}, bf16[136,128]{1,0:T(8,128)(2,1)S(1)}) custom-call(s32[1,1]{1,0:T(1,128)S(6)} %copy.14.count_ref, bf16[6,64,256]{2,1,0:T(8,128)(2,1)} %bitcast.8, bf16[64,256]{1,0:T(8,128)(2,1)} %bitcast.9, s32[1,64]{1,0:T(1,128)} %dest_ref.1, s32[1,64]{1,0:T(1,128)} %offset_ref.1), custom_call_target="tpu_custom_call" | custom-call | tf_op jit(solution)/shard_map/pack/pallas_call | solution.py:629
  6.9 0.1 collective-permute-start.4
  6.9 4.1 %collective-permute-done.far = bf16[6,64,256]{2,1,0:T(8,128)(2,1)S(1)} collective-permute-done((bf16[6,64,256]{2,1,0:T(8,128)(2,1)}, bf16[6,64,256]{2,1,0:T(8,128)(2,1)S(1)}, u32[]{:S(2)}, u32[]{:S(2)}) %collective-permute-start) | collective-permute-done | bytes 196640 | tf_op jit(solution)/shard_map/ppermute | solution.py:628
  11.1 3.0 %collective-permute-start.1 = (bf16[6,64,256]{2,1,0:T(8,128)(2,1)S(1)}, bf16[6,64,256]{2,1,0:T(8,128)(2,1)S(1)}, u32[]{:S(2)}, u32[]{:S(2)}) collective-permute-start(bf16[6,64,256]{2,1,0:T(8,128)(2,1)S(1)} %collective-permute-done.far), channel_id=1, source_target_pairs={{0,4},{4,0},{8,12},{12,8},{1,5},{5,1},{9,13},{13,9},{2,6},{6,2},{1... | collective-permute-start | bytes 589832 | tf_op jit(solution)/shard_map/ppermute | solution.py:673
  14.1 2.5 %collective-permute-start.2 = (bf16[136,128]{1,0:T(8,128)(2,1)S(1)}, bf16[136,128]{1,0:T(8,128)(2,1)S(1)}, u32[]{:S(2)}, u32[]{:S(2)}) collective-permute-start(bf16[136,128]{1,0:T(8,128)(2,1)S(1)} %get-tuple-element.22), channel_id=1, source_target_pairs={{0,12},{4,8},{8,4},{12,0},{1,13},{5,9},{9,5},{13,1},{2,14},{6,10},... | collective-permute-start | bytes 104456 | tf_op jit(solution)/shard_map/ppermute | solution.py:647
  16.6 1.4 %load.1 = (bf16[136,256]{1,0:T(8,128)(2,1)S(1)}, bf16[512,256]{1,0:T(8,128)(2,1)S(1)}, bf16[512,256]{1,0:T(8,128)(2,1)S(1)}, bf16[256,512]{1,0:T(8,128)(2,1)S(1)...) custom-call(bf16[8,136,256]{2,1,0:T(8,128)(2,1)} %constant.14.clone.column_ref, ...), custom_call_target="tpu_custom_call" | custom-call | tf_op jit(solution)/shard_map/load/pallas_call | solution.py:604
  18.0 1.1 %shard_map.118 = (f32[896,512]{1,0:T(8,128)S(1)}, bf16[24,512]{1,0:T(8,128)(2,1)S(1)}) custom-call(bf16[904,128]{1,0:T(8,128)(2,1)S(1)} %get-tuple-element.23.pack, bf16[136,256]{1,0:T(8,128)(2,1)S(1)} %get-tuple-element.24.column_ref, bf16[512,256]{1,0:T(8,128)(2,1)S(1)} %get-tuple-element.25.row1_ref, bf16[512,256]{1,0:T(8,128)(2,1)S(1)} %get-tuple-element.26.row23_ref), custom_call_target="tpu_custom_call" | custom-call | flops 117440512 | bytes 1048576 | tf_op jit(solution)/shard_map/pallas_call | solution.py:581
  19.1 0.1 collective-permute-start.6
  19.2 2.2 %collective-permute-done.2.note = bf16[136,128]{1,0:T(8,128)(2,1)S(1)} collective-permute-done((bf16[136,128]{1,0:T(8,128)(2,1)S(1)}, bf16[136,128]{1,0:T(8,128)(2,1)S(1)}, u32[]{:S(2)}, u32[]{:S(2)}) %collective-permute-start.2) | collective-permute-done | bytes 34848 | tf_op jit(solution)/shard_map/ppermute | solution.py:647
  21.4 0.6 %collective-permute-start.3 = (bf16[136,128]{1,0:T(8,128)(2,1)S(1)}, bf16[136,128]{1,0:T(8,128)(2,1)S(1)}, u32[]{:S(2)}, u32[]{:S(2)}) collective-permute-start(bf16[136,128]{1,0:T(8,128)(2,1)S(1)} %collective-permute-done.2.note), channel_id=1, source_target_pairs={{0,4},{4,0},{8,12},{12,8},{1,5},{5,1},{9,13},{13,9},{2,6},{6,2},{1... | collective-permute-start | bytes 104456 | tf_op jit(solution)/shard_map/ppermute | solution.py:674
  22.0 0.0 collective-permute-done.4.near
  22.0 1.3 %shard_map.119 = (f32[896,512]{1,0:T(8,128)S(1)}, bf16[24,512]{1,0:T(8,128)(2,1)S(1)}) custom-call(bf16[6,64,256]{2,1,0:T(8,128)(2,1)S(1)} %collective-permute-done.far, bf16[136,128]{1,0:T(8,128)(2,1)S(1)} %collective-permute-done.2.note, bf16[904,128]{1,0:T(8,128)(2,1)S(1)} %collective-permute-done.4.near, f32[896,512]{1,0:T(8,128)S(1)} %get-tuple-element.27.before_ref, ...), custom_call_target="tpu_custom_call" | custom-call | flops 469762048 | bytes 1048576 | tf_op jit(solution)/shard_map/pallas_call | solution.py:581
  23.3 1.0 %collective-permute-start.5 = (bf16[24,512]{1,0:T(8,128)(2,1)S(1)}, bf16[24,512]{1,0:T(8,128)(2,1)S(1)}, u32[]{:S(2)}, u32[]{:S(2)}) collective-permute-start(bf16[24,512]{1,0:T(8,128)(2,1)S(1)} %get-tuple-element.33), channel_id=1, source_target_pairs={{0,2},{2,0},{4,6},{6,4},{8,10},{10,8},{12,14},{14,12},{1,3},{3,1},... | collective-permute-start | bytes 73736 | tf_op jit(solution)/shard_map/ppermute | solution.py:670
  24.3 1.0 %collective-permute-done.3.note = bf16[136,128]{1,0:T(8,128)(2,1)S(1)} collective-permute-done((bf16[136,128]{1,0:T(8,128)(2,1)S(1)}, bf16[136,128]{1,0:T(8,128)(2,1)S(1)}, u32[]{:S(2)}, u32[]{:S(2)}) %collective-permute-start.3) | collective-permute-done | bytes 34848 | tf_op jit(solution)/shard_map/ppermute | solution.py:674
  25.3 0.0 collective-permute-done.1.late
  25.3 1.5 %shard_map.120 = (f32[7,32,512]{2,1,0:T(8,128)S(1)}, f32[7,24,256]{2,1,0:T(8,128)S(1)}, f32[7,16,128]{2,1,0:T(8,128)S(1)}, f32[7,8,128]{2,1,0:T(8,128)S(1)}) custom-call(bf16[6,64,256]{2,1,0:T(8,128)(2,1)S(1)} %collective-permute-done.1.late, bf16[136,128]{1,0:T(8,128)(2,1)S(1)} %collective-permute-done.3.note, f32[896,512]{1,0:T(8,128)S(1)} %get-tuple-element.28.before_ref, ...), custom_call_target="tpu_custom_call" | custom-call | flops 469762048 | bytes 1048576 | tf_op jit(solution)/shard_map/pallas_call | solution.py:581
  26.8 0.0 collective-permute-done.6.far_ref
  26.8 0.4 %collective-permute-done.5.near_ref = bf16[24,512]{1,0:T(8,128)(2,1)S(1)} collective-permute-done((bf16[24,512]{1,0:T(8,128)(2,1)S(1)}, bf16[24,512]{1,0:T(8,128)(2,1)S(1)}, u32[]{:S(2)}, u32[]{:S(2)}) %collective-permute-start.5) | collective-permute-done | bytes 24608 | tf_op jit(solution)/shard_map/ppermute | solution.py:670
  27.2 1.6 %shard_map.121 = bf16[6,32,512]{2,1,0:T(8,128)(2,1)} custom-call(f32[7,32,512]{2,1,0:T(8,128)S(1)} %get-tuple-element.29.a0_ref, f32[7,24,256]{2,1,0:T(8,128)S(1)} %get-tuple-element.30.a1_ref, f32[7,16,128]{2,1,0:T(8,128)S(1)} %get-tuple-element.31.a2_ref, f32[7,8,128]{2,1,0:T(8,128)S(1)} %get-tuple-element.32.a3_ref, ...), custom_call_target="tpu_custom_call" | custom-call | flops 469762048 | bytes 1048576 | tf_op jit(solution)/shard_map/pallas_call | solution.py:581
Async XLA Ops:
  0.0 11.1 %collective-permute-start = (bf16[6,64,256]{2,1,0:T(8,128)(2,1)}, bf16[6,64,256]{2,1,0:T(8,128)(2,1)S(1)}, u32[]{:S(2)}, u32[]{:S(2)}) collective-permute-start(bf16[6,64,256]{2,1,0:T(8,128)(2,1)} %bitcast.7), channel_id=1, source_target_pairs={{0,12},{4,8},{8,4},{12,0},{1,13},{5,9},{9,5},{13,1},{2,14},{6,10},... | collective-permute-start | bytes 589832 | tf_op jit(solution)/shard_map/ppermute | solution.py:628
  6.9 15.1 %collective-permute-start.4 = (bf16[904,128]{1,0:T(8,128)(2,1)S(1)}, bf16[904,128]{1,0:T(8,128)(2,1)S(1)}, u32[]{:S(2)}, u32[]{:S(2)}) collective-permute-start(bf16[904,128]{1,0:T(8,128)(2,1)S(1)} %get-tuple-element.23.pack), channel_id=1, source_target_pairs={{0,4},{4,0},{8,12},{12,8},{1,5},{5,1},{9,13},{13,9},{2,6},{6,2},{1... | collective-permute-start | bytes 694280 | tf_op jit(solution)/shard_map/ppermute | solution.py:648
  11.1 14.2 %collective-permute-start.1 = (bf16[6,64,256]{2,1,0:T(8,128)(2,1)S(1)}, bf16[6,64,256]{2,1,0:T(8,128)(2,1)S(1)}, u32[]{:S(2)}, u32[]{:S(2)}) collective-permute-start(bf16[6,64,256]{2,1,0:T(8,128)(2,1)S(1)} %collective-permute-done.far), channel_id=1, source_target_pairs={{0,4},{4,0},{8,12},{12,8},{1,5},{5,1},{9,13},{13,9},{2,6},{6,2},{1... | collective-permute-start | bytes 589832 | tf_op jit(solution)/shard_map/ppermute | solution.py:673
  14.1 7.2 %collective-permute-start.2 = (bf16[136,128]{1,0:T(8,128)(2,1)S(1)}, bf16[136,128]{1,0:T(8,128)(2,1)S(1)}, u32[]{:S(2)}, u32[]{:S(2)}) collective-permute-start(bf16[136,128]{1,0:T(8,128)(2,1)S(1)} %get-tuple-element.22), channel_id=1, source_target_pairs={{0,12},{4,8},{8,4},{12,0},{1,13},{5,9},{9,5},{13,1},{2,14},{6,10},... | collective-permute-start | bytes 104456 | tf_op jit(solution)/shard_map/ppermute | solution.py:647
  19.1 7.7 %collective-permute-start.6 = (bf16[24,512]{1,0:T(8,128)(2,1)S(1)}, bf16[24,512]{1,0:T(8,128)(2,1)S(1)}, u32[]{:S(2)}, u32[]{:S(2)}) collective-permute-start(bf16[24,512]{1,0:T(8,128)(2,1)S(1)} %get-tuple-element.34), channel_id=1, source_target_pairs={{0,10},{2,8},{4,14},{6,12},{8,2},{10,0},{12,6},{14,4},{1,11},{3,9}... | collective-permute-start | bytes 73736 | tf_op jit(solution)/shard_map/ppermute | solution.py:670
  21.4 3.9 %collective-permute-start.3 = (bf16[136,128]{1,0:T(8,128)(2,1)S(1)}, bf16[136,128]{1,0:T(8,128)(2,1)S(1)}, u32[]{:S(2)}, u32[]{:S(2)}) collective-permute-start(bf16[136,128]{1,0:T(8,128)(2,1)S(1)} %collective-permute-done.2.note), channel_id=1, source_target_pairs={{0,4},{4,0},{8,12},{12,8},{1,5},{5,1},{9,13},{13,9},{2,6},{6,2},{1... | collective-permute-start | bytes 104456 | tf_op jit(solution)/shard_map/ppermute | solution.py:674
  23.3 3.9 %collective-permute-start.5 = (bf16[24,512]{1,0:T(8,128)(2,1)S(1)}, bf16[24,512]{1,0:T(8,128)(2,1)S(1)}, u32[]{:S(2)}, u32[]{:S(2)}) collective-permute-start(bf16[24,512]{1,0:T(8,128)(2,1)S(1)} %get-tuple-element.33), channel_id=1, source_target_pairs={{0,2},{2,0},{4,6},{6,4},{8,10},{10,8},{12,14},{14,12},{1,3},{3,1},... | collective-permute-start | bytes 73736 | tf_op jit(solution)/shard_map/ppermute | solution.py:670

commit v8 on v7

--- a/solution.py
+++ b/solution.py
@@ -242,7 +242,7 @@
             self.at.append(self.at[-1] + size)
         self.low_at = self.at[LEVELS]
         self.main = self.low_at + self.size[3]
-        self.edge_rows = 8 * (LEVELS - 1)
+        self.edge_rows = 8 * LEVELS
         self.total = self.main + 2 * self.edge_rows
         self.near = 2 * BS
         self.half = BS * BS // 2
@@ -274,9 +274,11 @@
                             if 0 <= base + k < width >> level:
                                 row = grids[level][base + k, j * TS : (j + 1) * TS]
                                 row = row[TS - self.near :] if right else row[: self.near]
-                                tables[t, j, at + k, : self.near] = row
+                                tables[t, j, at + k, : 2 * self.near] = np.concatenate([row, row])
         high, low = split_table(tables)
         high[:, :, self.low_at : self.main] = low[:, :, self.at[3] : self.at[4]]
+        for at in (self.main + self.edge_rows, self.total):
+            high[:, :, at - 8 : at] = low[:, :, at - 16 : at - 8]
         return np.concatenate([high, high], axis=-1).reshape(n * m, self.total, 2 * TS)
 
 
@@ -393,22 +395,25 @@
             at = f * plan.half + 2 * u * BS
             pair = turn(plan, side_ref[at : at + BS], side_ref[at + BS : at + 2 * BS])
             for k, value in enumerate(pair):
-                tile[k * BS : (k + 1) * BS, u * TS : (u + 1) * TS] = value.astype(BF)
+                high, low = halves(value)
+                tile[k * BS : (k + 1) * BS, u * TS : (u + 1) * TS] = high
+                tile[plan.near + k * BS : plan.near + (k + 1) * BS, u * TS : (u + 1) * TS] = low
         cols = jnp.dot(table, tile[...], preferred_element_type=F32)
         z1_ref[f] = cols[:8]
-        z23_ref[f] = cols[8:]
-    out_ref[...] = jnp.zeros(out_ref.shape, out_ref.dtype)
-    z1 = z1_ref[...].reshape(planes * 8, rows).astype(BF)
-    z1 = jnp.dot(z1, row1_ref[...], preferred_element_type=F32).reshape(planes, 8, rows // 2)
-    z23 = z23_ref[...].reshape(planes * 16, rows).astype(BF)
-    z23 = jnp.dot(z23, row23_ref[...], preferred_element_type=F32).reshape(planes, 16, rows // 2)
+        z23_ref[f, :8] = cols[8:16]
+        z23_ref[f, 8:] = cols[16:24] + cols[24:]
+    kind = out_ref.dtype
+    out_ref[...] = jnp.zeros(out_ref.shape, kind)
+    z1 = dot2(z1_ref[...].reshape(planes * 8, rows), row1_ref[...])
+    z1 = z1.reshape(planes, 8, rows // 2)
+    z23 = dot2(z23_ref[...].reshape(planes * 16, rows), row23_ref[...])
+    z23 = z23.reshape(planes, 16, rows // 2)
     second = rows // 2 + rows // 4
     for f in range(planes):
         at = pl.ds(EDGE * f, EDGE)
-        out_ref[at, : rows // 2] = z1[f, :EDGE].astype(BF)
-        out_ref[at, rows // 2 : second] = z23[f, :EDGE, : rows // 4].astype(BF)
-        top = twin_sum(z23[f, 8:, rows // 4 :])
-        out_ref[at, second:] = top[:EDGE].astype(BF)
+        out_ref[at, : rows // 2] = z1[f, :EDGE].astype(kind)
+        out_ref[at, rows // 2 : second] = z23[f, :EDGE, : rows // 4].astype(kind)
+        out_ref[at, second:] = twin_sum(z23[f, 8:, rows // 4 :])[:EDGE].astype(kind)
 
 
 def side_of(plan, sums, right):
@@ -421,7 +426,7 @@
     sums = slot_sums(plan, pack, pack.at[pl.ds(plan.weight_at, plan.half + CODE_ROWS)], prod_ref)
     out_ref[...] = sums
     side_ref[...] = side_of(plan, sums, right)
-    table = column_ref[plan.main + plan.edge_rows :, : plan.near]
+    table = column_ref[plan.main + plan.edge_rows :, : 2 * plan.near]
     edge_of(plan, side_ref, table, row1_ref, row23_ref, edge_ref, tile_ref, z1_ref, z23_ref)
 
 
@@ -433,7 +438,7 @@
     sums = before_ref[...] + sums + slot_sums(plan, far, note, prod_ref.at[1])
     out_ref[...] = sums
     side_ref[...] = side_of(plan, sums, right)
-    table = column_ref[plan.main : plan.main + plan.edge_rows, : plan.near]
+    table = column_ref[plan.main : plan.main + plan.edge_rows, : 2 * plan.near]
     edge_of(plan, side_ref, table, row1_ref, row23_ref, edge_ref, tile_ref, z1_ref, z23_ref)
 
 
@@ -501,7 +506,7 @@
     first, last = row_tile == 0, row_tile == plan.n - 1
     left, right = first & (col_tile > 0), last & (col_tile < plan.m - 1)
     first, last = first & (col_tile == 0), last & (col_tile == plan.m - 1)
-    edges = near_ref[...].astype(F32) + far_ref[...].astype(F32)
+    edges = near_ref[...] + far_ref[...].astype(F32)
     start = 0
     for level, (src, dst) in enumerate(((a1_ref, g1_ref), (a2_ref, g2_ref), (a3_ref, g3_ref)), 1):
         lanes = src.shape[-1]
@@ -648,15 +653,14 @@
     near = lax.ppermute(pack, "tx", beside)
     edge_work = [
         pltpu.VMEM((planes * plan.half, TS), F32),
-        pltpu.VMEM((2, plan.near, plan.rows), BF),
+        pltpu.VMEM((2, 2 * plan.near, plan.rows), BF),
         pltpu.VMEM((planes, 8, plan.rows), F32),
         pltpu.VMEM((planes, 16, plan.rows), F32),
     ]
-    sums_and_edge = [sums_shape, pltpu.VMEM(edge_shape, BF)]
     sums, edge_far = call(
         own_kernel,
         [pack] + tables,
-        sums_and_edge,
+        [sums_shape, pltpu.VMEM(edge_shape, BF)],
         [pltpu.VMEM(prod_shape, BF)] + edge_work,
         flops=work,
     )
@@ -675,7 +679,7 @@
     sums, edge_near = call(
         first_kernel,
         [far, far_note, near, sums] + tables,
-        sums_and_edge,
+        [sums_shape, pltpu.VMEM(edge_shape, F32)],
         [pltpu.VMEM((2, *prod_shape), BF)] + edge_work,
         flops=4 * work,
     )

time: 29 us -> 31.4 us (1.083)
  starting transfers between devices: 12.3 us -> 15.4 us
  waiting for transfers between devices: 7.77 us -> 7.03 us
    ppermute x2, starting transfers between devices: 1.04 us -> 4.76 us  [over(): return lax.ppermute(value, ('tx', 'ty'), pairs)]
    ppermute x1, waiting for transfers between devices: 1.02 us -> 0.01 us  [strip_local(): late_note = lax.ppermute(far_note, 'tx', beside)]
    ppermute x1, starting transfers between devices: 0.63 us -> 0.01 us  [strip_local(): late_note = lax.ppermute(far_note, 'tx', beside)]
    ppermute x2, waiting for transfers between devices: 0.4 us -> 0.91 us  [over(): return lax.ppermute(value, ('tx', 'ty'), pairs)]
  transfers between devices with their start and end apart: 7 -> 7, of which waited for: 4 -> 3; matrix products, arithmetic and copies ran while one was open for 0% -> 0% of each run, Pallas kernels for 22% -> 21%
where the time goes in v8:
time: 31.4 us; the launch traced here: 31.3 us
  starting transfers between devices  15.4 us (49%)
  Pallas kernels  8.13 us (26%)
  waiting for transfers between devices  7.03 us (22%)
  between operations  0.69 us (2%)
    pallas_call x4, Pallas kernels, call(): pl.pallas_call(functools.partial(kernel, plan), out_shape=outputs, in_spe...  5.59 us
    ppermute x1, starting transfers between devices, strip_local(): far = lax.ppermute(blocks, 'tx', across)  5.08 us
    ppermute x2, starting transfers between devices, over(): return lax.ppermute(value, ('tx', 'ty'), pairs)  4.76 us
    ppermute x1, waiting for transfers between devices, strip_local(): far = lax.ppermute(blocks, 'tx', across)  4.15 us
    ppermute x1, starting transfers between devices, strip_local(): late = lax.ppermute(far, 'tx', beside)  3.03 us
    ppermute x1, starting transfers between devices, strip_local(): far_note = lax.ppermute(note, 'tx', across)  2.47 us
    ppermute x1, waiting for transfers between devices, strip_local(): far_note = lax.ppermute(note, 'tx', across)  1.97 us
    pallas_call x1, Pallas kernels, strip_local(): pl.pallas_call(functools.partial(load_kernel, plan), out_shape=[pltpu.VME...  1.42 us
  transfers between devices with their start and end apart: 7, of which 3 were waited for; matrix products, arithmetic and copies ran while one was open for 0% of the time, Pallas kernels for 21%

profile of v8, /device:TPU:0, one launch (start us, length us, event | category | flops | bytes accessed | tf_op | source)
XLA Modules:
  0.0 31.3 jit_solution(13892901268220073574)
XLA Ops:
  0.0 5.1 %collective-permute-start = (bf16[6,64,256]{2,1,0:T(8,128)(2,1)}, bf16[6,64,256]{2,1,0:T(8,128)(2,1)S(1)}, u32[]{:S(2)}, u32[]{:S(2)}) collective-permute-start(bf16[6,64,256]{2,1,0:T(8,128)(2,1)} %bitcast.7), channel_id=1, source_target_pairs={{0,12},{4,8},{8,4},{12,0},{1,13},{5,9},{9,5},{13,1},{2,14},{6,10},... | collective-permute-start | bytes 589832 | tf_op jit(solution)/shard_map/ppermute | solution.py:633
  5.7 1.1 %pack.1 = (bf16[904,128]{1,0:T(8,128)(2,1)S(1)}, bf16[136,128]{1,0:T(8,128)(2,1)S(1)}) custom-call(s32[1,1]{1,0:T(1,128)S(6)} %copy.14.count_ref, bf16[6,64,256]{2,1,0:T(8,128)(2,1)} %bitcast.8, bf16[64,256]{1,0:T(8,128)(2,1)} %bitcast.9, s32[1,64]{1,0:T(1,128)} %dest_ref.1, s32[1,64]{1,0:T(1,128)} %offset_ref.1), custom_call_target="tpu_custom_call" | custom-call | tf_op jit(solution)/shard_map/pack/pallas_call | solution.py:634
  6.9 0.1 collective-permute-start.4
  6.9 4.1 %collective-permute-done.far = bf16[6,64,256]{2,1,0:T(8,128)(2,1)S(1)} collective-permute-done((bf16[6,64,256]{2,1,0:T(8,128)(2,1)}, bf16[6,64,256]{2,1,0:T(8,128)(2,1)S(1)}, u32[]{:S(2)}, u32[]{:S(2)}) %collective-permute-start) | collective-permute-done | bytes 196640 | tf_op jit(solution)/shard_map/ppermute | solution.py:633
  11.1 3.0 %collective-permute-start.1 = (bf16[6,64,256]{2,1,0:T(8,128)(2,1)S(1)}, bf16[6,64,256]{2,1,0:T(8,128)(2,1)S(1)}, u32[]{:S(2)}, u32[]{:S(2)}) collective-permute-start(bf16[6,64,256]{2,1,0:T(8,128)(2,1)S(1)} %collective-permute-done.far), channel_id=1, source_target_pairs={{0,4},{4,0},{8,12},{12,8},{1,5},{5,1},{9,13},{13,9},{2,6},{6,2},{1... | collective-permute-start | bytes 589832 | tf_op jit(solution)/shard_map/ppermute | solution.py:677
  14.1 2.5 %collective-permute-start.2 = (bf16[136,128]{1,0:T(8,128)(2,1)S(1)}, bf16[136,128]{1,0:T(8,128)(2,1)S(1)}, u32[]{:S(2)}, u32[]{:S(2)}) collective-permute-start(bf16[136,128]{1,0:T(8,128)(2,1)S(1)} %get-tuple-element.22), channel_id=1, source_target_pairs={{0,12},{4,8},{8,4},{12,0},{1,13},{5,9},{9,5},{13,1},{2,14},{6,10},... | collective-permute-start | bytes 104456 | tf_op jit(solution)/shard_map/ppermute | solution.py:652
  16.6 1.4 %load.1 = (bf16[152,256]{1,0:T(8,128)(2,1)S(1)}, bf16[512,256]{1,0:T(8,128)(2,1)S(1)}, bf16[512,256]{1,0:T(8,128)(2,1)S(1)}, bf16[256,512]{1,0:T(8,128)(2,1)S(1)...) custom-call(bf16[8,152,256]{2,1,0:T(8,128)(2,1)} %constant.14.clone.column_ref, ...), custom_call_target="tpu_custom_call" | custom-call | tf_op jit(solution)/shard_map/load/pallas_call | solution.py:609
  18.0 1.1 %shard_map.118 = (f32[896,512]{1,0:T(8,128)S(1)}, bf16[24,512]{1,0:T(8,128)(2,1)S(1)}) custom-call(bf16[904,128]{1,0:T(8,128)(2,1)S(1)} %get-tuple-element.23.pack, bf16[152,256]{1,0:T(8,128)(2,1)S(1)} %get-tuple-element.24.column_ref, bf16[512,256]{1,0:T(8,128)(2,1)S(1)} %get-tuple-element.25.row1_ref, bf16[512,256]{1,0:T(8,128)(2,1)S(1)} %get-tuple-element.26.row23_ref), custom_call_target="tpu_custom_call" | custom-call | flops 117440512 | bytes 1048576 | tf_op jit(solution)/shard_map/pallas_call | solution.py:586
  19.1 2.0 %collective-permute-done.2.note = bf16[136,128]{1,0:T(8,128)(2,1)S(1)} collective-permute-done((bf16[136,128]{1,0:T(8,128)(2,1)S(1)}, bf16[136,128]{1,0:T(8,128)(2,1)S(1)}, u32[]{:S(2)}, u32[]{:S(2)}) %collective-permute-start.2) | collective-permute-done | bytes 34848 | tf_op jit(solution)/shard_map/ppermute | solution.py:652
  21.1 0.0 collective-permute-start.3
  21.1 0.0 collective-permute-done.4.near
  21.1 1.4 %shard_map.119 = (f32[896,512]{1,0:T(8,128)S(1)}, f32[24,512]{1,0:T(8,128)S(1)}) custom-call(bf16[6,64,256]{2,1,0:T(8,128)(2,1)S(1)} %collective-permute-done.far, bf16[136,128]{1,0:T(8,128)(2,1)S(1)} %collective-permute-done.2.note, bf16[904,128]{1,0:T(8,128)(2,1)S(1)} %collective-permute-done.4.near, f32[896,512]{1,0:T(8,128)S(1)} %get-tuple-element.27.before_ref, ...), custom_call_target="tpu_custom_call" | custom-call | flops 469762048 | bytes 1048576 | tf_op jit(solution)/shard_map/pallas_call | solution.py:586
  22.5 1.6 %collective-permute-start.5 = (f32[24,512]{1,0:T(8,128)S(1)}, f32[24,512]{1,0:T(8,128)S(1)}, u32[]{:S(2)}, u32[]{:S(2)}) collective-permute-start(f32[24,512]{1,0:T(8,128)S(1)} %get-tuple-element.33), channel_id=1, source_target_pairs={{0,2},{2,0},{4,6},{6,4},{8,10},{10,8},{12,14},{14,12},{1,3},{3,1},... | collective-permute-start | bytes 147464 | tf_op jit(solution)/shard_map/ppermute | solution.py:674
  24.0 3.2 %collective-permute-start.6 = (bf16[24,512]{1,0:T(8,128)(2,1)S(1)}, bf16[24,512]{1,0:T(8,128)(2,1)S(1)}, u32[]{:S(2)}, u32[]{:S(2)}) collective-permute-start(bf16[24,512]{1,0:T(8,128)(2,1)S(1)} %get-tuple-element.34), channel_id=1, source_target_pairs={{0,10},{2,8},{4,14},{6,12},{8,2},{10,0},{12,6},{14,4},{1,11},{3,9}... | collective-permute-start | bytes 73736 | tf_op jit(solution)/shard_map/ppermute | solution.py:674
  27.2 0.0 collective-permute-done.3.note
  27.2 0.0 collective-permute-done.1.late
  27.2 1.5 %shard_map.120 = (f32[7,32,512]{2,1,0:T(8,128)S(1)}, f32[7,24,256]{2,1,0:T(8,128)S(1)}, f32[7,16,128]{2,1,0:T(8,128)S(1)}, f32[7,8,128]{2,1,0:T(8,128)S(1)}) custom-call(bf16[6,64,256]{2,1,0:T(8,128)(2,1)S(1)} %collective-permute-done.1.late, bf16[136,128]{1,0:T(8,128)(2,1)S(1)} %collective-permute-done.3.note, f32[896,512]{1,0:T(8,128)S(1)} %get-tuple-element.28.before_ref, ...), custom_call_target="tpu_custom_call" | custom-call | flops 469762048 | bytes 1048576 | tf_op jit(solution)/shard_map/pallas_call | solution.py:586
  28.7 0.9 %collective-permute-done.6.far_ref = bf16[24,512]{1,0:T(8,128)(2,1)S(1)} collective-permute-done((bf16[24,512]{1,0:T(8,128)(2,1)S(1)}, bf16[24,512]{1,0:T(8,128)(2,1)S(1)}, u32[]{:S(2)}, u32[]{:S(2)}) %collective-permute-start.6) | collective-permute-done | bytes 24608 | tf_op jit(solution)/shard_map/ppermute | solution.py:674
  29.6 0.0 collective-permute-done.5.near_ref
  29.6 1.6 %shard_map.121 = bf16[6,32,512]{2,1,0:T(8,128)(2,1)} custom-call(f32[7,32,512]{2,1,0:T(8,128)S(1)} %get-tuple-element.29.a0_ref, f32[7,24,256]{2,1,0:T(8,128)S(1)} %get-tuple-element.30.a1_ref, f32[7,16,128]{2,1,0:T(8,128)S(1)} %get-tuple-element.31.a2_ref, f32[7,8,128]{2,1,0:T(8,128)S(1)} %get-tuple-element.32.a3_ref, ...), custom_call_target="tpu_custom_call" | custom-call | flops 469762048 | bytes 1048576 | tf_op jit(solution)/shard_map/pallas_call | solution.py:586
Async XLA Ops:
  0.0 11.1 %collective-permute-start = (bf16[6,64,256]{2,1,0:T(8,128)(2,1)}, bf16[6,64,256]{2,1,0:T(8,128)(2,1)S(1)}, u32[]{:S(2)}, u32[]{:S(2)}) collective-permute-start(bf16[6,64,256]{2,1,0:T(8,128)(2,1)} %bitcast.7), channel_id=1, source_target_pairs={{0,12},{4,8},{8,4},{12,0},{1,13},{5,9},{9,5},{13,1},{2,14},{6,10},... | collective-permute-start | bytes 589832 | tf_op jit(solution)/shard_map/ppermute | solution.py:633
  6.9 14.2 %collective-permute-start.4 = (bf16[904,128]{1,0:T(8,128)(2,1)S(1)}, bf16[904,128]{1,0:T(8,128)(2,1)S(1)}, u32[]{:S(2)}, u32[]{:S(2)}) collective-permute-start(bf16[904,128]{1,0:T(8,128)(2,1)S(1)} %get-tuple-element.23.pack), channel_id=1, source_target_pairs={{0,4},{4,0},{8,12},{12,8},{1,5},{5,1},{9,13},{13,9},{2,6},{6,2},{1... | collective-permute-start | bytes 694280 | tf_op jit(solution)/shard_map/ppermute | solution.py:653
  11.1 16.1 %collective-permute-start.1 = (bf16[6,64,256]{2,1,0:T(8,128)(2,1)S(1)}, bf16[6,64,256]{2,1,0:T(8,128)(2,1)S(1)}, u32[]{:S(2)}, u32[]{:S(2)}) collective-permute-start(bf16[6,64,256]{2,1,0:T(8,128)(2,1)S(1)} %collective-permute-done.far), channel_id=1, source_target_pairs={{0,4},{4,0},{8,12},{12,8},{1,5},{5,1},{9,13},{13,9},{2,6},{6,2},{1... | collective-permute-start | bytes 589832 | tf_op jit(solution)/shard_map/ppermute | solution.py:677
  14.1 7.0 %collective-permute-start.2 = (bf16[136,128]{1,0:T(8,128)(2,1)S(1)}, bf16[136,128]{1,0:T(8,128)(2,1)S(1)}, u32[]{:S(2)}, u32[]{:S(2)}) collective-permute-start(bf16[136,128]{1,0:T(8,128)(2,1)S(1)} %get-tuple-element.22), channel_id=1, source_target_pairs={{0,12},{4,8},{8,4},{12,0},{1,13},{5,9},{9,5},{13,1},{2,14},{6,10},... | collective-permute-start | bytes 104456 | tf_op jit(solution)/shard_map/ppermute | solution.py:652
  21.1 6.1 %collective-permute-start.3 = (bf16[136,128]{1,0:T(8,128)(2,1)S(1)}, bf16[136,128]{1,0:T(8,128)(2,1)S(1)}, u32[]{:S(2)}, u32[]{:S(2)}) collective-permute-start(bf16[136,128]{1,0:T(8,128)(2,1)S(1)} %collective-permute-done.2.note), channel_id=1, source_target_pairs={{0,4},{4,0},{8,12},{12,8},{1,5},{5,1},{9,13},{13,9},{2,6},{6,2},{1... | collective-permute-start | bytes 104456 | tf_op jit(solution)/shard_map/ppermute | solution.py:678
  22.5 7.2 %collective-permute-start.5 = (f32[24,512]{1,0:T(8,128)S(1)}, f32[24,512]{1,0:T(8,128)S(1)}, u32[]{:S(2)}, u32[]{:S(2)}) collective-permute-start(f32[24,512]{1,0:T(8,128)S(1)} %get-tuple-element.33), channel_id=1, source_target_pairs={{0,2},{2,0},{4,6},{6,4},{8,10},{10,8},{12,14},{14,12},{1,3},{3,1},... | collective-permute-start | bytes 147464 | tf_op jit(solution)/shard_map/ppermute | solution.py:674
  24.0 5.6 %collective-permute-start.6 = (bf16[24,512]{1,0:T(8,128)(2,1)S(1)}, bf16[24,512]{1,0:T(8,128)(2,1)S(1)}, u32[]{:S(2)}, u32[]{:S(2)}) collective-permute-start(bf16[24,512]{1,0:T(8,128)(2,1)S(1)} %get-tuple-element.34), channel_id=1, source_target_pairs={{0,10},{2,8},{4,14},{6,12},{8,2},{10,0},{12,6},{14,4},{1,11},{3,9}... | collective-permute-start | bytes 73736 | tf_op jit(solution)/shard_map/ppermute | solution.py:674

commit v9 on v8

--- a/solution.py
+++ b/solution.py
@@ -430,10 +430,9 @@
     edge_of(plan, side_ref, table, row1_ref, row23_ref, edge_ref, tile_ref, z1_ref, z23_ref)
 
 
-def first_kernel(plan, far, note, near, before_ref, column_ref, row1_ref, row23_ref,
+def first_kernel(plan, far, note, near, near_note, before_ref, column_ref, row1_ref, row23_ref,
                  out_ref, edge_ref, prod_ref, side_ref, tile_ref, z1_ref, z23_ref):
     right = 2 * lax.axis_index("tx") < plan.n
-    near_note = near.at[pl.ds(plan.weight_at, plan.half + CODE_ROWS)]
     sums = slot_sums(plan, near, near_note, prod_ref.at[0])
     sums = before_ref[...] + sums + slot_sums(plan, far, note, prod_ref.at[1])
     out_ref[...] = sums
@@ -631,6 +630,7 @@
     across = [(i, n - 1 - i) for i in range(n)]
     beside = [(i, i ^ 1) for i in range(n)]
     far = lax.ppermute(blocks, "tx", across)
+    near = lax.ppermute(blocks, "tx", beside)
     pack, note = pl.pallas_call(
         functools.partial(pack_kernel, plan),
         out_shape=[
@@ -650,7 +650,7 @@
     )(counts, *[off_chip(v) for v in (blocks, cloud[0], destination, offset)])
 
     far_note = lax.ppermute(note, "tx", across)
-    near = lax.ppermute(pack, "tx", beside)
+    near_note = lax.ppermute(note, "tx", beside)
     edge_work = [
         pltpu.VMEM((planes * plan.half, TS), F32),
         pltpu.VMEM((2, 2 * plan.near, plan.rows), BF),
@@ -678,7 +678,7 @@
     late_note = lax.ppermute(far_note, "tx", beside)
     sums, edge_near = call(
         first_kernel,
-        [far, far_note, near, sums] + tables,
+        [far, far_note, near, near_note, sums] + tables,
         [sums_shape, pltpu.VMEM(edge_shape, F32)],
         [pltpu.VMEM((2, *prod_shape), BF)] + edge_work,
         flops=4 * work,

time: 31.4 us -> 33.7 us (1.073)
  waiting for transfers between devices: 7.03 us -> 9.48 us
    ppermute x1, waiting for transfers between devices: 4.15 us -> 6 us  [strip_local(): far = lax.ppermute(blocks, 'tx', across)]
    ppermute x2, waiting for transfers between devices: 0.91 us -> 2.75 us  [over(): return lax.ppermute(value, ('tx', 'ty'), pairs)]
    ppermute x2, starting transfers between devices: 4.76 us -> 3.19 us  [over(): return lax.ppermute(value, ('tx', 'ty'), pairs)]
    ppermute x1, starting transfers between devices: 0.01 us -> 1.38 us  [strip_local(): late_note = lax.ppermute(far_note, 'tx', beside)]
    ppermute x1, waiting for transfers between devices: 1.97 us -> 0.72 us  [strip_local(): far_note = lax.ppermute(note, 'tx', across)]
  transfers between devices with their start and end apart: 7 -> 8, of which waited for: 3 -> 3; matrix products, arithmetic and copies ran while one was open for 0% -> 0% of each run, Pallas kernels for 21% -> 19%
where the time goes in v9:
time: 33.7 us; the launch traced here: 33.5 us
  starting transfers between devices  15.2 us (45%)
  waiting for transfers between devices  9.48 us (28%)
  Pallas kernels  8.14 us (24%)
  between operations  0.69 us (2%)
    ppermute x1, waiting for transfers between devices, strip_local(): far = lax.ppermute(blocks, 'tx', across)  6 us
    pallas_call x4, Pallas kernels, call(): pl.pallas_call(functools.partial(kernel, plan), out_shape=outputs, in_spe...  5.6 us
    ppermute x1, starting transfers between devices, strip_local(): far = lax.ppermute(blocks, 'tx', across)  5.08 us
    ppermute x2, starting transfers between devices, over(): return lax.ppermute(value, ('tx', 'ty'), pairs)  3.19 us
    ppermute x1, starting transfers between devices, strip_local(): late = lax.ppermute(far, 'tx', beside)  3.03 us
    ppermute x2, waiting for transfers between devices, over(): return lax.ppermute(value, ('tx', 'ty'), pairs)  2.75 us
    ppermute x1, starting transfers between devices, strip_local(): far_note = lax.ppermute(note, 'tx', across)  2.54 us
    pallas_call x1, Pallas kernels, strip_local(): pl.pallas_call(functools.partial(load_kernel, plan), out_shape=[pltpu.VME...  1.42 us
  transfers between devices with their start and end apart: 8, of which 3 were waited for; matrix products, arithmetic and copies ran while one was open for 0% of the time, Pallas kernels for 19%

profile of v9, /device:TPU:0, one launch (start us, length us, event | category | flops | bytes accessed | tf_op | source)
XLA Modules:
  0.0 33.5 jit_solution(7276540181709357791)
XLA Ops:
  0.0 5.1 %collective-permute-start = (bf16[6,64,256]{2,1,0:T(8,128)(2,1)}, bf16[6,64,256]{2,1,0:T(8,128)(2,1)S(1)}, u32[]{:S(2)}, u32[]{:S(2)}) collective-permute-start(bf16[6,64,256]{2,1,0:T(8,128)(2,1)} %bitcast.7), channel_id=1, source_target_pairs={{0,12},{4,8},{8,4},{12,0},{1,13},{5,9},{9,5},{13,1},{2,14},{6,10},... | collective-permute-start | bytes 589832 | tf_op jit(solution)/shard_map/ppermute | solution.py:632
  5.1 0.0 collective-permute-start.4
  5.1 6.0 %collective-permute-done.far = bf16[6,64,256]{2,1,0:T(8,128)(2,1)S(1)} collective-permute-done((bf16[6,64,256]{2,1,0:T(8,128)(2,1)}, bf16[6,64,256]{2,1,0:T(8,128)(2,1)S(1)}, u32[]{:S(2)}, u32[]{:S(2)}) %collective-permute-start) | collective-permute-done | bytes 196640 | tf_op jit(solution)/shard_map/ppermute | solution.py:632
  11.1 3.0 %collective-permute-start.1 = (bf16[6,64,256]{2,1,0:T(8,128)(2,1)S(1)}, bf16[6,64,256]{2,1,0:T(8,128)(2,1)S(1)}, u32[]{:S(2)}, u32[]{:S(2)}) collective-permute-start(bf16[6,64,256]{2,1,0:T(8,128)(2,1)S(1)} %collective-permute-done.far), channel_id=1, source_target_pairs={{0,4},{4,0},{8,12},{12,8},{1,5},{5,1},{9,13},{13,9},{2,6},{6,2},{1... | collective-permute-start | bytes 589832 | tf_op jit(solution)/shard_map/ppermute | solution.py:677
  14.8 1.1 %pack.1 = (bf16[904,128]{1,0:T(8,128)(2,1)S(1)}, bf16[136,128]{1,0:T(8,128)(2,1)S(1)}) custom-call(s32[1,1]{1,0:T(1,128)S(6)} %copy.14.count_ref, bf16[6,64,256]{2,1,0:T(8,128)(2,1)} %bitcast.9, bf16[64,256]{1,0:T(8,128)(2,1)} %bitcast.10, s32[1,64]{1,0:T(1,128)} %dest_ref.1, s32[1,64]{1,0:T(1,128)} %offset_ref.1), custom_call_target="tpu_custom_call" | custom-call | tf_op jit(solution)/shard_map/pack/pallas_call | solution.py:634
  15.9 2.5 %collective-permute-start.2 = (bf16[136,128]{1,0:T(8,128)(2,1)S(1)}, bf16[136,128]{1,0:T(8,128)(2,1)S(1)}, u32[]{:S(2)}, u32[]{:S(2)}) collective-permute-start(bf16[136,128]{1,0:T(8,128)(2,1)S(1)} %get-tuple-element.22), channel_id=1, source_target_pairs={{0,12},{4,8},{8,4},{12,0},{1,13},{5,9},{9,5},{13,1},{2,14},{6,10},... | collective-permute-start | bytes 104456 | tf_op jit(solution)/shard_map/ppermute | solution.py:652
  18.4 0.0 collective-permute-start.5
  18.4 1.4 %load.1 = (bf16[152,256]{1,0:T(8,128)(2,1)S(1)}, bf16[512,256]{1,0:T(8,128)(2,1)S(1)}, bf16[512,256]{1,0:T(8,128)(2,1)S(1)}, bf16[256,512]{1,0:T(8,128)(2,1)S(1)...) custom-call(bf16[8,152,256]{2,1,0:T(8,128)(2,1)} %constant.14.clone.column_ref, ...), custom_call_target="tpu_custom_call" | custom-call | tf_op jit(solution)/shard_map/load/pallas_call | solution.py:608
  19.9 1.1 %shard_map.118 = (f32[896,512]{1,0:T(8,128)S(1)}, bf16[24,512]{1,0:T(8,128)(2,1)S(1)}) custom-call(bf16[904,128]{1,0:T(8,128)(2,1)S(1)} %get-tuple-element.23.pack, bf16[152,256]{1,0:T(8,128)(2,1)S(1)} %get-tuple-element.24.column_ref, bf16[512,256]{1,0:T(8,128)(2,1)S(1)} %get-tuple-element.25.row1_ref, bf16[512,256]{1,0:T(8,128)(2,1)S(1)} %get-tuple-element.26.row23_ref), custom_call_target="tpu_custom_call" | custom-call | flops 117440512 | bytes 1048576 | tf_op jit(solution)/shard_map/pallas_call | solution.py:585
  21.0 0.7 %collective-permute-done.2.note = bf16[136,128]{1,0:T(8,128)(2,1)S(1)} collective-permute-done((bf16[136,128]{1,0:T(8,128)(2,1)S(1)}, bf16[136,128]{1,0:T(8,128)(2,1)S(1)}, u32[]{:S(2)}, u32[]{:S(2)}) %collective-permute-start.2) | collective-permute-done | bytes 34848 | tf_op jit(solution)/shard_map/ppermute | solution.py:652
  21.7 1.4 %collective-permute-start.3 = (bf16[136,128]{1,0:T(8,128)(2,1)S(1)}, bf16[136,128]{1,0:T(8,128)(2,1)S(1)}, u32[]{:S(2)}, u32[]{:S(2)}) collective-permute-start(bf16[136,128]{1,0:T(8,128)(2,1)S(1)} %collective-permute-done.2.note), channel_id=1, source_target_pairs={{0,4},{4,0},{8,12},{12,8},{1,5},{5,1},{9,13},{13,9},{2,6},{6,2},{1... | collective-permute-start | bytes 104456 | tf_op jit(solution)/shard_map/ppermute | solution.py:678
  23.1 0.0 collective-permute-done.5.near_note
  23.1 0.0 collective-permute-done.4.near
  23.1 1.4 %shard_map.119 = (f32[896,512]{1,0:T(8,128)S(1)}, f32[24,512]{1,0:T(8,128)S(1)}) custom-call(bf16[6,64,256]{2,1,0:T(8,128)(2,1)S(1)} %collective-permute-done.far, bf16[136,128]{1,0:T(8,128)(2,1)S(1)} %collective-permute-done.2.note, bf16[6,64,256]{2,1,0:T(8,128)(2,1)S(1)} %collective-permute-done.4.near, ...), custom_call_target="tpu_custom_call" | custom-call | flops 469762048 | bytes 1048576 | tf_op jit(solution)/shard_map/pallas_call | solution.py:585
  24.4 1.6 %collective-permute-start.6 = (f32[24,512]{1,0:T(8,128)S(1)}, f32[24,512]{1,0:T(8,128)S(1)}, u32[]{:S(2)}, u32[]{:S(2)}) collective-permute-start(f32[24,512]{1,0:T(8,128)S(1)} %get-tuple-element.33), channel_id=1, source_target_pairs={{0,2},{2,0},{4,6},{6,4},{8,10},{10,8},{12,14},{14,12},{1,3},{3,1},... | collective-permute-start | bytes 147464 | tf_op jit(solution)/shard_map/ppermute | solution.py:674
  26.0 1.6 %collective-permute-start.7 = (bf16[24,512]{1,0:T(8,128)(2,1)S(1)}, bf16[24,512]{1,0:T(8,128)(2,1)S(1)}, u32[]{:S(2)}, u32[]{:S(2)}) collective-permute-start(bf16[24,512]{1,0:T(8,128)(2,1)S(1)} %get-tuple-element.34), channel_id=1, source_target_pairs={{0,10},{2,8},{4,14},{6,12},{8,2},{10,0},{12,6},{14,4},{1,11},{3,9}... | collective-permute-start | bytes 73736 | tf_op jit(solution)/shard_map/ppermute | solution.py:674
  27.6 0.0 collective-permute-done.3.note
  27.6 0.0 collective-permute-done.1.late
  27.6 1.5 %shard_map.120 = (f32[7,32,512]{2,1,0:T(8,128)S(1)}, f32[7,24,256]{2,1,0:T(8,128)S(1)}, f32[7,16,128]{2,1,0:T(8,128)S(1)}, f32[7,8,128]{2,1,0:T(8,128)S(1)}) custom-call(bf16[6,64,256]{2,1,0:T(8,128)(2,1)S(1)} %collective-permute-done.1.late, bf16[136,128]{1,0:T(8,128)(2,1)S(1)} %collective-permute-done.3.note, f32[896,512]{1,0:T(8,128)S(1)} %get-tuple-element.28.before_ref, ...), custom_call_target="tpu_custom_call" | custom-call | flops 469762048 | bytes 1048576 | tf_op jit(solution)/shard_map/pallas_call | solution.py:585
  29.1 2.7 %collective-permute-done.7.far_ref = bf16[24,512]{1,0:T(8,128)(2,1)S(1)} collective-permute-done((bf16[24,512]{1,0:T(8,128)(2,1)S(1)}, bf16[24,512]{1,0:T(8,128)(2,1)S(1)}, u32[]{:S(2)}, u32[]{:S(2)}) %collective-permute-start.7) | collective-permute-done | bytes 24608 | tf_op jit(solution)/shard_map/ppermute | solution.py:674
  31.9 0.0 collective-permute-done.6.near_ref
  31.9 1.6 %shard_map.121 = bf16[6,32,512]{2,1,0:T(8,128)(2,1)} custom-call(f32[7,32,512]{2,1,0:T(8,128)S(1)} %get-tuple-element.29.a0_ref, f32[7,24,256]{2,1,0:T(8,128)S(1)} %get-tuple-element.30.a1_ref, f32[7,16,128]{2,1,0:T(8,128)S(1)} %get-tuple-element.31.a2_ref, f32[7,8,128]{2,1,0:T(8,128)S(1)} %get-tuple-element.32.a3_ref, ...), custom_call_target="tpu_custom_call" | custom-call | flops 469762048 | bytes 1048576 | tf_op jit(solution)/shard_map/pallas_call | solution.py:585
Async XLA Ops:
  0.0 11.1 %collective-permute-start = (bf16[6,64,256]{2,1,0:T(8,128)(2,1)}, bf16[6,64,256]{2,1,0:T(8,128)(2,1)S(1)}, u32[]{:S(2)}, u32[]{:S(2)}) collective-permute-start(bf16[6,64,256]{2,1,0:T(8,128)(2,1)} %bitcast.7), channel_id=1, source_target_pairs={{0,12},{4,8},{8,4},{12,0},{1,13},{5,9},{9,5},{13,1},{2,14},{6,10},... | collective-permute-start | bytes 589832 | tf_op jit(solution)/shard_map/ppermute | solution.py:632
  5.1 18.0 %collective-permute-start.4 = (bf16[6,64,256]{2,1,0:T(8,128)(2,1)}, bf16[6,64,256]{2,1,0:T(8,128)(2,1)S(1)}, u32[]{:S(2)}, u32[]{:S(2)}) collective-permute-start(bf16[6,64,256]{2,1,0:T(8,128)(2,1)} %bitcast.8), channel_id=1, source_target_pairs={{0,4},{4,0},{8,12},{12,8},{1,5},{5,1},{9,13},{13,9},{2,6},{6,2},{1... | collective-permute-start | bytes 589832 | tf_op jit(solution)/shard_map/ppermute | solution.py:633
  11.1 16.6 %collective-permute-start.1 = (bf16[6,64,256]{2,1,0:T(8,128)(2,1)S(1)}, bf16[6,64,256]{2,1,0:T(8,128)(2,1)S(1)}, u32[]{:S(2)}, u32[]{:S(2)}) collective-permute-start(bf16[6,64,256]{2,1,0:T(8,128)(2,1)S(1)} %collective-permute-done.far), channel_id=1, source_target_pairs={{0,4},{4,0},{8,12},{12,8},{1,5},{5,1},{9,13},{13,9},{2,6},{6,2},{1... | collective-permute-start | bytes 589832 | tf_op jit(solution)/shard_map/ppermute | solution.py:677
  15.9 5.8 %collective-permute-start.2 = (bf16[136,128]{1,0:T(8,128)(2,1)S(1)}, bf16[136,128]{1,0:T(8,128)(2,1)S(1)}, u32[]{:S(2)}, u32[]{:S(2)}) collective-permute-start(bf16[136,128]{1,0:T(8,128)(2,1)S(1)} %get-tuple-element.22), channel_id=1, source_target_pairs={{0,12},{4,8},{8,4},{12,0},{1,13},{5,9},{9,5},{13,1},{2,14},{6,10},... | collective-permute-start | bytes 104456 | tf_op jit(solution)/shard_map/ppermute | solution.py:652
  18.4 4.6 %collective-permute-start.5 = (bf16[136,128]{1,0:T(8,128)(2,1)S(1)}, bf16[136,128]{1,0:T(8,128)(2,1)S(1)}, u32[]{:S(2)}, u32[]{:S(2)}) collective-permute-start(bf16[136,128]{1,0:T(8,128)(2,1)S(1)} %get-tuple-element.22), channel_id=1, source_target_pairs={{0,4},{4,0},{8,12},{12,8},{1,5},{5,1},{9,13},{13,9},{2,6},{6,2},{1... | collective-permute-start | bytes 104456 | tf_op jit(solution)/shard_map/ppermute | solution.py:653
  21.7 5.9 %collective-permute-start.3 = (bf16[136,128]{1,0:T(8,128)(2,1)S(1)}, bf16[136,128]{1,0:T(8,128)(2,1)S(1)}, u32[]{:S(2)}, u32[]{:S(2)}) collective-permute-start(bf16[136,128]{1,0:T(8,128)(2,1)S(1)} %collective-permute-done.2.note), channel_id=1, source_target_pairs={{0,4},{4,0},{8,12},{12,8},{1,5},{5,1},{9,13},{13,9},{2,6},{6,2},{1... | collective-permute-start | bytes 104456 | tf_op jit(solution)/shard_map/ppermute | solution.py:678
  24.4 7.4 %collective-permute-start.6 = (f32[24,512]{1,0:T(8,128)S(1)}, f32[24,512]{1,0:T(8,128)S(1)}, u32[]{:S(2)}, u32[]{:S(2)}) collective-permute-start(f32[24,512]{1,0:T(8,128)S(1)} %get-tuple-element.33), channel_id=1, source_target_pairs={{0,2},{2,0},{4,6},{6,4},{8,10},{10,8},{12,14},{14,12},{1,3},{3,1},... | collective-permute-start | bytes 147464 | tf_op jit(solution)/shard_map/ppermute | solution.py:674
  26.0 5.9 %collective-permute-start.7 = (bf16[24,512]{1,0:T(8,128)(2,1)S(1)}, bf16[24,512]{1,0:T(8,128)(2,1)S(1)}, u32[]{:S(2)}, u32[]{:S(2)}) collective-permute-start(bf16[24,512]{1,0:T(8,128)(2,1)S(1)} %get-tuple-element.34), channel_id=1, source_target_pairs={{0,10},{2,8},{4,14},{6,12},{8,2},{10,0},{12,6},{14,4},{1,11},{3,9}... | collective-permute-start | bytes 73736 | tf_op jit(solution)/shard_map/ppermute | solution.py:674
